TPU v7x, 32 devices: a whole 2x2x4 slice. The times are simulated.
32 devices in a mesh: seq: 16 (over z, x, core), batch: 2 (over y).
Axes of the slice: x: 2, y: 2, z: 4, core: 2. Of those that a mesh axis runs over, the one named last changes fastest.
Arguments:
- tokens: bfloat16 [2, 4096, 768], P('batch', 'seq'), may hold values from -6 to 6
- cotangent: bfloat16 [2, 4096, 768], P('batch', 'seq'), may hold values from -6 to 6
- bank: bfloat16 [2, 8192, 768], P('batch', 'seq'), may hold values from -6 to 6
- prefix: int32 [2], P('batch'), may hold values from 409 to 2048
- blocks: int32 [2, 8], P('batch'), may hold values from 0 to 63
- self_qkv: bfloat16 [768, 2304], P(('seq', 'batch')), may hold values from -0.21875 to 0.21875
- self_out: bfloat16 [768, 768], P(('seq', 'batch')), may hold values from -3.5 to 3.5
- cross_q: bfloat16 [768, 768], P(('seq', 'batch')), may hold values from -0.21875 to 0.21875
- cross_kv: bfloat16 [768, 1536], P(('seq', 'batch')), may hold values from -0.21875 to 0.21875
- cross_out: bfloat16 [768, 768], P(('seq', 'batch')), may hold values from -1.75 to 1.75
- ffn_in: bfloat16 [768, 3072], P(('seq', 'batch')), may hold values from -0.21875 to 0.21875
- ffn_out: bfloat16 [3072, 768], P(('seq', 'batch')), may hold values from -0.109375 to 0.109375
- gains: bfloat16 [3, 768], P(None, ('seq', 'batch')), may hold values from 0.5 to 1.5
- biases: bfloat16 [14, 768], P(None, ('seq', 'batch')), may hold values from -1.75 to 1.75
Outputs:
- output: bfloat16 [2, 4096, 768], P('batch', 'seq')
- tokens_grad: float32 [2, 4096, 768], P('batch', 'seq')
- bank_grad: float32 [2, 8192, 768], P('batch', 'seq')
- self_qkv_grad: float32 [768, 2304], P(('seq', 'batch'))
- self_out_grad: float32 [768, 768], P(('seq', 'batch'))
- cross_q_grad: float32 [768, 768], P(('seq', 'batch'))
- cross_kv_grad: float32 [768, 1536], P(('seq', 'batch'))
- cross_out_grad: float32 [768, 768], P(('seq', 'batch'))
- ffn_in_grad: float32 [768, 3072], P(('seq', 'batch'))
- ffn_out_grad: float32 [3072, 768], P(('seq', 'batch'))
- gains_grad: float32 [3, 768], P(None, ('seq', 'batch'))
- biases_grad: float32 [14, 768], P(None, ('seq', 'batch'))
All inputs are finite; a program needn't handle non-finite values.
Results may differ from a plain program's by a relative error of at most 0.025.
Values may be sent and summed in bfloat16 or wider, within the bound.
No kernel may reach another device: no remote copies, remote signals or barrier semaphores. Data moves between devices by JAX's collectives and lax.ppermute only.
A program may use at most 256 MiB of HBM per device.

v0:
```python
import functools

import jax
import jax.numpy as jnp
from jax import lax
from jax.experimental import pallas as pl
from jax.experimental.pallas import tpu as pltpu
from jax.sharding import PartitionSpec as P

HEADS = 12
HEAD_DIM = 64
BANK_BLOCK = 128
GROUPS = 4
GROUP_HEADS = HEADS // GROUPS
GROUP_WIDTH = GROUP_HEADS * HEAD_DIM
QUERY, SIDE = 256, 384
PACK = QUERY + SIDE
EPSILON = 1e-05
NEGATIVE = -1e30
SCALE = HEAD_DIM ** (-0.5)
LANES_IN = (((1,), (1,)), ((), ()))
ROWS_IN = (((0,), (0,)), ((), ()))
VMEM_LIMIT = 60 * 1024 * 1024


def layer_norm(values, gain, shift):
    centered = values - jnp.mean(values, axis=-1, keepdims=True)
    variance = jnp.mean(centered * centered, axis=-1, keepdims=True)
    return centered * lax.rsqrt(variance + EPSILON) * gain + shift


def gelu_exact(values):
    return jax.nn.gelu(values, approximate=False)


def rounded(values):
    return values.astype(jnp.bfloat16)


def wide(values):
    return values.astype(jnp.float32)


def matmul(left, right):
    return jnp.dot(left, right, preferred_element_type=jnp.float32)


def weight_grad(left, right):
    return lax.dot_general(left, right, ROWS_IN, preferred_element_type=jnp.float32)


def back_matmul(left, right):
    return lax.dot_general(left, right, LANES_IN, preferred_element_type=jnp.float32)


def column_sums(values):
    return jnp.sum(wide(values), axis=0)


class Grid:
    def __init__(self, mesh):
        self.seq = mesh.shape["seq"]
        self.y = mesh.shape["batch"]
        self.z = GROUPS
        self.c = self.h = self.l = 2
        self.x = self.seq // (self.z * self.c)

    def coords(self, index):
        spot, y = divmod(index, self.y)
        spot, c = divmod(spot, self.c)
        z, x = divmod(spot, self.x)
        return z, x, c, y

    def index(self, z, x, c, y):
        return ((z * self.x + x) * self.c + c) * self.y + y

    def send(self, array, axis, shift, mirror=False):
        if axis in "hl":
            axis, shift = "z", shift * (2 if axis == "h" else 1)
        place = "zxcy".index(axis)
        pairs = []
        for index in range(self.seq * self.y):
            spot = list(self.coords(index))
            spot[place] ^= shift
            if mirror:
                spot[1], spot[2] = self.x - 1 - spot[1], self.c - 1 - spot[2]
            pairs.append((index, self.index(*spot)))
        return lax.ppermute(array, ("seq", "batch"), pairs)


def in_order(pieces, me):
    pieces = list(pieces)
    bit = 1
    while bit < len(pieces):
        swap = (me & bit) != 0
        pieces = [jnp.where(swap, pieces[j ^ bit], piece) for j, piece in enumerate(pieces)]
        bit *= 2
    return jnp.stack(pieces)


def take(array, index, axis):
    return lax.dynamic_index_in_dim(array, index, axis, keepdims=False)


def head_parts(block, scale, third_low):
    lane = lax.broadcasted_iota(jnp.int32, (block.shape[0], 128), 1)
    first = wide(block[:, 0:128]) * scale
    third = wide(block[:, 128:256]) * scale
    third = jnp.where(lane < 64, third, 0.0)
    if not third_low:
        third = pltpu.roll(third, 64, 1)
    return (
        rounded(jnp.where(lane < 64, first, 0.0)),
        rounded(jnp.where(lane >= 64, first, 0.0)),
        rounded(third),
    )


def key_tiles(ref, start, size):
    rows = pl.ds(start, size)
    keys = ref[rows, 0:128]
    values = ref[rows, 128:256]
    third = ref[rows, 256:384]
    return (keys, keys, third), (values, values, third)


def allowed_keys(key_first, query_first, prefix_len, shape):
    key_pos = key_first + lax.broadcasted_iota(jnp.int32, shape, 0)
    query_pos = query_first + lax.broadcasted_iota(jnp.int32, shape, 1)
    return (key_pos <= query_pos) | (key_pos < prefix_len)


def each_block(table, refs, rows, query_first, prefix_len, work):
    count = refs[0].shape[0] // rows
    for part, ref in enumerate(refs):

        def step(local, carry, part=part, ref=ref):
            block = part * count + local
            key_first = table[block]
            last = key_first + rows - 1
            seen = (key_first <= query_first + rows - 1) | (key_first < prefix_len)
            whole = (last <= query_first) | (last < prefix_len)

            @pl.when(seen & whole)
            def _():
                work(ref, local * rows, block, key_first, False)

            @pl.when(seen & jnp.logical_not(whole))
            def _():
                work(ref, local * rows, block, key_first, True)

            return carry

        lax.fori_loop(0, count, step, 0)


def forward_kernel(rows, parts, first, last, table, query_in, *refs):
    refs = list(refs)
    sides = [refs.pop(0) for _ in range(parts)]
    if not first:
        accum_in, stats_in = refs.pop(0), refs.pop(0)
    out, state, query, accum, stats = refs
    m = pl.program_id(0)
    blocks = parts * (sides[0].shape[0] // rows)
    query_first = table[blocks + m]
    prefix_len = table[blocks + GROUPS]
    for head, part in enumerate(head_parts(query_in[0], SCALE, True)):
        query[head] = part
    if first:
        accum[...] = jnp.zeros_like(accum)
        stats[0:8, :] = jnp.full((8, rows), NEGATIVE, jnp.float32)
        stats[8:16, :] = jnp.zeros((8, rows), jnp.float32)
    else:
        accum[...] = accum_in[0]
        stats[...] = stats_in[0]

    def work(ref, start, block, key_first, masked):
        keys, values = key_tiles(ref, start, rows)
        if masked:
            mask = allowed_keys(key_first, query_first, prefix_len, (rows, rows))
        for head in range(GROUP_HEADS):
            scores = lax.dot_general(
                keys[head], query[head], LANES_IN, preferred_element_type=jnp.float32
            )
            if masked:
                scores = jnp.where(mask, scores, NEGATIVE)
            old = stats[head : head + 1, :]
            top = jnp.maximum(old, jnp.max(scores, axis=0, keepdims=True))
            weights = jnp.exp(scores - top)
            shrink = jnp.exp(old - top)
            stats[head : head + 1, :] = top
            stats[8 + head : 9 + head, :] = stats[8 + head : 9 + head, :] * shrink + jnp.sum(
                weights, axis=0, keepdims=True
            )
            accum[head] = accum[head] * shrink + lax.dot_general(
                values[head], rounded(weights), ROWS_IN, preferred_element_type=jnp.float32
            )

    each_block(table, sides, rows, query_first, prefix_len, work)
    if not last:
        out[0] = accum[...]
        state[0] = stats[...]
        return
    totals = stats[8 : 8 + GROUP_HEADS, :]
    final = [accum[head] / totals[head : head + 1, :] for head in range(GROUP_HEADS)]
    line = lax.broadcasted_iota(jnp.int32, (128, rows), 0)
    out[0, :, 0:128] = jnp.where(line < 64, final[0], final[1]).T
    third = jnp.concatenate([final[2][64:128], jnp.zeros((64, rows), jnp.float32)], axis=0)
    out[0, :, 128:256] = third.T
    state[0] = jnp.zeros((8, rows), jnp.float32)
    state[0, 0:GROUP_HEADS, :] = stats[0:GROUP_HEADS, :] + jnp.log(totals)


def backward_kernel(rows, parts, first, last, table, query_in, dout, state, *refs):
    refs = list(refs)
    sides = [refs.pop(0) for _ in range(parts)]
    carried = refs.pop(0)
    grads_out = [refs.pop(0) for _ in range(parts)]
    qgrad_out = refs.pop(0)
    if first:
        state_out = refs.pop(0)
    query, accum, qgrad, lines = refs
    m = pl.program_id(0)
    count = sides[0].shape[0] // rows
    blocks = parts * count
    query_first = table[blocks + m]
    prefix_len = table[blocks + GROUPS]

    @pl.when(m == 0)
    def _():
        def clear(index, carry):
            accum[pl.ds(index * rows, rows), :] = jnp.zeros((rows, SIDE), jnp.float32)
            return carry

        lax.fori_loop(0, blocks, clear, 0)

    for head, part in enumerate(head_parts(query_in[0], SCALE, True)):
        query[head] = part
    for head, part in enumerate(head_parts(dout[0], 1.0, False)):
        query[GROUP_HEADS + head] = part
    lines[...] = state[0]
    if first:
        pair_prod = (wide(dout[0, :, 0:128]) * carried[0, :, 0:128]).T
        third_prod = (wide(dout[0, :, 128:256]) * carried[0, :, 128:256]).T
        lines[3:4, :] = jnp.sum(pair_prod[0:64], axis=0, keepdims=True)
        lines[4:5, :] = jnp.sum(pair_prod[64:128], axis=0, keepdims=True)
        lines[5:6, :] = jnp.sum(third_prod[0:64], axis=0, keepdims=True)
        state_out[0] = lines[...]
        qgrad[...] = jnp.zeros_like(qgrad)
    else:
        qgrad[...] = carried[0]

    def work(ref, start, block, key_first, masked):
        keys, values = key_tiles(ref, start, rows)
        if masked:
            mask = allowed_keys(key_first, query_first, prefix_len, (rows, rows))
        key_parts, value_parts = [], []
        for head in range(GROUP_HEADS):
            scores = lax.dot_general(
                keys[head], query[head], LANES_IN, preferred_element_type=jnp.float32
            )
            if masked:
                scores = jnp.where(mask, scores, NEGATIVE)
            probs = jnp.exp(scores - lines[head : head + 1, :])
            slopes = lax.dot_general(
                values[head],
                query[GROUP_HEADS + head],
                LANES_IN,
                preferred_element_type=jnp.float32,
            )
            low = rounded(probs * (slopes - lines[3 + head : 4 + head, :]))
            value_parts.append(matmul(rounded(probs), query[GROUP_HEADS + head]))
            key_parts.append(matmul(low, query[head]))
            qgrad[head] += lax.dot_general(
                keys[head], low, ROWS_IN, preferred_element_type=jnp.float32
            )
        span = pl.ds(pl.multiple_of(block * rows, rows), rows)
        accum[span, 0:128] += key_parts[0] + key_parts[1]
        accum[span, 128:256] += value_parts[0] + value_parts[1]
        accum[span, 256:384] += key_parts[2] + value_parts[2]

    each_block(table, sides, rows, query_first, prefix_len, work)
    if last:
        line = lax.broadcasted_iota(jnp.int32, (128, rows), 0)
        qgrad_out[0, :, 0:128] = rounded(jnp.where(line < 64, qgrad[0], qgrad[1]).T * SCALE)
        qgrad_out[0, :, 128:256] = rounded(jnp.where(line < 64, qgrad[2], 0.0).T * SCALE)
    else:
        qgrad_out[0] = qgrad[...]

    @pl.when(m == GROUPS - 1)
    def _():
        for part, ref in enumerate(grads_out):

            def write(index, carry, part=part, ref=ref):
                source = pl.ds((part * count + index) * rows, rows)
                ref[pl.ds(index * rows, rows), :] = rounded(accum[source, :])
                return carry

            lax.fori_loop(0, count, write, 0)


def whole(shape):
    return pl.BlockSpec(shape, lambda *_: (0,) * len(shape), pipeline_mode=pl.Buffered(1))


def slab(shape):
    return pl.BlockSpec((1,) + shape, lambda m, *_: (m,) + (0,) * len(shape))


def self_forward(table, queries, sides, carried, last):
    rows = queries.shape[1]
    parts, length = len(sides), sides[0].shape[0]
    pairs = GROUPS * parts * length // rows * GROUP_HEADS // 2
    accum, stats = (GROUP_HEADS, 128, rows), (16, rows)
    outs = [(rows, 256), (8, rows)] if last else [accum, stats]
    first = carried is None
    return pl.pallas_call(
        functools.partial(forward_kernel, rows, parts, first, last),
        grid_spec=pltpu.PrefetchScalarGridSpec(
            num_scalar_prefetch=1,
            grid=(GROUPS,),
            in_specs=[slab((rows, QUERY))]
            + [whole((length, SIDE))] * parts
            + ([] if first else [slab(accum), slab(stats)]),
            out_specs=[slab(shape) for shape in outs],
            scratch_shapes=[
                pltpu.VMEM((GROUP_HEADS, rows, 128), jnp.bfloat16),
                pltpu.VMEM(accum, jnp.float32),
                pltpu.VMEM(stats, jnp.float32),
            ],
        ),
        out_shape=[jax.ShapeDtypeStruct((GROUPS,) + shape, jnp.float32) for shape in outs],
        compiler_params=pltpu.CompilerParams(vmem_limit_bytes=VMEM_LIMIT),
        cost_estimate=pl.CostEstimate(
            flops=pairs * rows * rows * 128 * 16,
            bytes_accessed=4 * length * parts * SIDE,
            transcendentals=pairs * rows * rows,
        ),
        name="self_forward",
    )(table, queries, *sides, *(() if first else carried))


def self_backward(table, queries, dout, state, sides, carried, first, last):
    rows = queries.shape[1]
    parts, length = len(sides), sides[0].shape[0]
    pairs = GROUPS * parts * length // rows * GROUP_HEADS // 2
    slope = (GROUP_HEADS, 128, rows)
    outs = [jax.ShapeDtypeStruct((length, SIDE), jnp.bfloat16)] * parts
    out_specs = [whole((length, SIDE))] * parts
    if last:
        outs = outs + [jax.ShapeDtypeStruct((GROUPS, rows, QUERY), jnp.bfloat16)]
        out_specs = out_specs + [slab((rows, QUERY))]
    else:
        outs = outs + [jax.ShapeDtypeStruct((GROUPS,) + slope, jnp.float32)]
        out_specs = out_specs + [slab(slope)]
    if first:
        outs = outs + [jax.ShapeDtypeStruct((GROUPS, 8, rows), jnp.float32)]
        out_specs = out_specs + [slab((8, rows))]
    return pl.pallas_call(
        functools.partial(backward_kernel, rows, parts, first, last),
        grid_spec=pltpu.PrefetchScalarGridSpec(
            num_scalar_prefetch=1,
            grid=(GROUPS,),
            in_specs=[slab((rows, QUERY)), slab((rows, 256)), slab((8, rows))]
            + [whole((length, SIDE))] * parts
            + [slab((rows, 256)) if first else slab(slope)],
            out_specs=out_specs,
            scratch_shapes=[
                pltpu.VMEM((2 * GROUP_HEADS, rows, 128), jnp.bfloat16),
                pltpu.VMEM((parts * length, SIDE), jnp.float32),
                pltpu.VMEM(slope, jnp.float32),
                pltpu.VMEM((8, rows), jnp.float32),
            ],
        ),
        out_shape=outs,
        compiler_params=pltpu.CompilerParams(vmem_limit_bytes=VMEM_LIMIT),
        cost_estimate=pl.CostEstimate(
            flops=pairs * rows * rows * 128 * 20,
            bytes_accessed=8 * length * parts * SIDE,
            transcendentals=pairs * rows * rows,
        ),
        name="self_backward",
    )(table, queries, dout, state, *sides, carried)


def pair_heads(block, scale=1.0):
    lane = lax.broadcasted_iota(jnp.int32, block.shape, 1)
    values = wide(block) * scale
    return rounded(jnp.where(lane < 64, values, 0.0)), rounded(jnp.where(lane >= 64, values, 0.0))


def cross_forward_kernel(query, keys, values, out, lse):
    rows = query.shape[0]
    parts = pair_heads(query[...], SCALE)
    sides = []
    lse[0] = jnp.zeros((8, rows), jnp.float32)
    for head in range(2):
        scores = lax.dot_general(
            keys[...], parts[head], LANES_IN, preferred_element_type=jnp.float32
        )
        top = jnp.max(scores, axis=0, keepdims=True)
        weights = jnp.exp(scores - top)
        total = jnp.sum(weights, axis=0, keepdims=True)
        mixed = lax.dot_general(
            values[...], rounded(weights), ROWS_IN, preferred_element_type=jnp.float32
        )
        sides.append(mixed / total)
        lse[0, head : head + 1, :] = top + jnp.log(total)
    line = lax.broadcasted_iota(jnp.int32, (128, rows), 0)
    out[...] = rounded(jnp.where(line < 64, sides[0], sides[1]).T)


def cross_backward_kernel(query, keys, values, dout, lse, qgrad, kgrad, vgrad):
    rows = query.shape[0]
    parts = pair_heads(query[...], SCALE)
    grads = pair_heads(dout[...])
    sides, key_parts, value_parts = [], [], []
    for head in range(2):
        scores = lax.dot_general(
            keys[...], parts[head], LANES_IN, preferred_element_type=jnp.float32
        )
        probs = jnp.exp(scores - lse[0, head : head + 1, :])
        slopes = lax.dot_general(
            values[...], grads[head], LANES_IN, preferred_element_type=jnp.float32
        )
        delta = jnp.sum(probs * slopes, axis=0, keepdims=True)
        low = rounded(probs * (slopes - delta))
        value_parts.append(matmul(rounded(probs), grads[head]))
        key_parts.append(matmul(low, parts[head]))
        sides.append(lax.dot_general(keys[...], low, ROWS_IN, preferred_element_type=jnp.float32))
    line = lax.broadcasted_iota(jnp.int32, (128, rows), 0)
    qgrad[...] = rounded(jnp.where(line < 64, sides[0], sides[1]).T * SCALE)
    kgrad[...] = rounded(key_parts[0] + key_parts[1])
    vgrad[...] = rounded(value_parts[0] + value_parts[1])


def cross_forward(query, pair):
    rows, width = query.shape
    count = width // 128
    kept = pair.shape[0]
    return pl.pallas_call(
        cross_forward_kernel,
        grid=(count,),
        in_specs=[
            pl.BlockSpec((rows, 128), lambda i: (0, i)),
            pl.BlockSpec((kept, 128), lambda i: (0, i)),
            pl.BlockSpec((kept, 128), lambda i: (0, count + i)),
        ],
        out_specs=[
            pl.BlockSpec((rows, 128), lambda i: (0, i)),
            pl.BlockSpec((1, 8, rows), lambda i: (i, 0, 0)),
        ],
        out_shape=[
            jax.ShapeDtypeStruct((rows, width), jnp.bfloat16),
            jax.ShapeDtypeStruct((count, 8, rows), jnp.float32),
        ],
        compiler_params=pltpu.CompilerParams(vmem_limit_bytes=VMEM_LIMIT),
        cost_estimate=pl.CostEstimate(
            flops=8 * rows * kept * width, bytes_accessed=4 * kept * width, transcendentals=12 * rows * kept
        ),
        name="cross_forward",
    )(query, pair, pair)


def cross_backward(query, pair, dout, lse):
    rows, width = query.shape
    count = width // 128
    kept = pair.shape[0]
    return pl.pallas_call(
        cross_backward_kernel,
        grid=(count,),
        in_specs=[
            pl.BlockSpec((rows, 128), lambda i: (0, i)),
            pl.BlockSpec((kept, 128), lambda i: (0, i)),
            pl.BlockSpec((kept, 128), lambda i: (0, count + i)),
            pl.BlockSpec((rows, 128), lambda i: (0, i)),
            pl.BlockSpec((1, 8, rows), lambda i: (i, 0, 0)),
        ],
        out_specs=[
            pl.BlockSpec((rows, 128), lambda i: (0, i)),
            pl.BlockSpec((kept, 128), lambda i: (0, i)),
            pl.BlockSpec((kept, 128), lambda i: (0, i)),
        ],
        out_shape=[
            jax.ShapeDtypeStruct((rows, width), jnp.bfloat16),
            jax.ShapeDtypeStruct((kept, width), jnp.bfloat16),
            jax.ShapeDtypeStruct((kept, width), jnp.bfloat16),
        ],
        compiler_params=pltpu.CompilerParams(vmem_limit_bytes=VMEM_LIMIT),
        cost_estimate=pl.CostEstimate(
            flops=20 * rows * kept * width, bytes_accessed=8 * kept * width, transcendentals=12 * rows * kept
        ),
        name="cross_backward",
    )(query, pair, pair, dout, lse)


def pick_kernel(table, bank, out):
    i = pl.program_id(0)
    keep = table[pl.num_programs(0) + i]
    out[0] = jnp.where(keep > 0, bank[0], jnp.zeros_like(bank[0]))


def pick_rows(chunks, spots, found):
    count = spots.shape[0]
    size = chunks.shape[1:]
    table = jnp.concatenate([spots, found.astype(jnp.int32)])
    return pl.pallas_call(
        pick_kernel,
        grid_spec=pltpu.PrefetchScalarGridSpec(
            num_scalar_prefetch=1,
            grid=(count,),
            in_specs=[pl.BlockSpec((1,) + size, lambda i, t: (t[i], 0, 0))],
            out_specs=pl.BlockSpec((1,) + size, lambda i, t: (i, 0, 0)),
        ),
        out_shape=jax.ShapeDtypeStruct((count,) + size, chunks.dtype),
        name="pick_rows",
    )(table, chunks)


def place_kernel(count, table, grads, out):
    spot = pl.program_id(0)
    out[...] = jnp.zeros_like(out)
    for i in range(count):

        @pl.when(table[i] == spot)
        def _(i=i):
            out[0] += wide(grads[i])


def place_rows(grads, spots, chunks):
    count = spots.shape[0]
    size = grads.shape[1:]
    return pl.pallas_call(
        functools.partial(place_kernel, count),
        grid_spec=pltpu.PrefetchScalarGridSpec(
            num_scalar_prefetch=1,
            grid=(chunks,),
            in_specs=[whole((count,) + size)],
            out_specs=pl.BlockSpec((1,) + size, lambda n, t: (n, 0, 0)),
        ),
        out_shape=jax.ShapeDtypeStruct((chunks,) + size, jnp.float32),
        name="place_rows",
    )(spots, grads)


class Chain:
    def __init__(self, stages):
        self.stages = stages
        self.result = None
        self.pending = next(stages)

    def step(self, pending):
        try:
            self.pending = self.stages.send(pending)
        except StopIteration as stop:
            self.pending, self.result = (), stop.value


def meet(values, *chains):
    values, pending = lax.optimization_barrier((values, [chain.pending for chain in chains]))
    for chain, arrays in zip(chains, pending):
        chain.step(arrays)
    return values


def total_of(arrays):
    total = wide(arrays[0])
    for array in arrays[1:]:
        total = total + wide(array)
    return total


def body(
    grid,
    tokens,
    cotangent,
    bank,
    prefix,
    blocks,
    self_qkv,
    self_out,
    cross_q,
    cross_kv,
    cross_out,
    ffn_in,
    ffn_out,
    gains,
    biases,
):
    Z, X, C, Y = grid.z, grid.x, grid.c, grid.y
    devices = grid.seq * Y
    seq_index = lax.axis_index("seq")
    me = {
        "y": lax.axis_index("batch"),
        "c": seq_index % C,
        "x": (seq_index // C) % X,
        "z": seq_index // (C * X),
        "h": seq_index // (2 * C * X),
        "l": seq_index // (C * X) % 2,
    }
    my_z, my_x, my_c = me["z"], me["x"], me["c"]
    rows, width = tokens.shape[1:]
    hidden = ffn_in.shape[1]
    part = width // devices
    fan = hidden // width
    inputs = tokens[0]

    def parted(array, axis, place):
        size = getattr(grid, axis)
        kept = [take(array, me[axis], place)]
        for shift in range(1, size):
            kept.append(grid.send(take(array, me[axis] ^ shift, place), axis, shift))
        return kept

    def reduction(array, axes, lead=0, final=True):
        names = ["h", "l", "x", "c", "y"]
        for axis in axes:
            place = lead + names.index(axis)
            names.remove(axis)
            arrays = yield parted(array, axis, place)
            total = total_of(arrays)
            array = rounded(total)
        return total if final else array

    def sharded(array):
        return array.reshape(2, 2, X, C, Y, array.shape[0] // devices, array.shape[1])

    grouped = self_qkv.reshape(part, 3, GROUPS, GROUP_WIDTH)
    extra = jnp.stack([biases[3], biases[4]], axis=1)
    extra = jnp.broadcast_to(
        jnp.pad(extra, ((0, 0), (0, QUERY - GROUP_WIDTH - 2)))[:, None],
        (part, GROUPS, QUERY - GROUP_WIDTH),
    )
    packed = jnp.concatenate(
        [
            grouped[:, 0],
            extra,
            grouped[:, 1, :, :128],
            grouped[:, 2, :, :128],
            grouped[:, 1, :, 128:],
            grouped[:, 2, :, 128:],
        ],
        axis=2,
    ).transpose(1, 0, 2)
    pieces = parted(packed, "z", 0)

    small = jnp.concatenate([gains, biases], axis=0).T
    small = jnp.pad(small, ((0, 0), (0, 128 - small.shape[1])))
    first_pack = jnp.concatenate([self_out, cross_q, cross_out, cross_kv, small], axis=1)
    inner_columns = (
        ffn_in.reshape(part, devices, fan, part).transpose(0, 2, 1, 3).reshape(part, hidden)
    )
    outer_blocks = ffn_out.reshape(fan, part, width).transpose(1, 0, 2).reshape(part, hidden)
    second_pack = jnp.stack([inner_columns, outer_blocks])
    first_all = lax.all_gather(first_pack, ("seq", "batch"), axis=0, tiled=True)
    second_all = lax.all_gather(second_pack, ("seq", "batch"), axis=1, tiled=True)

    pieces, inputs = lax.optimization_barrier((pieces, inputs))
    across = grid.send(inputs, "h", 1)
    token_parts = [inputs, grid.send(inputs, "l", 1), across, grid.send(across, "l", 1)]

    chunk = BANK_BLOCK * blocks.shape[1] // grid.seq
    per_block = BANK_BLOCK // chunk
    local_chunks = bank.shape[1] // chunk
    local_blocks = bank.shape[1] // BANK_BLOCK
    bank_chunks = bank[0].reshape(local_chunks, chunk, width)
    home = seq_index * local_blocks
    every = jnp.arange(grid.seq, dtype=jnp.int32)
    wanted = jnp.take(blocks[0], every // per_block) - home
    found = (wanted >= 0) & (wanted < local_blocks)
    spots = jnp.where(found, wanted * per_block + every % per_block, 0)
    picked = pick_rows(bank_chunks, spots, found).reshape(2, 2, X, C, 1, chunk, width)

    def spreading(own):
        array = own
        for axis in "hlxc":
            size = getattr(grid, axis)
            array = jnp.stack((yield [array] + [grid.send(array, axis, m) for m in range(1, size)]))
        return array

    def retrieval():
        own = (yield from reduction(picked, "cxlh", final=False))[0]
        every_row = yield from spreading(own)
        return own, every_row.reshape(grid.seq * chunk, width)

    retrieve = Chain(retrieval())
    gathered = in_order(pieces, my_z)
    for axis in "yxc":
        pieces = [gathered] + [grid.send(gathered, axis, m) for m in range(1, getattr(grid, axis))]
        if axis == "y":
            pieces = meet(pieces, retrieve)
        gathered = in_order(pieces, me[axis])
    qkv_group = gathered.transpose(3, 1, 0, 2, 4, 5).reshape(width, PACK)
    column = jnp.arange(PACK, dtype=jnp.int32)
    real = (column < GROUP_WIDTH) | (column >= QUERY)
    is_query = column < GROUP_WIDTH
    is_pair_value = (column >= QUERY + 128) & (column < QUERY + 256)
    is_value = is_pair_value | (column >= QUERY + 320)
    local = jnp.where(is_query, column, column - jnp.where(is_pair_value, QUERY + 128, QUERY + 192))
    line = jnp.where(is_query | is_value, local + my_z * GROUP_WIDTH, -1)
    chosen = (jnp.arange(width, dtype=jnp.int32)[:, None] == line[None]).astype(jnp.bfloat16)
    picked_bias = weight_grad(qkv_group[:, GROUP_WIDTH:QUERY], chosen)
    qkv_bias = jnp.where(is_query, picked_bias[0], picked_bias[1])
    qkv_weight = jnp.where(real[None], qkv_group, jnp.zeros_like(qkv_group))

    qkv_weight, qkv_bias, token_parts = meet((qkv_weight, qkv_bias, token_parts), retrieve)

    token_column = jnp.concatenate(token_parts, axis=0)
    own_queries = rounded(matmul(token_column, qkv_weight[:, :QUERY]) + qkv_bias[:QUERY])
    own_side = rounded(matmul(token_column, qkv_weight[:, QUERY:]) + qkv_bias[QUERY:])
    own_queries = own_queries.reshape(GROUPS, rows, QUERY)

    far_queries = grid.send(own_queries[1::2], "z", 0, mirror=True)
    near_other = grid.send(own_side, "c", 1)
    far_queries, side = lax.optimization_barrier((far_queries, own_side))
    far_own = [grid.send(side, "x", m) for m in range(1, X)]
    queries = jnp.stack(
        [own_queries[m] if m % 2 == 0 else far_queries[m // 2] for m in range(GROUPS)]
    )

    turn = jnp.arange(GROUPS, dtype=jnp.int32)
    turn_z = my_z ^ turn

    def key_firsts(x, c):
        return ((turn_z * X + x) * C + c) * rows

    query_firsts = jnp.where(
        turn % 2 == 0, key_firsts(my_x, my_c), key_firsts(X - 1 - my_x, C - 1 - my_c)
    )

    def table_of(shifts, c):
        keys = [key_firsts(my_x ^ m, c) for m in shifts]
        return jnp.concatenate(keys + [query_firsts, prefix]).astype(jnp.int32)

    far = list(range(1, X))
    tables = {
        "near own": table_of([0], my_c),
        "near other": table_of([0], C - 1 - my_c),
        "far own": table_of(far, my_c),
        "far other": table_of(far, C - 1 - my_c),
    }

    carry = self_forward(tables["near own"], queries, [own_side], None, False)
    carry, near_other = meet((carry, near_other), retrieve)
    carry = self_forward(tables["near other"], queries, [near_other], carry, False)
    carry, far_own = meet((carry, far_own), retrieve)
    far_other = [grid.send(side, "c", 1) for side in far_own]
    carry = self_forward(tables["far own"], queries, far_own, carry, False)
    carry, far_other = meet((carry, far_other), retrieve)
    attention, lse = self_forward(tables["far other"], queries, far_other, carry, True)
    attention, lse = meet((attention, lse), retrieve)
    attention_mine = rounded(attention)

    def swapped(array, m):
        return grid.send(array, "z", m, mirror=m % 2 == 1)

    pieces = [attention_mine[0]] + [swapped(attention_mine[m], m) for m in range(1, Z)]
    pieces = meet(pieces, retrieve)
    retrieve.step(retrieve.pending)
    own_rows, all_rows = retrieve.result
    attention_low = (
        in_order(pieces, my_z)[:, :, :GROUP_WIDTH].transpose(1, 0, 2).reshape(rows, width)
    )

    selfout_full = first_all[:, :width]
    crossq_full = first_all[:, width : 2 * width]
    crossout_full = first_all[:, 2 * width : 3 * width]
    crosskv_full = first_all[:, 3 * width : 5 * width]
    small_full = wide(first_all[:, 5 * width :].T)
    gain = small_full[:3]
    bias = small_full[3:17]
    ffnin_full = second_all[0]
    outer = [second_all[1, :, f * width : (f + 1) * width] for f in range(fan)]
    inner_bias = bias[10:14].reshape(devices, fan, part).transpose(1, 0, 2).reshape(-1)

    resid_one = wide(inputs) + matmul(attention_low, selfout_full) + bias[5]
    hidden_one = layer_norm(resid_one, gain[0], bias[0])
    hidden_one_low = rounded(hidden_one)
    cross_query = rounded(matmul(hidden_one_low, crossq_full) + bias[6])
    cross_pair = rounded(
        matmul(all_rows, crosskv_full) + jnp.concatenate([jnp.zeros((width,), jnp.float32), bias[7]])
    )
    cross_att, cross_lse = cross_forward(cross_query, cross_pair)
    resid_two = hidden_one + matmul(cross_att, crossout_full) + bias[8]
    hidden_two = layer_norm(resid_two, gain[1], bias[1])
    hidden_two_low = rounded(hidden_two)
    inner = matmul(hidden_two_low, ffnin_full) + inner_bias
    activated = rounded(gelu_exact(inner))

    def fan_part(array, f):
        return array[:, f * width : (f + 1) * width]

    resid_three = hidden_two + bias[9]
    for f in range(fan):
        resid_three = resid_three + matmul(fan_part(activated, f), outer[f])
    output = layer_norm(resid_three, gain[2], bias[2])

    _unused, norm_three = jax.vjp(layer_norm, resid_three, gain[2], bias[2])
    dresid_three, dgain_three, dshift_three = norm_three(wide(cotangent[0]))
    douter_low = rounded(dresid_three)
    grad_ffnout = rounded(weight_grad(activated, douter_low))
    reduce_ffnout = Chain(
        reduction(grad_ffnout.reshape(fan, 2, 2, X, C, Y, part, width), "cyxlh", lead=1)
    )
    _unused, gelu_back = jax.vjp(gelu_exact, inner)
    dactivated = jnp.concatenate([back_matmul(douter_low, block) for block in outer], axis=1)
    dinner_low = rounded(gelu_back(dactivated)[0])
    grad_ffnin = rounded(weight_grad(hidden_two_low, dinner_low))
    reduce_ffnin = Chain(reduction(sharded(grad_ffnin), "cyxlh"))

    _unused, norm_two = jax.vjp(layer_norm, resid_two, gain[1], bias[1])
    dresid_two, dgain_two, dshift_two = norm_two(dresid_three + back_matmul(dinner_low, ffnin_full))
    dcross_low = rounded(dresid_two)
    dcross_att = rounded(back_matmul(dcross_low, crossout_full))
    dcross_query, dcross_key, dcross_value = cross_backward(
        cross_query, cross_pair, dcross_att, cross_lse
    )
    dcross_query, dcross_key, dcross_value = meet(
        (dcross_query, dcross_key, dcross_value), reduce_ffnout, reduce_ffnin
    )

    dcross_all = jnp.concatenate([dcross_key, dcross_value], axis=1)
    dcross_all = dcross_all.reshape(C, X, 2, 2, chunk, 2 * width)

    def unspreading(array):
        for axis in "cxlh":
            size = getattr(grid, axis)
            arrays = yield [array[0]] + [grid.send(array[m], axis, m) for m in range(1, size)]
            array = rounded(total_of(arrays))
        return array

    unspread = Chain(unspreading(dcross_all))

    _unused, norm_one = jax.vjp(layer_norm, resid_one, gain[0], bias[0])
    dresid_one, dgain_one, dshift_one = norm_one(dresid_two + back_matmul(dcross_query, crossq_full))
    dbranch_low = rounded(dresid_one)
    datt_low = rounded(back_matmul(dbranch_low, selfout_full))
    datt_groups = jnp.pad(
        datt_low.reshape(rows, GROUPS, GROUP_WIDTH).transpose(1, 0, 2),
        ((0, 0), (0, 0), (0, 256 - GROUP_WIDTH)),
    )
    pieces = [take(datt_groups, my_z, 0)]
    for m in range(1, Z):
        pieces.append(swapped(take(datt_groups, my_z ^ m, 0), m))
    grad_mid = jnp.stack(
        [
            rounded(weight_grad(attention_low, dbranch_low)),
            rounded(weight_grad(hidden_one_low, dcross_query)),
            rounded(weight_grad(cross_att, dcross_low)),
        ]
    )
    grad_mid, pieces = meet((grad_mid, pieces), unspread)
    reduce_mid = Chain(reduction(grad_mid.reshape(3, 2, 2, X, C, Y, part, width), "cyxlh", lead=1))
    dout = jnp.stack(pieces)

    *far_other_grad, slopes, state = self_backward(
        tables["far other"], queries, dout, lse, far_other, attention, True, False
    )
    far_other_grad, slopes = meet(
        (far_other_grad, slopes), reduce_ffnout, reduce_mid, unspread
    )
    far_moved = [grid.send(grad, "c", 1) for grad in far_other_grad]
    *far_own_grad, slopes = self_backward(
        tables["far own"], queries, dout, state, far_own, slopes, False, False
    )
    far_own_grad, far_moved, slopes = meet(
        (far_own_grad, far_moved, slopes), unspread, reduce_ffnout, reduce_ffnin
    )
    far_grad = [rounded(total_of(pair)) for pair in zip(far_own_grad, far_moved)]
    far_moved = [grid.send(grad, "x", m) for m, grad in zip(far, far_grad)]
    near_other_grad, slopes = self_backward(
        tables["near other"], queries, dout, state, [near_other], slopes, False, False
    )
    near_other_grad, slopes = meet(
        (near_other_grad, slopes), unspread, reduce_ffnout, reduce_ffnin, reduce_mid
    )
    near_moved = grid.send(near_other_grad, "c", 1)

    dcross_pair = unspread.result
    bias_rows = jnp.stack(
        [
            dgain_one,
            dgain_two,
            dgain_three,
            dshift_one,
            dshift_two,
            dshift_three,
            column_sums(dbranch_low),
            column_sums(dcross_query),
            column_sums(dcross_pair[:, width:]),
            column_sums(dcross_low),
            column_sums(douter_low),
        ]
    )
    inner_sums = column_sums(dinner_low).reshape(fan, devices, part).transpose(1, 0, 2)
    bias_rows = jnp.concatenate([bias_rows, inner_sums.reshape(fan, width)], axis=0)
    bias_columns = jnp.pad(rounded(bias_rows.T), ((0, 0), (0, 128 - bias_rows.shape[0])))
    grad_late = jnp.concatenate([rounded(weight_grad(own_rows, dcross_pair)), bias_columns], axis=1)
    reduce_late = Chain(reduction(sharded(grad_late), "cyxlh"))
    spread_back = Chain(spreading(rounded(back_matmul(dcross_pair, crosskv_full))))

    near_own_grad, query_grad = self_backward(
        tables["near own"], queries, dout, state, [own_side], slopes, False, True
    )
    near_own_grad, near_moved, far_moved, query_grad = meet(
        (near_own_grad, near_moved, far_moved, query_grad)
    )

    far_query_grad = grid.send(query_grad[1::2], "z", 0, mirror=True)
    side_grad = rounded(total_of([near_own_grad, near_moved] + far_moved))
    query_grad = jnp.stack(
        [query_grad[m] if m % 2 == 0 else far_query_grad[m // 2] for m in range(GROUPS)]
    )
    dqkv = jnp.concatenate([query_grad.reshape(GROUPS * rows, QUERY), side_grad], axis=1)
    far_tokens_grad = rounded(back_matmul(dqkv[rows:], qkv_weight)).reshape(Z - 1, rows, width)
    dqkv, far_tokens_grad = meet(
        (dqkv, far_tokens_grad), reduce_ffnout, reduce_ffnin, reduce_mid, reduce_late, spread_back
    )
    third = grid.send(far_tokens_grad[2], "l", 1)
    first = grid.send(far_tokens_grad[0], "l", 1)
    grad_group = weight_grad(token_column, dqkv)
    sums = jnp.sum(wide(dqkv), axis=0)
    sums = jnp.stack([jnp.where(is_query, sums, 0.0), jnp.where(is_value, sums, 0.0)])
    sums = jnp.pad(rounded(sums), ((0, QUERY - GROUP_WIDTH - 2), (0, 0)))
    grad_group = jnp.concatenate(
        [grad_group[:, :GROUP_WIDTH], back_matmul(chosen, sums), grad_group[:, QUERY:]], axis=1
    )
    reduce_group = Chain(reduction(sharded(rounded(grad_group)), "cyx", final=False))
    tokens_base = dresid_one + back_matmul(dqkv[:rows], qkv_weight)
    second = grid.send(rounded(total_of([far_tokens_grad[1], third])), "h", 1)
    tokens_base = meet(tokens_base, reduce_group, spread_back, reduce_late)
    tokens_base = meet(tokens_base, reduce_group, spread_back, reduce_mid)
    tokens_base = meet(tokens_base, reduce_group, spread_back, reduce_late)
    pieces = parted(reduce_group.result.reshape(Z, part, PACK), "z", 0)
    tokens_grad = total_of([tokens_base, first, second])
    for chain in (reduce_ffnin, reduce_mid, reduce_late, reduce_late):
        chain.step(chain.pending)

    spot = jnp.arange(grid.seq, dtype=jnp.int32)
    spot_z = my_z ^ (spot % 2 * 2 + spot // 2 % 2)
    source = (spot_z * X + (my_x ^ (spot // Z % X))) * C + (my_c ^ (spot // (Z * X)))
    target = jnp.take(blocks[0], source // per_block) - home
    inside = (target >= 0) & (target < local_blocks)
    places = jnp.where(inside, target * per_block + source % per_block, -1)
    drows = spread_back.result.reshape(grid.seq, chunk, width)
    bank_grad = place_rows(drows, places, local_chunks).reshape(bank.shape[1], width)

    grad_groups = wide(in_order(pieces, my_z))
    sides = grad_groups[:, :, QUERY:]
    out_qkv = jnp.stack(
        [
            grad_groups[:, :, :GROUP_WIDTH],
            jnp.concatenate([sides[:, :, :128], sides[:, :, 256:320]], axis=2),
            jnp.concatenate([sides[:, :, 128:256], sides[:, :, 320:384]], axis=2),
        ]
    )
    out_qkv = out_qkv.transpose(2, 0, 1, 3).reshape(part, 3 * width)
    late_bias = jnp.sum(grad_groups[:, :, GROUP_WIDTH : GROUP_WIDTH + 2], axis=0)

    out_late, out_mid = reduce_late.result, reduce_mid.result
    out_ffnin = (
        reduce_ffnin.result.reshape(part, fan, devices, part)
        .transpose(0, 2, 1, 3)
        .reshape(part, hidden)
    )
    out_small = out_late[:, 2 * width :].T
    bias_grad = jnp.concatenate([out_small[3:6], late_bias.T, out_small[6:15]], axis=0)
    return (
        rounded(output)[None],
        tokens_grad[None],
        bank_grad[None],
        out_qkv,
        out_mid[0],
        out_mid[1],
        out_late[:, : 2 * width],
        out_mid[2],
        out_ffnin,
        reduce_ffnout.result.reshape(fan * part, width),
        out_small[:3],
        bias_grad,
    )


def solution(mesh):
    split = P("batch", "seq", None)
    shard = P(("seq", "batch"), None)
    flat = P(None, ("seq", "batch"))
    return jax.shard_map(
        functools.partial(body, Grid(mesh)),
        mesh=mesh,
        in_specs=(split, split, split, P("batch"), P("batch", None)) + (shard,) * 7 + (flat, flat),
        out_specs=(split, split, split) + (shard,) * 7 + (flat, flat),
        check_vma=False,
    )
```

profile of v0, /device:TPU:0, one launch (start us, length us, event | category | flops | bytes accessed | tf_op | source)
XLA Modules:
  0.0 531.3 jit_solution(7842512359983052783)
XLA Ops:
  18.8 7.2 %pick_rows.1 = bf16[16,64,768]{2,1,0:T(8,128)(2,1)} custom-call(s32[32]{0:T(128)} %pad_add_fusion.table, bf16[8,64,768]{2,1,0:T(8,128)(2,1)} %bitcast.435), custom_call_target="tpu_custom_call" | custom-call | tf_op jit(solution)/shard_map/pick_rows/pallas_call | solution.py:507
  43.3 4.7 collective-permute-done.3
  55.5 14.9 %collective-permute-done.8 = bf16[256,768]{1,0:T(8,128)(2,1)S(1)} collective-permute-done((bf16[256,768]{1,0:T(8,128)(2,1)S(1)}, bf16[256,768]{1,0:T(8,128)(2,1)S(1)}, u32[]{:S(2)}, u32[]{:S(2)}) %collective-permute-start.8) | collective-permute-done | bytes 393248 | tf_op jit(solution)/shard_map/ppermute | solution.py:88
  73.3 11.3 %collective-permute-done.7 = bf16[256,768]{1,0:T(8,128)(2,1)S(1)} collective-permute-done((bf16[256,768]{1,0:T(8,128)(2,1)S(1)}, bf16[256,768]{1,0:T(8,128)(2,1)S(1)}, u32[]{:S(2)}, u32[]{:S(2)}) %collective-permute-start.7) | collective-permute-done | bytes 393248 | tf_op jit(solution)/shard_map/ppermute | solution.py:88
  84.6 15.3 %collective-permute-done.9 = bf16[256,768]{1,0:T(8,128)(2,1)S(1)} collective-permute-done((bf16[256,768]{1,0:T(8,128)(2,1)S(1)}, bf16[256,768]{1,0:T(8,128)(2,1)S(1)}, u32[]{:S(2)}, u32[]{:S(2)}) %collective-permute-start.9) | collective-permute-done | bytes 393248 | tf_op jit(solution)/shard_map/ppermute | solution.py:88
  104.0 5.1 collective-permute-done.11
  112.0 14.2 %self_forward.4 = (f32[4,3,128,256]{3,2,1,0:T(8,128)}, f32[4,16,256]{2,1,0:T(8,128)}) custom-call(s32[9]{0:T(128)} %get-tuple-element.533.table, bf16[4,256,256]{2,1,0:T(8,128)(2,1)} %pad_maximum_fusion.11.query_in, bf16[1024,384]{1,0:T(8,128)(2,1)} %copy-done.83), custom_call_target="tpu_custom_call" | custom-call | flops 3221225472 | bytes 1572864 | tf_op jit(solution)/shard_map/self_forward/pallas_call | solution.py:317
  127.1 13.5 %self_forward.5 = (f32[4,3,128,256]{3,2,1,0:T(8,128)}, f32[4,16,256]{2,1,0:T(8,128)}) custom-call(s32[9]{0:T(128)} %get-tuple-element.535.table, bf16[4,256,256]{2,1,0:T(8,128)(2,1)} %pad_maximum_fusion.11.query_in, bf16[1024,384]{1,0:T(8,128)(2,1)} %copy-done.84, f32[4,3,128,256]{3,2,1,0:T(8,128)} %get-tuple-element.178.refs_1_, ...), custom_call_target="tpu_custom_call" | custom-call | flops 3221225472 | bytes 1572864 | tf_op jit(solution)/shard_map/self_forward/pallas_call | solution.py:317
  144.1 13.5 %self_forward.6 = (f32[4,3,128,256]{3,2,1,0:T(8,128)}, f32[4,16,256]{2,1,0:T(8,128)}) custom-call(s32[9]{0:T(128)} %get-tuple-element.534.table, bf16[4,256,256]{2,1,0:T(8,128)(2,1)} %pad_maximum_fusion.11.query_in, bf16[1024,384]{1,0:T(8,128)(2,1)} %copy-done.85, f32[4,3,128,256]{3,2,1,0:T(8,128)} %get-tuple-element.186.refs_1_, ...), custom_call_target="tpu_custom_call" | custom-call | flops 3221225472 | bytes 1572864 | tf_op jit(solution)/shard_map/self_forward/pallas_call | solution.py:317
  158.5 13.3 %self_forward.7 = (f32[4,256,256]{2,1,0:T(8,128)}, f32[4,8,256]{2,1,0:T(8,128)}) custom-call(s32[9]{0:T(128)} %add_add_fusion.4.table, bf16[4,256,256]{2,1,0:T(8,128)(2,1)} %pad_maximum_fusion.11.query_in, bf16[1024,384]{1,0:T(8,128)(2,1)} %copy-done.86, f32[4,3,128,256]{3,2,1,0:T(8,128)} %get-tuple-element.193.refs_1_, f32[4,16,256]{2,1,0:T(8,128)} %get-tuple-element.194.refs_2_), custom_call_target="tpu_custom_call" | custom-call | flops 3221225472 | bytes 1572864 | tf_op jit(solution)/shard_map/self_forward/pallas_call | solution.py:317
  178.1 7.5 %collective-permute-done.19 = bf16[256,256]{1,0:T(8,128)(2,1)S(1)} collective-permute-done((bf16[256,256]{1,0:T(8,128)(2,1)S(1)}, bf16[256,256]{1,0:T(8,128)(2,1)S(1)}, u32[]{:S(2)}, u32[]{:S(2)}) %collective-permute-start.19) | collective-permute-done | bytes 131104 | tf_op jit(solution)/shard_map/ppermute | solution.py:88
  185.6 5.0 collective-permute-done.21
  210.6 11.1 %cross_forward.1 = (bf16[256,768]{1,0:T(8,128)(2,1)}, f32[6,8,256]{2,1,0:T(8,128)}) custom-call(bf16[256,768]{1,0:T(8,128)(2,1)} %fusion.22.query, bf16[1024,1536]{1,0:T(8,128)(2,1)} %add_convert_fusion.keys.values, bf16[1024,1536]{1,0:T(8,128)(2,1)} %add_convert_fusion.keys.values), custom_call_target="tpu_custom_call" | custom-call | flops 1610612736 | bytes 3145728 | tf_op jit(solution)/shard_map/cross_forward/pallas_call | solution.py:441
  224.0 10.1 %multiply_convert_fusion = (bf16[256,3072]{1,0:T(8,128)(2,1)S(1)}, f32[256,3072]{1,0:T(8,128)S(1)}, f32[256,3072]{1,0:T(8,128)S(1)}) fusion(f32[3072]{0:T(1024)S(1)} %add.598, bf16[2,768,3072]{2,1,0:T(8,128)(2,1)} %all-gather.5.cloned.1.call-done, f32[256,768]{1,0:T(8,128)S(1)} %get-tuple-element.537, f32[768]{0:T(1024)S(1)} %get-tuple-element.384, ...), kind=kOutput, calls=%fused_computation.21 | convolution fusion | flops 1260847104 | bytes 13389824 | tf_op jit(solution)/shard_map/dot_general | solution.py:45
  264.1 13.7 %cross_backward.1 = (bf16[256,768]{1,0:T(8,128)(2,1)}, bf16[1024,768]{1,0:T(8,128)(2,1)}, bf16[1024,768]{1,0:T(8,128)(2,1)}) custom-call(bf16[256,768]{1,0:T(8,128)(2,1)} %fusion.22.query, bf16[1024,1536]{1,0:T(8,128)(2,1)} %add_convert_fusion.keys.values, bf16[1024,1536]{1,0:T(8,128)(2,1)} %add_convert_fusion.keys.values, ...), custom_call_target="tpu_custom_call" | custom-call | flops 4026531840 | bytes 6291456 | tf_op jit(solution)/shard_map/cross_backward/pallas_call | solution.py:469
  320.1 13.6 %self_backward.4 = (bf16[1024,384]{1,0:T(8,128)(2,1)}, f32[4,3,128,256]{3,2,1,0:T(8,128)}, f32[4,8,256]{2,1,0:T(8,128)}) custom-call(s32[9]{0:T(128)} %add_add_fusion.4.table, bf16[4,256,256]{2,1,0:T(8,128)(2,1)} %pad_maximum_fusion.11.query_in, bf16[4,256,256]{2,1,0:T(8,128)(2,1)} %pad_maximum_fusion.12.dout, f32[4,8,256]{2,1,0:T(8,128)} %get-tuple-element.220.state, ...), custom_call_target="tpu_custom_call" | custom-call | flops 4026531840 | bytes 3145728 | tf_op jit(solution)/shard_map/self_backward/pallas_call | solution.py:359
  347.3 14.6 %self_backward.5 = (bf16[1024,384]{1,0:T(8,128)(2,1)}, f32[4,3,128,256]{3,2,1,0:T(8,128)}) custom-call(s32[9]{0:T(128)} %get-tuple-element.534.table, bf16[4,256,256]{2,1,0:T(8,128)(2,1)} %pad_maximum_fusion.11.query_in, bf16[4,256,256]{2,1,0:T(8,128)(2,1)} %pad_maximum_fusion.12.dout, f32[4,8,256]{2,1,0:T(8,128)} %get-tuple-element.221.state, ...), custom_call_target="tpu_custom_call" | custom-call | flops 4026531840 | bytes 3145728 | tf_op jit(solution)/shard_map/self_backward/pallas_call | solution.py:359
  376.8 14.2 %self_backward.6 = (bf16[1024,384]{1,0:T(8,128)(2,1)}, f32[4,3,128,256]{3,2,1,0:T(8,128)}) custom-call(s32[9]{0:T(128)} %get-tuple-element.535.table, bf16[4,256,256]{2,1,0:T(8,128)(2,1)} %pad_maximum_fusion.11.query_in, bf16[4,256,256]{2,1,0:T(8,128)(2,1)} %pad_maximum_fusion.12.dout, f32[4,8,256]{2,1,0:T(8,128)} %get-tuple-element.221.state, ...), custom_call_target="tpu_custom_call" | custom-call | flops 4026531840 | bytes 3145728 | tf_op jit(solution)/shard_map/self_backward/pallas_call | solution.py:359
  405.1 15.7 %self_backward.7 = (bf16[1024,384]{1,0:T(8,128)(2,1)}, bf16[4,256,256]{2,1,0:T(8,128)(2,1)}) custom-call(s32[9]{0:T(128)} %get-tuple-element.533.table, bf16[4,256,256]{2,1,0:T(8,128)(2,1)} %pad_maximum_fusion.11.query_in, bf16[4,256,256]{2,1,0:T(8,128)(2,1)} %pad_maximum_fusion.12.dout, f32[4,8,256]{2,1,0:T(8,128)} %get-tuple-element.221.state, ...), custom_call_target="tpu_custom_call" | custom-call | flops 4026531840 | bytes 3145728 | tf_op jit(solution)/shard_map/self_backward/pallas_call | solution.py:359
  425.1 4.9 collective-permute-done.43
  455.1 7.4 %collective-permute-done.67 = bf16[24,3072]{1,0:T(8,128)(2,1)S(1)} collective-permute-done((bf16[24,3072]{1,0:T(8,128)(2,1)S(1)}, bf16[24,3072]{1,0:T(8,128)(2,1)S(1)}, u32[]{:S(2)}, u32[]{:S(2)}) %collective-permute-start.67) | collective-permute-done | bytes 147488 | tf_op jit(solution)/shard_map/ppermute | solution.py:88
  480.2 7.5 %collective-permute-done.53 = bf16[2,2,64,768]{3,2,1,0:T(8,128)(2,1)S(1)} collective-permute-done((bf16[2,2,64,768]{3,2,1,0:T(8,128)(2,1)S(1)}, bf16[2,2,64,768]{3,2,1,0:T(8,128)(2,1)S(1)}, u32[]{:S(2)}, u32[]{:S(2)}) %collective-permute-start.53) | collective-permute-done | bytes 393248 | tf_op jit(solution)/shard_map/ppermute | solution.py:88
  491.1 6.6 %collective-permute-done.64 = bf16[3,24,768]{2,1,0:T(8,128)(2,1)S(1)} collective-permute-done((bf16[3,24,768]{2,1,0:T(8,128)(2,1)S(1)}, bf16[3,24,768]{2,1,0:T(8,128)(2,1)S(1)}, u32[]{:S(2)}, u32[]{:S(2)}) %collective-permute-start.64) | collective-permute-done | bytes 110624 | tf_op jit(solution)/shard_map/ppermute | solution.py:88
  509.7 5.6 %place_rows.1 = f32[8,64,768]{2,1,0:T(8,128)} custom-call(s32[16]{0:T(128)} %and_select_fusion.3.table, bf16[16,64,768]{2,1,0:T(8,128)(2,1)} %bitcast.412), custom_call_target="tpu_custom_call" | custom-call | tf_op jit(solution)/shard_map/place_rows/pallas_call | solution.py:533
  (584 shorter events, 263.6 us)
Async XLA Ops:
  7.2 191.9 %all-gather.3.cloned.1.call-start = ((), (), s32[]{:S(2)}) async-start(), calls=%async_computation | async-start | bytes 6285312 | tf_op jit(solution)/shard_map/all_gather | solution.py:655
  12.0 212.0 %all-gather.5.cloned.1.call-start = ((), (), s32[]{:S(2)}) async-start(), calls=%async_computation.1 | async-start | bytes 9732096 | tf_op jit(solution)/shard_map/all_gather | solution.py:656
  55.5 29.1 %collective-permute-start.7 = (bf16[256,768]{1,0:T(8,128)(2,1)S(1)}, bf16[256,768]{1,0:T(8,128)(2,1)S(1)}, u32[]{:S(2)}, u32[]{:S(2)}) collective-permute-start(bf16[256,768]{1,0:T(8,128)(2,1)S(1)} %bitcast.445), channel_id=1, source_target_pairs={{0,8},{1,9},{2,10},{3,11},{4,12},{5,13},{6,14},{7,15},{8,0},{9,1},... | collective-permute-start | bytes 1179656 | tf_op jit(solution)/shard_map/ppermute | solution.py:88
  70.4 29.5 %collective-permute-start.9 = (bf16[256,768]{1,0:T(8,128)(2,1)S(1)}, bf16[256,768]{1,0:T(8,128)(2,1)S(1)}, u32[]{:S(2)}, u32[]{:S(2)}) collective-permute-start(bf16[256,768]{1,0:T(8,128)(2,1)S(1)} %collective-permute-done.8), channel_id=1, source_target_pairs={{0,8},{1,9},{2,10},{3,11},{4,12},{5,13},{6,14},{7,15},{8,0},{9,1},... | collective-permute-start | bytes 1179656 | tf_op jit(solution)/shard_map/ppermute | solution.py:88
  70.7 29.3 %collective-permute-start.10 = (bf16[2,2,1,64,768]{4,3,1,0,2:T(8,128)(2,1)S(1)}, bf16[2,2,1,64,768]{4,3,1,0,2:T(8,128)(2,1)S(1)}, u32[]{:S(2)}, u32[]{:S(2)}) collective-permute-start(bf16[2,2,1,64,768]{4,3,1,0,2:T(8,128)(2,1)S(1)} %get-tuple-element.455), channel_id=1, source_target_pairs={{0,4},{1,5},{2,6},{3,7},{4,0},{5,1},{6,2},{7,3},{8,12},{9,13},{10,... | collective-permute-start | bytes 1179656 | tf_op jit(solution)/shard_map/ppermute | solution.py:88
  109.1 31.4 %collective-permute-start.14 = (bf16[1024,384]{1,0:T(8,128)(2,1)S(1)}, bf16[1024,384]{1,0:T(8,128)(2,1)S(1)}, u32[]{:S(2)}, u32[]{:S(2)}) collective-permute-start(bf16[1024,384]{1,0:T(8,128)(2,1)S(1)} %add_convert_fusion.13.refs_0_), channel_id=1, source_target_pairs={{0,4},{1,5},{2,6},{3,7},{4,0},{5,1},{6,2},{7,3},{8,12},{9,13},{10,... | collective-permute-start | bytes 2359304 | tf_op jit(solution)/shard_map/ppermute | solution.py:88
  241.4 36.4 %collective-permute-start.24 = (bf16[4,2,2,2,2,24,768]{6,5,4,3,2,1,0:T(8,128)(2,1)}, bf16[4,2,2,2,2,24,768]{6,5,4,3,2,1,0:T(8,128)(2,1)}, u32[]{:S(2)}, u32[]{:S(2)}) collective-permute-start(bf16[4,2,2,2,2,24,768]{6,5,4,3,2,1,0:T(8,128)(2,1)} %get-tuple-element.418), channel_id=1, source_target_pairs={{0,2},{1,3},{2,0},{3,1},{4,6},{5,7},{6,4},{7,5},{8,10},{9,11},{10,... | collective-permute-start | bytes 7077896 | tf_op jit(solution)/shard_map/ppermute | solution.py:88
  251.2 26.6 %collective-permute-start.25 = (bf16[2,2,2,2,24,3072]{5,4,2,1,0,3:T(8,128)(2,1)}, bf16[2,2,2,2,24,3072]{5,4,2,1,0,3:T(8,128)(2,1)}, u32[]{:S(2)}, u32[]{:S(2)}) collective-permute-start(bf16[2,2,2,2,24,3072]{5,4,2,1,0,3:T(8,128)(2,1)} %bitcast.389), channel_id=1, source_target_pairs={{0,2},{1,3},{2,0},{3,1},{4,6},{5,7},{6,4},{7,5},{8,10},{9,11},{10,... | collective-permute-start | bytes 7077896 | tf_op jit(solution)/shard_map/ppermute | solution.py:88
  305.0 29.2 %collective-permute-start.30 = (bf16[4,2,2,2,24,768]{5,4,3,2,1,0:T(8,128)(2,1)}, bf16[4,2,2,2,24,768]{5,4,3,2,1,0:T(8,128)(2,1)}, u32[]{:S(2)}, u32[]{:S(2)}) collective-permute-start(bf16[4,2,2,2,24,768]{5,4,3,2,1,0:T(8,128)(2,1)} %get-tuple-element.428), channel_id=1, source_target_pairs={{0,1},{1,0},{2,3},{3,2},{4,5},{5,4},{6,7},{7,6},{8,9},{9,8},{10,11... | collective-permute-start | bytes 3538952 | tf_op jit(solution)/shard_map/ppermute | solution.py:88
  315.5 46.4 %collective-permute-start.36 = (bf16[2,2,2,24,3072]{4,3,2,1,0:T(8,128)(2,1)}, bf16[2,2,2,24,3072]{4,3,2,1,0:T(8,128)(2,1)}, u32[]{:S(2)}, u32[]{:S(2)}) collective-permute-start(bf16[2,2,2,24,3072]{4,3,2,1,0:T(8,128)(2,1)} %get-tuple-element.426), channel_id=1, source_target_pairs={{0,1},{1,0},{2,3},{3,2},{4,5},{5,4},{6,7},{7,6},{8,9},{9,8},{10,11... | collective-permute-start | bytes 3538952 | tf_op jit(solution)/shard_map/ppermute | solution.py:88
  335.1 26.9 %collective-permute-start.33 = (bf16[1024,384]{1,0:T(8,128)(2,1)}, bf16[1024,384]{1,0:T(8,128)(2,1)}, u32[]{:S(2)}, u32[]{:S(2)}) collective-permute-start(bf16[1024,384]{1,0:T(8,128)(2,1)} %get-tuple-element.231), channel_id=1, source_target_pairs={{0,2},{1,3},{2,0},{3,1},{4,6},{5,7},{6,4},{7,5},{8,10},{9,11},{10,... | collective-permute-start | bytes 2359304 | tf_op jit(solution)/shard_map/ppermute | solution.py:88
  337.9 24.0 %collective-permute-start.34 = (bf16[2,64,1536]{2,1,0:T(8,128)(2,1)}, bf16[2,64,1536]{2,1,0:T(8,128)(2,1)S(1)}, u32[]{:S(2)}, u32[]{:S(2)}) collective-permute-start(bf16[2,64,1536]{2,1,0:T(8,128)(2,1)} %get-tuple-element.451), channel_id=1, source_target_pairs={{0,8},{1,9},{2,10},{3,11},{4,12},{5,13},{6,14},{7,15},{8,0},{9,1},... | collective-permute-start | bytes 1179656 | tf_op jit(solution)/shard_map/ppermute | solution.py:88
  347.3 43.7 %collective-permute-start.40 = (bf16[3,2,2,2,24,768]{5,4,3,2,1,0:T(8,128)(2,1)}, bf16[3,2,2,2,24,768]{5,4,3,2,1,0:T(8,128)(2,1)S(1)}, u32[]{:S(2)}, u32[]{:S(2)}) collective-permute-start(bf16[3,2,2,2,24,768]{5,4,3,2,1,0:T(8,128)(2,1)} %get-tuple-element.430), channel_id=1, source_target_pairs={{0,1},{1,0},{2,3},{3,2},{4,5},{5,4},{6,7},{7,6},{8,9},{9,8},{10,11... | collective-permute-start | bytes 2654216 | tf_op jit(solution)/shard_map/ppermute | solution.py:88
  364.7 26.3 %collective-permute-start.37 = (bf16[64,1536]{1,0:T(8,128)(2,1)}, bf16[64,1536]{1,0:T(8,128)(2,1)S(1)}, u32[]{:S(2)}, u32[]{:S(2)}) collective-permute-start(bf16[64,1536]{1,0:T(8,128)(2,1)} %get-tuple-element.481), channel_id=1, source_target_pairs={{0,16},{1,17},{2,18},{3,19},{4,20},{5,21},{6,22},{7,23},{8,24},{9,... | collective-permute-start | bytes 589832 | tf_op jit(solution)/shard_map/ppermute | solution.py:88
  375.7 45.1 %collective-permute-start.42 = (bf16[1024,384]{1,0:T(8,128)(2,1)}, bf16[1024,384]{1,0:T(8,128)(2,1)}, u32[]{:S(2)}, u32[]{:S(2)}) collective-permute-start(bf16[1024,384]{1,0:T(8,128)(2,1)} %add_convert_fusion.11), channel_id=1, source_target_pairs={{0,4},{1,5},{2,6},{3,7},{4,0},{5,1},{6,2},{7,3},{8,12},{9,13},{10,... | collective-permute-start | bytes 2359304 | tf_op jit(solution)/shard_map/ppermute | solution.py:88
  393.7 27.2 %collective-permute-start.41 = (bf16[1024,384]{1,0:T(8,128)(2,1)}, bf16[1024,384]{1,0:T(8,128)(2,1)}, u32[]{:S(2)}, u32[]{:S(2)}) collective-permute-start(bf16[1024,384]{1,0:T(8,128)(2,1)} %get-tuple-element.252), channel_id=1, source_target_pairs={{0,2},{1,3},{2,0},{3,1},{4,6},{5,7},{6,4},{7,5},{8,10},{9,11},{10,... | collective-permute-start | bytes 2359304 | tf_op jit(solution)/shard_map/ppermute | solution.py:88
  394.6 43.6 %collective-permute-start.44 = (bf16[4,24,768]{2,1,0:T(8,128)(2,1)}, bf16[4,24,768]{2,1,0:T(8,128)(2,1)}, u32[]{:S(2)}, u32[]{:S(2)}) collective-permute-start(bf16[4,24,768]{2,1,0:T(8,128)(2,1)} %get-tuple-element.489), channel_id=1, source_target_pairs={{0,16},{1,17},{2,18},{3,19},{4,20},{5,21},{6,22},{7,23},{8,24},{9,... | collective-permute-start | bytes 442376 | tf_op jit(solution)/shard_map/ppermute | solution.py:88
  396.9 41.3 %collective-permute-start.45 = (bf16[2,24,3072]{2,1,0:T(8,128)(2,1)}, bf16[2,24,3072]{2,1,0:T(8,128)(2,1)}, u32[]{:S(2)}, u32[]{:S(2)}) collective-permute-start(bf16[2,24,3072]{2,1,0:T(8,128)(2,1)} %get-tuple-element.459), channel_id=1, source_target_pairs={{0,8},{1,9},{2,10},{3,11},{4,12},{5,13},{6,14},{7,15},{8,0},{9,1},... | collective-permute-start | bytes 884744 | tf_op jit(solution)/shard_map/ppermute | solution.py:88
  398.8 39.4 %collective-permute-start.46 = (bf16[3,2,2,24,768]{4,3,2,1,0:T(8,128)(2,1)}, bf16[3,2,2,24,768]{4,3,2,1,0:T(8,128)(2,1)}, u32[]{:S(2)}, u32[]{:S(2)}) collective-permute-start(bf16[3,2,2,24,768]{4,3,2,1,0:T(8,128)(2,1)} %get-tuple-element.448), channel_id=1, source_target_pairs={{0,4},{1,5},{2,6},{3,7},{4,0},{5,1},{6,2},{7,3},{8,12},{9,13},{10,... | collective-permute-start | bytes 1327112 | tf_op jit(solution)/shard_map/ppermute | solution.py:88
  442.4 25.1 %collective-permute-start.59 = (bf16[256,768]{1,0:T(8,128)(2,1)}, bf16[256,768]{1,0:T(8,128)(2,1)}, u32[]{:S(2)}, u32[]{:S(2)}) collective-permute-start(bf16[256,768]{1,0:T(8,128)(2,1)} %get-tuple-element.439), channel_id=1, source_target_pairs={{0,8},{1,9},{2,10},{3,11},{4,12},{5,13},{6,14},{7,15},{8,0},{9,1},... | collective-permute-start | bytes 1179656 | tf_op jit(solution)/shard_map/ppermute | solution.py:88
  445.2 26.7 %collective-permute-start.49 = (bf16[2,2,2,2,24,640]{5,4,2,1,0,3:T(8,128)(2,1)}, bf16[2,2,2,2,24,640]{5,4,2,1,0,3:T(8,128)(2,1)}, u32[]{:S(2)}, u32[]{:S(2)}) collective-permute-start(bf16[2,2,2,2,24,640]{5,4,2,1,0,3:T(8,128)(2,1)} %bitcast.393), channel_id=1, source_target_pairs={{0,2},{1,3},{2,0},{3,1},{4,6},{5,7},{6,4},{7,5},{8,10},{9,11},{10,... | collective-permute-start | bytes 1474568 | tf_op jit(solution)/shard_map/ppermute | solution.py:88
  445.9 24.9 %collective-permute-start.50 = (bf16[2,64,768]{2,1,0:T(8,128)(2,1)}, bf16[2,64,768]{2,1,0:T(8,128)(2,1)}, u32[]{:S(2)}, u32[]{:S(2)}) collective-permute-start(bf16[2,64,768]{2,1,0:T(8,128)(2,1)} %pad_maximum_fusion.20), channel_id=1, source_target_pairs={{0,8},{1,9},{2,10},{3,11},{4,12},{5,13},{6,14},{7,15},{8,0},{9,1},... | collective-permute-start | bytes 589832 | tf_op jit(solution)/shard_map/ppermute | solution.py:88
  467.5 39.7 %collective-permute-start.58 = (bf16[256,768]{1,0:T(8,128)(2,1)}, bf16[256,768]{1,0:T(8,128)(2,1)S(1)}, u32[]{:S(2)}, u32[]{:S(2)}) collective-permute-start(bf16[256,768]{1,0:T(8,128)(2,1)} %get-tuple-element.438), channel_id=1, source_target_pairs={{0,8},{1,9},{2,10},{3,11},{4,12},{5,13},{6,14},{7,15},{8,0},{9,1},... | collective-permute-start | bytes 1179656 | tf_op jit(solution)/shard_map/ppermute | solution.py:88
  470.8 36.6 %collective-permute-start.60 = (bf16[256,768]{1,0:T(8,128)(2,1)S(1)}, bf16[256,768]{1,0:T(8,128)(2,1)S(1)}, u32[]{:S(2)}, u32[]{:S(2)}) collective-permute-start(bf16[256,768]{1,0:T(8,128)(2,1)S(1)} %fusion.46), channel_id=1, source_target_pairs={{0,16},{1,17},{2,18},{3,19},{4,20},{5,21},{6,22},{7,23},{8,24},{9,... | collective-permute-start | bytes 1179656 | tf_op jit(solution)/shard_map/ppermute | solution.py:88
  (133 other events, 1229.8 us)
Sparse Core Ops, SparseCore 0:
  12.1 90.1 all-gather.2
  105.8 102.9 all-gather.4
where the time goes:
time: 537 us; the launch traced here: 531 us
  Pallas kernels  150 us (28%)
  waiting for transfers between devices  115 us (21%)
  local copies, waits for them, and re-layouts  74.5 us (14%)
  starting transfers between devices  68.2 us (13%)
  other arithmetic  57.3 us (11%)
  matrix products  48.8 us (9%)
  between operations  17.2 us (3%)
    ppermute x68, waiting for transfers between devices, send(): return lax.ppermute(array, ('seq', 'batch'), pairs)  115 us
    ppermute x68, starting transfers between devices, send(): return lax.ppermute(array, ('seq', 'batch'), pairs)  68.2 us
    pallas_call x4, Pallas kernels, self_backward(): pl.pallas_call(functools.partial(backward_kernel, rows, parts, first, las...  58.1 us
    pallas_call x4, Pallas kernels, self_forward(): pl.pallas_call(functools.partial(forward_kernel, rows, parts, first, last...  54.5 us
    convert_element_type x30, other arithmetic, rounded(): return values.astype(jnp.bfloat16)  29.5 us
    dot_general x11, matrix products, matmul(): return jnp.dot(left, right, preferred_element_type=jnp.float32)  23 us
    dot_general x12, matrix products, back_matmul(): lax.dot_general(left, right, LANES_IN, preferred_element_type=jnp.float32)  17.3 us
    squeeze x24, local copies, waits for them, and re-layouts, take(): return lax.dynamic_index_in_dim(array, index, axis, keepdims=False)  16 us
  transfers between devices with their start and end apart: 70, of which 22 were waited for; matrix products, arithmetic and copies ran while one was open for 25% of the time, Pallas kernels for 28%

commit v1 on v0

--- a/solution.py
+++ b/solution.py
@@ -563,6 +563,13 @@
     return values
 
 
+def hold(values, *chains):
+    values, pending = lax.optimization_barrier((values, [chain.pending for chain in chains]))
+    for chain, arrays in zip(chains, pending):
+        chain.pending = arrays
+    return values
+
+
 def total_of(arrays):
     total = wide(arrays[0])
     for array in arrays[1:]:
@@ -626,11 +633,11 @@
         return array.reshape(2, 2, X, C, Y, array.shape[0] // devices, array.shape[1])
 
     grouped = self_qkv.reshape(part, 3, GROUPS, GROUP_WIDTH)
-    extra = jnp.stack([biases[3], biases[4]], axis=1)
-    extra = jnp.broadcast_to(
-        jnp.pad(extra, ((0, 0), (0, QUERY - GROUP_WIDTH - 2)))[:, None],
-        (part, GROUPS, QUERY - GROUP_WIDTH),
-    )
+    spare = QUERY - GROUP_WIDTH
+    small = jnp.concatenate([gains, biases], axis=0).T
+    smalls = small.shape[1]
+    extra = jnp.pad(small, ((0, 0), (0, spare - smalls)))
+    extra = jnp.broadcast_to(extra[:, None], (part, GROUPS, spare))
     packed = jnp.concatenate(
         [
             grouped[:, 0],
@@ -644,20 +651,24 @@
     ).transpose(1, 0, 2)
     pieces = parted(packed, "z", 0)
 
-    small = jnp.concatenate([gains, biases], axis=0).T
-    small = jnp.pad(small, ((0, 0), (0, 128 - small.shape[1])))
-    first_pack = jnp.concatenate([self_out, cross_q, cross_out, cross_kv, small], axis=1)
-    inner_columns = (
-        ffn_in.reshape(part, devices, fan, part).transpose(0, 2, 1, 3).reshape(part, hidden)
-    )
-    outer_blocks = ffn_out.reshape(fan, part, width).transpose(1, 0, 2).reshape(part, hidden)
-    second_pack = jnp.stack([inner_columns, outer_blocks])
-    first_all = lax.all_gather(first_pack, ("seq", "batch"), axis=0, tiled=True)
-    second_all = lax.all_gather(second_pack, ("seq", "batch"), axis=1, tiled=True)
+    both = 2 * width
+    halves = hidden // both
+    planes = jnp.concatenate(
+        [
+            ffn_in.reshape(part, devices, halves, 2, part)
+            .transpose(2, 0, 3, 1, 4)
+            .reshape(halves, part, both),
+            ffn_out.reshape(halves, 2, part, width).transpose(0, 2, 1, 3).reshape(halves, part, both),
+            jnp.concatenate([self_out, cross_q], axis=1)[None],
+            jnp.pad(cross_out, ((0, 0), (0, width)))[None],
+            cross_kv[None],
+        ]
+    )
+    planes = lax.all_gather(planes, ("seq", "batch"), axis=1, tiled=True)
 
     pieces, inputs = lax.optimization_barrier((pieces, inputs))
     across = grid.send(inputs, "h", 1)
-    token_parts = [inputs, grid.send(inputs, "l", 1), across, grid.send(across, "l", 1)]
+    beside = grid.send(inputs, "l", 1)
 
     chunk = BANK_BLOCK * blocks.shape[1] // grid.seq
     per_block = BANK_BLOCK // chunk
@@ -688,8 +699,9 @@
     for axis in "yxc":
         pieces = [gathered] + [grid.send(gathered, axis, m) for m in range(1, getattr(grid, axis))]
         if axis == "y":
-            pieces = meet(pieces, retrieve)
+            pieces, across = meet((pieces, across), retrieve)
         gathered = in_order(pieces, me[axis])
+    token_parts = [inputs, beside, across, grid.send(across, "l", 1)]
     qkv_group = gathered.transpose(3, 1, 0, 2, 4, 5).reshape(width, PACK)
     column = jnp.arange(PACK, dtype=jnp.int32)
     real = (column < GROUP_WIDTH) | (column >= QUERY)
@@ -700,7 +712,7 @@
     line = jnp.where(is_query | is_value, local + my_z * GROUP_WIDTH, -1)
     chosen = (jnp.arange(width, dtype=jnp.int32)[:, None] == line[None]).astype(jnp.bfloat16)
     picked_bias = weight_grad(qkv_group[:, GROUP_WIDTH:QUERY], chosen)
-    qkv_bias = jnp.where(is_query, picked_bias[0], picked_bias[1])
+    qkv_bias = jnp.where(is_query, picked_bias[3 + 3], picked_bias[3 + 4])
     qkv_weight = jnp.where(real[None], qkv_group, jnp.zeros_like(qkv_group))
 
     qkv_weight, qkv_bias, token_parts = meet((qkv_weight, qkv_bias, token_parts), retrieve)
@@ -762,16 +774,18 @@
         in_order(pieces, my_z)[:, :, :GROUP_WIDTH].transpose(1, 0, 2).reshape(rows, width)
     )
 
-    selfout_full = first_all[:, :width]
-    crossq_full = first_all[:, width : 2 * width]
-    crossout_full = first_all[:, 2 * width : 3 * width]
-    crosskv_full = first_all[:, 3 * width : 5 * width]
-    small_full = wide(first_all[:, 5 * width :].T)
+    ffnin_full = [planes[k] for k in range(halves)]
+    outer = [
+        [planes[halves + k, :, j * width : (j + 1) * width] for j in range(2)] for k in range(halves)
+    ]
+    selfout_full = planes[2 * halves, :, :width]
+    crossq_full = planes[2 * halves, :, width:]
+    crossout_full = planes[2 * halves + 1, :, :width]
+    crosskv_full = planes[2 * halves + 2]
+    small_full = wide(qkv_group[:, GROUP_WIDTH : GROUP_WIDTH + smalls].T)
     gain = small_full[:3]
-    bias = small_full[3:17]
-    ffnin_full = second_all[0]
-    outer = [second_all[1, :, f * width : (f + 1) * width] for f in range(fan)]
-    inner_bias = bias[10:14].reshape(devices, fan, part).transpose(1, 0, 2).reshape(-1)
+    bias = small_full[3:]
+    inner_bias = bias[10:14].reshape(devices, fan, part).transpose(1, 0, 2).reshape(halves, both)
 
     resid_one = wide(inputs) + matmul(attention_low, selfout_full) + bias[5]
     hidden_one = layer_norm(resid_one, gain[0], bias[0])
@@ -784,32 +798,35 @@
     resid_two = hidden_one + matmul(cross_att, crossout_full) + bias[8]
     hidden_two = layer_norm(resid_two, gain[1], bias[1])
     hidden_two_low = rounded(hidden_two)
-    inner = matmul(hidden_two_low, ffnin_full) + inner_bias
-    activated = rounded(gelu_exact(inner))
-
-    def fan_part(array, f):
-        return array[:, f * width : (f + 1) * width]
-
+    inner = [matmul(hidden_two_low, plane) + inner_bias[k] for k, plane in enumerate(ffnin_full)]
+    activated = [rounded(gelu_exact(values)) for values in inner]
     resid_three = hidden_two + bias[9]
-    for f in range(fan):
-        resid_three = resid_three + matmul(fan_part(activated, f), outer[f])
+    for values, sides in zip(activated, outer):
+        for j, plane in enumerate(sides):
+            resid_three = resid_three + matmul(values[:, j * width : (j + 1) * width], plane)
     output = layer_norm(resid_three, gain[2], bias[2])
 
     _unused, norm_three = jax.vjp(layer_norm, resid_three, gain[2], bias[2])
     dresid_three, dgain_three, dshift_three = norm_three(wide(cotangent[0]))
     douter_low = rounded(dresid_three)
-    grad_ffnout = rounded(weight_grad(activated, douter_low))
+    grad_ffnout = jnp.stack([rounded(weight_grad(values, douter_low)) for values in activated])
     reduce_ffnout = Chain(
         reduction(grad_ffnout.reshape(fan, 2, 2, X, C, Y, part, width), "cyxlh", lead=1)
     )
-    _unused, gelu_back = jax.vjp(gelu_exact, inner)
-    dactivated = jnp.concatenate([back_matmul(douter_low, block) for block in outer], axis=1)
-    dinner_low = rounded(gelu_back(dactivated)[0])
-    grad_ffnin = rounded(weight_grad(hidden_two_low, dinner_low))
-    reduce_ffnin = Chain(reduction(sharded(grad_ffnin), "cyxlh"))
+    dinner_low = []
+    for values, sides in zip(inner, outer):
+        _unused, gelu_back = jax.vjp(gelu_exact, values)
+        slopes = jnp.concatenate([back_matmul(douter_low, plane) for plane in sides], axis=1)
+        dinner_low.append(rounded(gelu_back(slopes)[0]))
+    grad_ffnin = jnp.stack([rounded(weight_grad(hidden_two_low, values)) for values in dinner_low])
+    reduce_ffnin = Chain(
+        reduction(grad_ffnin.reshape(halves, 2, 2, X, C, Y, part, both), "cxylh", lead=1)
+    )
 
     _unused, norm_two = jax.vjp(layer_norm, resid_two, gain[1], bias[1])
-    dresid_two, dgain_two, dshift_two = norm_two(dresid_three + back_matmul(dinner_low, ffnin_full))
+    dresid_two, dgain_two, dshift_two = norm_two(
+        sum((back_matmul(*pair) for pair in zip(dinner_low, ffnin_full)), dresid_three)
+    )
     dcross_low = rounded(dresid_two)
     dcross_att = rounded(back_matmul(dcross_low, crossout_full))
     dcross_query, dcross_key, dcross_value = cross_backward(
@@ -871,8 +888,8 @@
     near_other_grad, slopes = self_backward(
         tables["near other"], queries, dout, state, [near_other], slopes, False, False
     )
-    near_other_grad, slopes = meet(
-        (near_other_grad, slopes), unspread, reduce_ffnout, reduce_ffnin, reduce_mid
+    near_other_grad, far_moved, slopes = meet(
+        (near_other_grad, far_moved, slopes), unspread, reduce_ffnin, reduce_mid
     )
     near_moved = grid.send(near_other_grad, "c", 1)
 
@@ -892,7 +909,8 @@
             column_sums(douter_low),
         ]
     )
-    inner_sums = column_sums(dinner_low).reshape(fan, devices, part).transpose(1, 0, 2)
+    inner_sums = jnp.concatenate([column_sums(values) for values in dinner_low])
+    inner_sums = inner_sums.reshape(fan, devices, part).transpose(1, 0, 2)
     bias_rows = jnp.concatenate([bias_rows, inner_sums.reshape(fan, width)], axis=0)
     bias_columns = jnp.pad(rounded(bias_rows.T), ((0, 0), (0, 128 - bias_rows.shape[0])))
     grad_late = jnp.concatenate([rounded(weight_grad(own_rows, dcross_pair)), bias_columns], axis=1)
@@ -902,8 +920,8 @@
     near_own_grad, query_grad = self_backward(
         tables["near own"], queries, dout, state, [own_side], slopes, False, True
     )
-    near_own_grad, near_moved, far_moved, query_grad = meet(
-        (near_own_grad, near_moved, far_moved, query_grad)
+    near_own_grad, near_moved, query_grad = hold(
+        (near_own_grad, near_moved, query_grad), reduce_late, spread_back, reduce_ffnin, reduce_mid
     )
 
     far_query_grad = grid.send(query_grad[1::2], "z", 0, mirror=True)
@@ -921,19 +939,19 @@
     grad_group = weight_grad(token_column, dqkv)
     sums = jnp.sum(wide(dqkv), axis=0)
     sums = jnp.stack([jnp.where(is_query, sums, 0.0), jnp.where(is_value, sums, 0.0)])
-    sums = jnp.pad(rounded(sums), ((0, QUERY - GROUP_WIDTH - 2), (0, 0)))
+    sums = jnp.pad(rounded(sums), ((0, spare - 2), (0, 0)))
     grad_group = jnp.concatenate(
         [grad_group[:, :GROUP_WIDTH], back_matmul(chosen, sums), grad_group[:, QUERY:]], axis=1
     )
     reduce_group = Chain(reduction(sharded(rounded(grad_group)), "cyx", final=False))
     tokens_base = dresid_one + back_matmul(dqkv[:rows], qkv_weight)
+    tokens_base, third = meet((tokens_base, third), reduce_group, spread_back, reduce_late)
     second = grid.send(rounded(total_of([far_tokens_grad[1], third])), "h", 1)
-    tokens_base = meet(tokens_base, reduce_group, spread_back, reduce_late)
-    tokens_base = meet(tokens_base, reduce_group, spread_back, reduce_mid)
-    tokens_base = meet(tokens_base, reduce_group, spread_back, reduce_late)
+    tokens_base = meet(tokens_base, reduce_group, spread_back, reduce_late, reduce_mid)
+    tokens_base = meet(tokens_base, reduce_group, spread_back, reduce_ffnin)
     pieces = parted(reduce_group.result.reshape(Z, part, PACK), "z", 0)
     tokens_grad = total_of([tokens_base, first, second])
-    for chain in (reduce_ffnin, reduce_mid, reduce_late, reduce_late):
+    for chain in (reduce_ffnout, reduce_mid, reduce_late, reduce_late):
         chain.step(chain.pending)
 
     spot = jnp.arange(grid.seq, dtype=jnp.int32)
@@ -959,8 +977,8 @@
 
     out_late, out_mid = reduce_late.result, reduce_mid.result
     out_ffnin = (
-        reduce_ffnin.result.reshape(part, fan, devices, part)
-        .transpose(0, 2, 1, 3)
+        reduce_ffnin.result.reshape(halves, part, 2, devices, part)
+        .transpose(1, 3, 0, 2, 4)
         .reshape(part, hidden)
     )
     out_small = out_late[:, 2 * width :].T

time: 537 us -> 574 us (1.069)
  waiting for transfers between devices: 115 us -> 150 us
  matrix products: 48.8 us -> 58.2 us
  other arithmetic: 57.3 us -> 50.9 us
    ppermute x68, waiting for transfers between devices: 115 us -> 150 us  [send(): return lax.ppermute(array, ('seq', 'batch'), pairs)]
    dot_general x12 -> x13, matrix products: 17.3 us -> 22.4 us  [back_matmul(): lax.dot_general(left, right, LANES_IN, preferred_element_type=jnp.float32)]
    dot_general x11 -> x12, matrix products: 23 us -> 27.1 us  [matmul(): return jnp.dot(left, right, preferred_element_type=jnp.float32)]
    convert_element_type x30 -> x31, other arithmetic: 29.5 us -> 25.4 us  [rounded(): return values.astype(jnp.bfloat16)]
    squeeze x24 -> x23, local copies, waits for them, and re-layouts: 16 us -> 12.8 us  [take(): return lax.dynamic_index_in_dim(array, index, axis, keepdims=False)]
    unnamed x190 -> x210, local copies, waits for them, and re-layouts: 12.4 us -> 15.6 us
    dynamic_slice x17 -> x19, local copies, waits for them, and re-layouts: 13.5 us -> 13.7 us  [take(): return lax.dynamic_index_in_dim(array, index, axis, keepdims=False)]
  transfers between devices with their start and end apart: 70 -> 69, of which waited for: 22 -> 26; matrix products, arithmetic and copies ran while one was open for 25% -> 17% of each run, Pallas kernels for 28% -> 25%
where the time goes in v1:
time: 574 us; the launch traced here: 569 us
  Pallas kernels  152 us (26%)
  waiting for transfers between devices  150 us (26%)
  local copies, waits for them, and re-layouts  73.1 us (13%)
  starting transfers between devices  67.8 us (12%)
  matrix products  58.2 us (10%)
  other arithmetic  50.9 us (9%)
  between operations  17.5 us (3%)
    ppermute x68, waiting for transfers between devices, send(): return lax.ppermute(array, ('seq', 'batch'), pairs)  150 us
    ppermute x68, starting transfers between devices, send(): return lax.ppermute(array, ('seq', 'batch'), pairs)  67.8 us
    pallas_call x4, Pallas kernels, self_backward(): pl.pallas_call(functools.partial(backward_kernel, rows, parts, first, las...  58.5 us
    pallas_call x4, Pallas kernels, self_forward(): pl.pallas_call(functools.partial(forward_kernel, rows, parts, first, last...  55.3 us
    dot_general x12, matrix products, matmul(): return jnp.dot(left, right, preferred_element_type=jnp.float32)  27.1 us
    convert_element_type x31, other arithmetic, rounded(): return values.astype(jnp.bfloat16)  25.4 us
    dot_general x13, matrix products, back_matmul(): lax.dot_general(left, right, LANES_IN, preferred_element_type=jnp.float32)  22.4 us
    unnamed x210, local copies, waits for them, and re-layouts  15.6 us
  transfers between devices with their start and end apart: 69, of which 26 were waited for; matrix products, arithmetic and copies ran while one was open for 17% of the time, Pallas kernels for 25%

profile of v1, /device:TPU:0, one launch (start us, length us, event | category | flops | bytes accessed | tf_op | source)
XLA Modules:
  0.0 569.2 jit_solution(16897334758170444700)
XLA Ops:
  14.4 7.9 %pick_rows.1 = bf16[16,64,768]{2,1,0:T(8,128)(2,1)} custom-call(s32[32]{0:T(128)} %pad_add_fusion.table, bf16[8,64,768]{2,1,0:T(8,128)(2,1)} %bitcast.486), custom_call_target="tpu_custom_call" | custom-call | tf_op jit(solution)/shard_map/pick_rows/pallas_call | solution.py:507
  44.5 14.6 %collective-permute-done.4 = bf16[256,768]{1,0:T(8,128)(2,1)S(1)} collective-permute-done((bf16[256,768]{1,0:T(8,128)(2,1)S(1)}, bf16[256,768]{1,0:T(8,128)(2,1)S(1)}, u32[]{:S(2)}, u32[]{:S(2)}) %collective-permute-start.4) | collective-permute-done | bytes 393248 | tf_op jit(solution)/shard_map/ppermute | solution.py:88
  63.2 10.7 %collective-permute-done.6 = bf16[2,4,24,640]{3,2,1,0:T(8,128)(2,1)S(1)} collective-permute-done((bf16[2,4,24,640]{3,2,1,0:T(8,128)(2,1)S(1)}, bf16[2,4,24,640]{3,2,1,0:T(8,128)(2,1)S(1)}, u32[]{:S(2)}, u32[]{:S(2)}) %collective-permute-start.6) | collective-permute-done | bytes 245792 | tf_op jit(solution)/shard_map/ppermute | solution.py:88
  79.3 15.8 %collective-permute-done.8 = bf16[256,768]{1,0:T(8,128)(2,1)S(1)} collective-permute-done((bf16[256,768]{1,0:T(8,128)(2,1)S(1)}, bf16[256,768]{1,0:T(8,128)(2,1)S(1)}, u32[]{:S(2)}, u32[]{:S(2)}) %collective-permute-start.8) | collective-permute-done | bytes 393248 | tf_op jit(solution)/shard_map/ppermute | solution.py:88
  95.1 8.2 %collective-permute-done.9 = bf16[256,768]{1,0:T(8,128)(2,1)S(1)} collective-permute-done((bf16[256,768]{1,0:T(8,128)(2,1)S(1)}, bf16[256,768]{1,0:T(8,128)(2,1)S(1)}, u32[]{:S(2)}, u32[]{:S(2)}) %collective-permute-start.9) | collective-permute-done | bytes 393248 | tf_op jit(solution)/shard_map/ppermute | solution.py:88
  107.3 11.9 %collective-permute-done.11 = bf16[2,256,256]{2,1,0:T(8,128)(2,1)S(1)} collective-permute-done((bf16[2,256,256]{2,1,0:T(8,128)(2,1)S(1)}, bf16[2,256,256]{2,1,0:T(8,128)(2,1)S(1)}, u32[]{:S(2)}, u32[]{:S(2)}) %collective-permute-start.11) | collective-permute-done | bytes 262176 | tf_op jit(solution)/shard_map/ppermute | solution.py:88
  121.3 14.3 %self_forward.4 = (f32[4,3,128,256]{3,2,1,0:T(8,128)}, f32[4,16,256]{2,1,0:T(8,128)}) custom-call(s32[9]{0:T(128)} %get-tuple-element.569.table, bf16[4,256,256]{2,1,0:T(8,128)(2,1)} %pad_maximum_fusion.13.query_in, bf16[1024,384]{1,0:T(8,128)(2,1)} %copy-done.91), custom_call_target="tpu_custom_call" | custom-call | flops 3221225472 | bytes 1572864 | tf_op jit(solution)/shard_map/self_forward/pallas_call | solution.py:317
  137.2 13.5 %self_forward.5 = (f32[4,3,128,256]{3,2,1,0:T(8,128)}, f32[4,16,256]{2,1,0:T(8,128)}) custom-call(s32[9]{0:T(128)} %get-tuple-element.571.table, bf16[4,256,256]{2,1,0:T(8,128)(2,1)} %pad_maximum_fusion.13.query_in, bf16[1024,384]{1,0:T(8,128)(2,1)} %copy-done.92, f32[4,3,128,256]{3,2,1,0:T(8,128)} %get-tuple-element.189.refs_1_, ...), custom_call_target="tpu_custom_call" | custom-call | flops 3221225472 | bytes 1572864 | tf_op jit(solution)/shard_map/self_forward/pallas_call | solution.py:317
  159.8 13.4 %self_forward.6 = (f32[4,3,128,256]{3,2,1,0:T(8,128)}, f32[4,16,256]{2,1,0:T(8,128)}) custom-call(s32[9]{0:T(128)} %get-tuple-element.570.table, bf16[4,256,256]{2,1,0:T(8,128)(2,1)} %pad_maximum_fusion.13.query_in, bf16[1024,384]{1,0:T(8,128)(2,1)} %collective-permute-done.14.refs_0_, f32[4,3,128,256]{3,2,1,0:T(8,128)} %get-tuple-element.197.refs_1_, ...), custom_call_target="tpu_custom_call" | custom-call | flops 3221225472 | bytes 1572864 | tf_op jit(solution)/shard_map/self_forward/pallas_call | solution.py:317
  174.4 14.1 %self_forward.7 = (f32[4,256,256]{2,1,0:T(8,128)}, f32[4,8,256]{2,1,0:T(8,128)}) custom-call(s32[9]{0:T(128)} %add_add_fusion.4.table, bf16[4,256,256]{2,1,0:T(8,128)(2,1)} %pad_maximum_fusion.13.query_in, bf16[1024,384]{1,0:T(8,128)(2,1)} %copy-done.93, f32[4,3,128,256]{3,2,1,0:T(8,128)} %get-tuple-element.204.refs_1_, f32[4,16,256]{2,1,0:T(8,128)} %get-tuple-element.205.refs_2_), custom_call_target="tpu_custom_call" | custom-call | flops 3221225472 | bytes 1572864 | tf_op jit(solution)/shard_map/self_forward/pallas_call | solution.py:317
  201.6 6.9 %collective-permute-done.20 = bf16[256,256]{1,0:T(8,128)(2,1)S(1)} collective-permute-done((bf16[256,256]{1,0:T(8,128)(2,1)S(1)}, bf16[256,256]{1,0:T(8,128)(2,1)S(1)}, u32[]{:S(2)}, u32[]{:S(2)}) %collective-permute-start.20) | collective-permute-done | bytes 131104 | tf_op jit(solution)/shard_map/ppermute | solution.py:88
  217.8 5.7 add_convert_fusion.keys.values
  226.0 11.1 %cross_forward.1 = (bf16[256,768]{1,0:T(8,128)(2,1)}, f32[6,8,256]{2,1,0:T(8,128)}) custom-call(bf16[256,768]{1,0:T(8,128)(2,1)} %fusion.30.query, bf16[1024,1536]{1,0:T(8,128)(2,1)} %add_convert_fusion.keys.values, bf16[1024,1536]{1,0:T(8,128)(2,1)} %add_convert_fusion.keys.values), custom_call_target="tpu_custom_call" | custom-call | flops 1610612736 | bytes 3145728 | tf_op jit(solution)/shard_map/cross_forward/pallas_call | solution.py:441
  239.7 6.1 %multiply_convert_fusion = (bf16[256,1536]{1,0:T(8,128)(2,1)S(1)}, f32[256,1536]{1,0:T(8,128)S(1)}, f32[256,1536]{1,0:T(8,128)S(1)}) fusion(f32[1536]{0:T(1024)S(1)} %add.616, bf16[256,768]{1,0:T(8,128)(2,1)S(1)} %fusion.48, bf16[7,768,1536]{2,1,0:T(8,128)(2,1)} %all-gather.2.cloned.1.call-done), kind=kOutput, calls=%fused_computation.60 | convolution fusion | flops 629932032 | bytes 6690816 | tf_op jit(solution)/shard_map/dot_general | solution.py:45
  288.5 13.4 %cross_backward.1 = (bf16[256,768]{1,0:T(8,128)(2,1)}, bf16[1024,768]{1,0:T(8,128)(2,1)}, bf16[1024,768]{1,0:T(8,128)(2,1)}) custom-call(bf16[256,768]{1,0:T(8,128)(2,1)} %fusion.30.query, bf16[1024,1536]{1,0:T(8,128)(2,1)} %add_convert_fusion.keys.values, bf16[1024,1536]{1,0:T(8,128)(2,1)} %add_convert_fusion.keys.values, ...), custom_call_target="tpu_custom_call" | custom-call | flops 4026531840 | bytes 6291456 | tf_op jit(solution)/shard_map/cross_backward/pallas_call | solution.py:469
  344.4 14.6 %self_backward.4 = (bf16[1024,384]{1,0:T(8,128)(2,1)}, f32[4,3,128,256]{3,2,1,0:T(8,128)}, f32[4,8,256]{2,1,0:T(8,128)}) custom-call(s32[9]{0:T(128)} %add_add_fusion.4.table, bf16[4,256,256]{2,1,0:T(8,128)(2,1)} %pad_maximum_fusion.13.query_in, bf16[4,256,256]{2,1,0:T(8,128)(2,1)} %pad_maximum_fusion.14.dout, f32[4,8,256]{2,1,0:T(8,128)} %get-tuple-element.231.state, ...), custom_call_target="tpu_custom_call" | custom-call | flops 4026531840 | bytes 3145728 | tf_op jit(solution)/shard_map/self_backward/pallas_call | solution.py:359
  369.9 14.2 %self_backward.5 = (bf16[1024,384]{1,0:T(8,128)(2,1)}, f32[4,3,128,256]{3,2,1,0:T(8,128)}) custom-call(s32[9]{0:T(128)} %get-tuple-element.570.table, bf16[4,256,256]{2,1,0:T(8,128)(2,1)} %pad_maximum_fusion.13.query_in, bf16[4,256,256]{2,1,0:T(8,128)(2,1)} %pad_maximum_fusion.14.dout, f32[4,8,256]{2,1,0:T(8,128)} %get-tuple-element.232.state, ...), custom_call_target="tpu_custom_call" | custom-call | flops 4026531840 | bytes 3145728 | tf_op jit(solution)/shard_map/self_backward/pallas_call | solution.py:359
  385.7 12.1 %collective-permute-done.35 = bf16[4,2,2,24,768]{4,3,2,1,0:T(8,128)(2,1)} collective-permute-done((bf16[4,2,2,24,768]{4,3,2,1,0:T(8,128)(2,1)}, bf16[4,2,2,24,768]{4,3,2,1,0:T(8,128)(2,1)}, u32[]{:S(2)}, u32[]{:S(2)}) %collective-permute-start.35) | collective-permute-done | bytes 589856 | tf_op jit(solution)/shard_map/ppermute | solution.py:88
  404.7 14.2 %self_backward.6 = (bf16[1024,384]{1,0:T(8,128)(2,1)}, f32[4,3,128,256]{3,2,1,0:T(8,128)}) custom-call(s32[9]{0:T(128)} %get-tuple-element.571.table, bf16[4,256,256]{2,1,0:T(8,128)(2,1)} %pad_maximum_fusion.13.query_in, bf16[4,256,256]{2,1,0:T(8,128)(2,1)} %pad_maximum_fusion.14.dout, f32[4,8,256]{2,1,0:T(8,128)} %get-tuple-element.232.state, ...), custom_call_target="tpu_custom_call" | custom-call | flops 4026531840 | bytes 3145728 | tf_op jit(solution)/shard_map/self_backward/pallas_call | solution.py:359
  434.8 15.6 %self_backward.7 = (bf16[1024,384]{1,0:T(8,128)(2,1)}, bf16[4,256,256]{2,1,0:T(8,128)(2,1)}) custom-call(s32[9]{0:T(128)} %get-tuple-element.569.table, bf16[4,256,256]{2,1,0:T(8,128)(2,1)} %pad_maximum_fusion.13.query_in, bf16[4,256,256]{2,1,0:T(8,128)(2,1)} %pad_maximum_fusion.14.dout, f32[4,8,256]{2,1,0:T(8,128)} %get-tuple-element.232.state, ...), custom_call_target="tpu_custom_call" | custom-call | flops 4026531840 | bytes 3145728 | tf_op jit(solution)/shard_map/self_backward/pallas_call | solution.py:359
  455.9 6.4 %collective-permute-done.46 = bf16[2,256,256]{2,1,0:T(8,128)(2,1)S(1)} collective-permute-done((bf16[2,256,256]{2,1,0:T(8,128)(2,1)S(1)}, bf16[2,256,256]{2,1,0:T(8,128)(2,1)S(1)}, u32[]{:S(2)}, u32[]{:S(2)}) %collective-permute-start.46) | collective-permute-done | bytes 262176 | tf_op jit(solution)/shard_map/ppermute | solution.py:88
  485.5 9.2 %collective-permute-done.48 = bf16[256,768]{1,0:T(8,128)(2,1)S(1)} collective-permute-done((bf16[256,768]{1,0:T(8,128)(2,1)S(1)}, bf16[256,768]{1,0:T(8,128)(2,1)S(1)}, u32[]{:S(2)}, u32[]{:S(2)}) %collective-permute-start.48) | collective-permute-done | bytes 393248 | tf_op jit(solution)/shard_map/ppermute | solution.py:88
  516.3 11.3 %collective-permute-done.64 = bf16[3,24,768]{2,1,0:T(8,128)(2,1)S(1)} collective-permute-done((bf16[3,24,768]{2,1,0:T(8,128)(2,1)S(1)}, bf16[3,24,768]{2,1,0:T(8,128)(2,1)S(1)}, u32[]{:S(2)}, u32[]{:S(2)}) %collective-permute-start.64) | collective-permute-done | bytes 110624 | tf_op jit(solution)/shard_map/ppermute | solution.py:88
  527.6 5.7 %collective-permute-done.65 = bf16[2,24,1664]{2,1,0:T(8,128)(2,1)S(1)} collective-permute-done((bf16[2,24,1664]{2,1,0:T(8,128)(2,1)S(1)}, bf16[2,24,1664]{2,1,0:T(8,128)(2,1)S(1)}, u32[]{:S(2)}, u32[]{:S(2)}) %collective-permute-start.65) | collective-permute-done | bytes 159776 | tf_op jit(solution)/shard_map/ppermute | solution.py:88
  (617 shorter events, 280.8 us)
Async XLA Ops:
  7.2 208.3 %all-gather.2.cloned.1.call-start = ((), (), s32[]{:S(2)}) async-start(), calls=%async_computation | async-start | bytes 17031168 | tf_op jit(solution)/shard_map/all_gather | solution.py:667
  23.9 35.2 %collective-permute-start.5 = (bf16[2,2,2,1,64,768]{5,4,2,1,0,3:T(8,128)(2,1)S(1)}, bf16[2,2,2,1,64,768]{5,4,2,1,0,3:T(8,128)(2,1)S(1)}, u32[]{:S(2)}, u32[]{:S(2)}) collective-permute-start(bf16[2,2,2,1,64,768]{5,4,2,1,0,3:T(8,128)(2,1)S(1)} %get-tuple-element.470), channel_id=1, source_target_pairs={{0,2},{1,3},{2,0},{3,1},{4,6},{5,7},{6,4},{7,5},{8,10},{9,11},{10,... | collective-permute-start | bytes 2359304 | tf_op jit(solution)/shard_map/ppermute | solution.py:88
  74.2 29.1 %collective-permute-start.9 = (bf16[256,768]{1,0:T(8,128)(2,1)S(1)}, bf16[256,768]{1,0:T(8,128)(2,1)S(1)}, u32[]{:S(2)}, u32[]{:S(2)}) collective-permute-start(bf16[256,768]{1,0:T(8,128)(2,1)S(1)} %collective-permute-done.4), channel_id=1, source_target_pairs={{0,8},{1,9},{2,10},{3,11},{4,12},{5,13},{6,14},{7,15},{8,0},{9,1},... | collective-permute-start | bytes 1179656 | tf_op jit(solution)/shard_map/ppermute | solution.py:88
  76.5 26.8 %collective-permute-start.10 = (bf16[2,2,1,64,768]{4,3,1,0,2:T(8,128)(2,1)S(1)}, bf16[2,2,1,64,768]{4,3,1,0,2:T(8,128)(2,1)S(1)}, u32[]{:S(2)}, u32[]{:S(2)}) collective-permute-start(bf16[2,2,1,64,768]{4,3,1,0,2:T(8,128)(2,1)S(1)} %get-tuple-element.491), channel_id=1, source_target_pairs={{0,4},{1,5},{2,6},{3,7},{4,0},{5,1},{6,2},{7,3},{8,12},{9,13},{10,... | collective-permute-start | bytes 1179656 | tf_op jit(solution)/shard_map/ppermute | solution.py:88
  103.5 32.1 %collective-permute-start.13 = (bf16[2,1,64,768]{3,2,0,1:T(8,128)(2,1)S(1)}, bf16[2,1,64,768]{3,2,0,1:T(8,128)(2,1)S(1)}, u32[]{:S(2)}, u32[]{:S(2)}) collective-permute-start(bf16[2,1,64,768]{3,2,0,1:T(8,128)(2,1)S(1)} %get-tuple-element.523), channel_id=1, source_target_pairs={{0,8},{1,9},{2,10},{3,11},{4,12},{5,13},{6,14},{7,15},{8,0},{9,1},... | collective-permute-start | bytes 589832 | tf_op jit(solution)/shard_map/ppermute | solution.py:88
  106.8 28.8 %collective-permute-start.12 = (bf16[1024,384]{1,0:T(8,128)(2,1)S(1)}, bf16[1024,384]{1,0:T(8,128)(2,1)S(1)}, u32[]{:S(2)}, u32[]{:S(2)}) collective-permute-start(bf16[1024,384]{1,0:T(8,128)(2,1)S(1)} %add_convert_fusion.14.refs_0_), channel_id=1, source_target_pairs={{0,2},{1,3},{2,0},{3,1},{4,6},{5,7},{6,4},{7,5},{8,10},{9,11},{10,... | collective-permute-start | bytes 2359304 | tf_op jit(solution)/shard_map/ppermute | solution.py:88
  119.2 37.2 %collective-permute-start.14 = (bf16[1024,384]{1,0:T(8,128)(2,1)S(1)}, bf16[1024,384]{1,0:T(8,128)(2,1)}, u32[]{:S(2)}, u32[]{:S(2)}) collective-permute-start(bf16[1024,384]{1,0:T(8,128)(2,1)S(1)} %add_convert_fusion.14.refs_0_), channel_id=1, source_target_pairs={{0,4},{1,5},{2,6},{3,7},{4,0},{5,1},{6,2},{7,3},{8,12},{9,13},{10,... | collective-permute-start | bytes 2359304 | tf_op jit(solution)/shard_map/ppermute | solution.py:88
  267.9 34.0 %collective-permute-start.24 = (bf16[4,2,2,2,2,24,768]{6,5,3,2,1,0,4:T(8,128)(2,1)}, bf16[4,2,2,2,2,24,768]{6,5,3,2,1,0,4:T(8,128)(2,1)}, u32[]{:S(2)}, u32[]{:S(2)}) collective-permute-start(bf16[4,2,2,2,2,24,768]{6,5,3,2,1,0,4:T(8,128)(2,1)} %bitcast.435), channel_id=1, source_target_pairs={{0,2},{1,3},{2,0},{3,1},{4,6},{5,7},{6,4},{7,5},{8,10},{9,11},{10,... | collective-permute-start | bytes 7077896 | tf_op jit(solution)/shard_map/ppermute | solution.py:88
  268.3 33.6 %collective-permute-start.25 = (bf16[2,2,2,2,2,24,1536]{6,5,4,2,1,0,3:T(8,128)(2,1)}, bf16[2,2,2,2,2,24,1536]{6,5,4,2,1,0,3:T(8,128)(2,1)}, u32[]{:S(2)}, u32[]{:S(2)}) collective-permute-start(bf16[2,2,2,2,2,24,1536]{6,5,4,2,1,0,3:T(8,128)(2,1)} %bitcast.433), channel_id=1, source_target_pairs={{0,2},{1,3},{2,0},{3,1},{4,6},{5,7},{6,4},{7,5},{8,10},{9,11},{10,... | collective-permute-start | bytes 7077896 | tf_op jit(solution)/shard_map/ppermute | solution.py:88
  331.0 28.3 %collective-permute-start.30 = (bf16[4,2,2,2,24,768]{5,4,3,2,1,0:T(8,128)(2,1)}, bf16[4,2,2,2,24,768]{5,4,3,2,1,0:T(8,128)(2,1)}, u32[]{:S(2)}, u32[]{:S(2)}) collective-permute-start(bf16[4,2,2,2,24,768]{5,4,3,2,1,0:T(8,128)(2,1)} %get-tuple-element.464), channel_id=1, source_target_pairs={{0,1},{1,0},{2,3},{3,2},{4,5},{5,4},{6,7},{7,6},{8,9},{9,8},{10,11... | collective-permute-start | bytes 3538952 | tf_op jit(solution)/shard_map/ppermute | solution.py:88
  338.1 22.3 %collective-permute-start.31 = (bf16[3,2,2,2,2,24,768]{6,5,3,2,1,0,4:T(8,128)(2,1)}, bf16[3,2,2,2,2,24,768]{6,5,3,2,1,0,4:T(8,128)(2,1)}, u32[]{:S(2)}, u32[]{:S(2)}) collective-permute-start(bf16[3,2,2,2,2,24,768]{6,5,3,2,1,0,4:T(8,128)(2,1)} %bitcast.437), channel_id=1, source_target_pairs={{0,2},{1,3},{2,0},{3,1},{4,6},{5,7},{6,4},{7,5},{8,10},{9,11},{10,... | collective-permute-start | bytes 5308424 | tf_op jit(solution)/shard_map/ppermute | solution.py:88
  341.3 44.3 %collective-permute-start.36 = (bf16[2,2,2,2,24,1536]{5,4,3,2,1,0:T(8,128)(2,1)}, bf16[2,2,2,2,24,1536]{5,4,3,2,1,0:T(8,128)(2,1)}, u32[]{:S(2)}, u32[]{:S(2)}) collective-permute-start(bf16[2,2,2,2,24,1536]{5,4,3,2,1,0:T(8,128)(2,1)} %get-tuple-element.462), channel_id=1, source_target_pairs={{0,4},{1,5},{2,6},{3,7},{4,0},{5,1},{6,2},{7,3},{8,12},{9,13},{10,... | collective-permute-start | bytes 3538952 | tf_op jit(solution)/shard_map/ppermute | solution.py:88
  362.7 23.0 %collective-permute-start.34 = (bf16[2,64,1536]{2,1,0:T(8,128)(2,1)}, bf16[2,64,1536]{2,1,0:T(8,128)(2,1)S(1)}, u32[]{:S(2)}, u32[]{:S(2)}) collective-permute-start(bf16[2,64,1536]{2,1,0:T(8,128)(2,1)} %get-tuple-element.487), channel_id=1, source_target_pairs={{0,8},{1,9},{2,10},{3,11},{4,12},{5,13},{6,14},{7,15},{8,0},{9,1},... | collective-permute-start | bytes 1179656 | tf_op jit(solution)/shard_map/ppermute | solution.py:88
  362.7 35.1 %collective-permute-start.33 = (bf16[1024,384]{1,0:T(8,128)(2,1)}, bf16[1024,384]{1,0:T(8,128)(2,1)}, u32[]{:S(2)}, u32[]{:S(2)}) collective-permute-start(bf16[1024,384]{1,0:T(8,128)(2,1)} %get-tuple-element.242), channel_id=1, source_target_pairs={{0,2},{1,3},{2,0},{3,1},{4,6},{5,7},{6,4},{7,5},{8,10},{9,11},{10,... | collective-permute-start | bytes 2359304 | tf_op jit(solution)/shard_map/ppermute | solution.py:88
  365.1 32.6 %collective-permute-start.35 = (bf16[4,2,2,24,768]{4,3,2,1,0:T(8,128)(2,1)}, bf16[4,2,2,24,768]{4,3,2,1,0:T(8,128)(2,1)}, u32[]{:S(2)}, u32[]{:S(2)}) collective-permute-start(bf16[4,2,2,24,768]{4,3,2,1,0:T(8,128)(2,1)} %get-tuple-element.478), channel_id=1, source_target_pairs={{0,4},{1,5},{2,6},{3,7},{4,0},{5,1},{6,2},{7,3},{8,12},{9,13},{10,... | collective-permute-start | bytes 1769480 | tf_op jit(solution)/shard_map/ppermute | solution.py:88
  368.6 52.4 %collective-permute-start.40 = (bf16[3,2,2,2,24,768]{5,4,3,2,1,0:T(8,128)(2,1)}, bf16[3,2,2,2,24,768]{5,4,3,2,1,0:T(8,128)(2,1)S(1)}, u32[]{:S(2)}, u32[]{:S(2)}) collective-permute-start(bf16[3,2,2,2,24,768]{5,4,3,2,1,0:T(8,128)(2,1)} %get-tuple-element.466), channel_id=1, source_target_pairs={{0,1},{1,0},{2,3},{3,2},{4,5},{5,4},{6,7},{7,6},{8,9},{9,8},{10,11... | collective-permute-start | bytes 2654216 | tf_op jit(solution)/shard_map/ppermute | solution.py:88
  397.9 23.1 %collective-permute-start.38 = (bf16[64,1536]{1,0:T(8,128)(2,1)S(1)}, bf16[64,1536]{1,0:T(8,128)(2,1)S(1)}, u32[]{:S(2)}, u32[]{:S(2)}) collective-permute-start(bf16[64,1536]{1,0:T(8,128)(2,1)S(1)} %get-tuple-element.517), channel_id=1, source_target_pairs={{0,16},{1,17},{2,18},{3,19},{4,20},{5,21},{6,22},{7,23},{8,24},{9,... | collective-permute-start | bytes 589832 | tf_op jit(solution)/shard_map/ppermute | solution.py:88
  425.4 25.0 %collective-permute-start.43 = (bf16[64,768]{1,0:T(8,128)(2,1)S(1)}, bf16[64,768]{1,0:T(8,128)(2,1)}, u32[]{:S(2)}, u32[]{:S(2)}) collective-permute-start(bf16[64,768]{1,0:T(8,128)(2,1)S(1)} %fusion.32), channel_id=1, source_target_pairs={{0,16},{1,17},{2,18},{3,19},{4,20},{5,21},{6,22},{7,23},{8,24},{9,... | collective-permute-start | bytes 294920 | tf_op jit(solution)/shard_map/ppermute | solution.py:88
  428.7 23.9 %collective-permute-start.41 = (bf16[1024,384]{1,0:T(8,128)(2,1)}, bf16[1024,384]{1,0:T(8,128)(2,1)}, u32[]{:S(2)}, u32[]{:S(2)}) collective-permute-start(bf16[1024,384]{1,0:T(8,128)(2,1)} %get-tuple-element.263), channel_id=1, source_target_pairs={{0,2},{1,3},{2,0},{3,1},{4,6},{5,7},{6,4},{7,5},{8,10},{9,11},{10,... | collective-permute-start | bytes 2359304 | tf_op jit(solution)/shard_map/ppermute | solution.py:88
  430.2 22.4 %collective-permute-start.42 = (bf16[2,2,2,2,24,1664]{5,4,3,2,1,0:T(8,128)(2,1)}, bf16[2,2,2,2,24,1664]{5,4,3,2,1,0:T(8,128)(2,1)}, u32[]{:S(2)}, u32[]{:S(2)}) collective-permute-start(bf16[2,2,2,2,24,1664]{5,4,3,2,1,0:T(8,128)(2,1)} %get-tuple-element.460), channel_id=1, source_target_pairs={{0,2},{1,3},{2,0},{3,1},{4,6},{5,7},{6,4},{7,5},{8,10},{9,11},{10,... | collective-permute-start | bytes 3833864 | tf_op jit(solution)/shard_map/ppermute | solution.py:88
  483.1 57.2 %collective-permute-start.58 = (bf16[2,24,1536]{2,1,0:T(8,128)(2,1)S(1)}, bf16[2,24,1536]{2,1,0:T(8,128)(2,1)S(1)}, u32[]{:S(2)}, u32[]{:S(2)}) collective-permute-start(bf16[2,24,1536]{2,1,0:T(8,128)(2,1)S(1)} %get-tuple-element.525), channel_id=1, source_target_pairs={{0,16},{1,17},{2,18},{3,19},{4,20},{5,21},{6,22},{7,23},{8,24},{9,... | collective-permute-start | bytes 442376 | tf_op jit(solution)/shard_map/ppermute | solution.py:88
  500.2 45.4 %collective-permute-start.59 = (bf16[256,768]{1,0:T(8,128)(2,1)}, bf16[256,768]{1,0:T(8,128)(2,1)}, u32[]{:S(2)}, u32[]{:S(2)}) collective-permute-start(bf16[256,768]{1,0:T(8,128)(2,1)} %get-tuple-element.474), channel_id=1, source_target_pairs={{0,8},{1,9},{2,10},{3,11},{4,12},{5,13},{6,14},{7,15},{8,0},{9,1},... | collective-permute-start | bytes 1179656 | tf_op jit(solution)/shard_map/ppermute | solution.py:88
  505.3 40.4 %collective-permute-start.60 = (bf16[256,768]{1,0:T(8,128)(2,1)}, bf16[256,768]{1,0:T(8,128)(2,1)}, u32[]{:S(2)}, u32[]{:S(2)}) collective-permute-start(bf16[256,768]{1,0:T(8,128)(2,1)} %fusion.46), channel_id=1, source_target_pairs={{0,16},{1,17},{2,18},{3,19},{4,20},{5,21},{6,22},{7,23},{8,24},{9,... | collective-permute-start | bytes 1179656 | tf_op jit(solution)/shard_map/ppermute | solution.py:88
  515.7 24.6 %collective-permute-start.56 = (bf16[2,2,24,640]{3,2,1,0:T(8,128)(2,1)S(1)}, bf16[2,2,24,640]{3,2,1,0:T(8,128)(2,1)S(1)}, u32[]{:S(2)}, u32[]{:S(2)}) collective-permute-start(bf16[2,2,24,640]{3,2,1,0:T(8,128)(2,1)S(1)} %get-tuple-element.535), channel_id=1, source_target_pairs={{0,4},{1,5},{2,6},{3,7},{4,0},{5,1},{6,2},{7,3},{8,12},{9,13},{10,... | collective-permute-start | bytes 368648 | tf_op jit(solution)/shard_map/ppermute | solution.py:88
  (146 other events, 1215.6 us)
Sparse Core Ops, SparseCore 0:
  13.1 168.7 all-gather.1

commit v2 on v0

--- a/solution.py
+++ b/solution.py
@@ -642,6 +642,10 @@
         ],
         axis=2,
     ).transpose(1, 0, 2)
+    packed, later = lax.optimization_barrier(
+        (packed, (self_out, cross_q, cross_out, cross_kv, ffn_in, ffn_out, gains, biases))
+    )
+    self_out, cross_q, cross_out, cross_kv, ffn_in, ffn_out, gains, biases = later
     pieces = parted(packed, "z", 0)
 
     small = jnp.concatenate([gains, biases], axis=0).T
@@ -655,15 +659,15 @@
     first_all = lax.all_gather(first_pack, ("seq", "batch"), axis=0, tiled=True)
     second_all = lax.all_gather(second_pack, ("seq", "batch"), axis=1, tiled=True)
 
-    pieces, inputs = lax.optimization_barrier((pieces, inputs))
+    pieces, inputs, bank_rows = lax.optimization_barrier((pieces, inputs, bank[0]))
     across = grid.send(inputs, "h", 1)
-    token_parts = [inputs, grid.send(inputs, "l", 1), across, grid.send(across, "l", 1)]
+    beside = grid.send(inputs, "l", 1)
 
     chunk = BANK_BLOCK * blocks.shape[1] // grid.seq
     per_block = BANK_BLOCK // chunk
     local_chunks = bank.shape[1] // chunk
     local_blocks = bank.shape[1] // BANK_BLOCK
-    bank_chunks = bank[0].reshape(local_chunks, chunk, width)
+    bank_chunks = bank_rows.reshape(local_chunks, chunk, width)
     home = seq_index * local_blocks
     every = jnp.arange(grid.seq, dtype=jnp.int32)
     wanted = jnp.take(blocks[0], every // per_block) - home
@@ -687,9 +691,10 @@
     gathered = in_order(pieces, my_z)
     for axis in "yxc":
         pieces = [gathered] + [grid.send(gathered, axis, m) for m in range(1, getattr(grid, axis))]
-        if axis == "y":
-            pieces = meet(pieces, retrieve)
+        if axis == "x":
+            pieces, across, beside = meet((pieces, across, beside), retrieve)
         gathered = in_order(pieces, me[axis])
+    token_parts = [inputs, beside, across, grid.send(across, "l", 1)]
     qkv_group = gathered.transpose(3, 1, 0, 2, 4, 5).reshape(width, PACK)
     column = jnp.arange(PACK, dtype=jnp.int32)
     real = (column < GROUP_WIDTH) | (column >= QUERY)
@@ -871,8 +876,8 @@
     near_other_grad, slopes = self_backward(
         tables["near other"], queries, dout, state, [near_other], slopes, False, False
     )
-    near_other_grad, slopes = meet(
-        (near_other_grad, slopes), unspread, reduce_ffnout, reduce_ffnin, reduce_mid
+    near_other_grad, far_moved, slopes = meet(
+        (near_other_grad, far_moved, slopes), unspread, reduce_ffnout, reduce_ffnin, reduce_mid
     )
     near_moved = grid.send(near_other_grad, "c", 1)
 
@@ -902,8 +907,8 @@
     near_own_grad, query_grad = self_backward(
         tables["near own"], queries, dout, state, [own_side], slopes, False, True
     )
-    near_own_grad, near_moved, far_moved, query_grad = meet(
-        (near_own_grad, near_moved, far_moved, query_grad)
+    near_own_grad, near_moved, query_grad = meet(
+        (near_own_grad, near_moved, query_grad), reduce_late, spread_back, reduce_ffnin, reduce_mid
     )
 
     far_query_grad = grid.send(query_grad[1::2], "z", 0, mirror=True)
@@ -914,7 +919,7 @@
     dqkv = jnp.concatenate([query_grad.reshape(GROUPS * rows, QUERY), side_grad], axis=1)
     far_tokens_grad = rounded(back_matmul(dqkv[rows:], qkv_weight)).reshape(Z - 1, rows, width)
     dqkv, far_tokens_grad = meet(
-        (dqkv, far_tokens_grad), reduce_ffnout, reduce_ffnin, reduce_mid, reduce_late, spread_back
+        (dqkv, far_tokens_grad), reduce_ffnin, reduce_late, spread_back
     )
     third = grid.send(far_tokens_grad[2], "l", 1)
     first = grid.send(far_tokens_grad[0], "l", 1)
@@ -927,14 +932,14 @@
     )
     reduce_group = Chain(reduction(sharded(rounded(grad_group)), "cyx", final=False))
     tokens_base = dresid_one + back_matmul(dqkv[:rows], qkv_weight)
+    tokens_base, first, third = meet(
+        (tokens_base, first, third), reduce_group, reduce_late, spread_back, reduce_mid
+    )
     second = grid.send(rounded(total_of([far_tokens_grad[1], third])), "h", 1)
-    tokens_base = meet(tokens_base, reduce_group, spread_back, reduce_late)
-    tokens_base = meet(tokens_base, reduce_group, spread_back, reduce_mid)
-    tokens_base = meet(tokens_base, reduce_group, spread_back, reduce_late)
+    tokens_base, second = meet((tokens_base, second), reduce_group, reduce_late, spread_back, reduce_mid)
+    tokens_grad = total_of([tokens_base, first, second])
+    meet((), reduce_group, reduce_late, reduce_ffnout)
     pieces = parted(reduce_group.result.reshape(Z, part, PACK), "z", 0)
-    tokens_grad = total_of([tokens_base, first, second])
-    for chain in (reduce_ffnin, reduce_mid, reduce_late, reduce_late):
-        chain.step(chain.pending)
 
     spot = jnp.arange(grid.seq, dtype=jnp.int32)
     spot_z = my_z ^ (spot % 2 * 2 + spot // 2 % 2)

time: 537 us -> 546 us (1.017)
  starting transfers between devices: 68.2 us -> 80.1 us
  waiting for transfers between devices: 115 us -> 107 us
  other arithmetic: 57.3 us -> 64.5 us
  Pallas kernels: 150 us -> 144 us
    ppermute x68, starting transfers between devices: 68.2 us -> 80 us  [send(): return lax.ppermute(array, ('seq', 'batch'), pairs)]
    ppermute x68, waiting for transfers between devices: 115 us -> 107 us  [send(): return lax.ppermute(array, ('seq', 'batch'), pairs)]
    dynamic_slice x17 -> x18, local copies, waits for them, and re-layouts: 13.5 us -> 12.9 us  [take(): return lax.dynamic_index_in_dim(array, index, axis, keepdims=False)]
    unnamed x190 -> x206, local copies, waits for them, and re-layouts: 12.4 us -> 12.2 us
  transfers between devices with their start and end apart: 70 -> 70, of which waited for: 22 -> 19; matrix products, arithmetic and copies ran while one was open for 25% -> 27% of each run, Pallas kernels for 28% -> 27%
where the time goes in v2:
time: 546 us; the launch traced here: 539 us
  Pallas kernels  144 us (26%)
  waiting for transfers between devices  107 us (20%)
  starting transfers between devices  80.1 us (15%)
  local copies, waits for them, and re-layouts  76.7 us (14%)
  other arithmetic  64.5 us (12%)
  matrix products  48.8 us (9%)
  between operations  17.3 us (3%)
    ppermute x68, waiting for transfers between devices, send(): return lax.ppermute(array, ('seq', 'batch'), pairs)  107 us
    ppermute x68, starting transfers between devices, send(): return lax.ppermute(array, ('seq', 'batch'), pairs)  80 us
    pallas_call x4, Pallas kernels, self_backward(): pl.pallas_call(functools.partial(backward_kernel, rows, parts, first, las...  55 us
    pallas_call x4, Pallas kernels, self_forward(): pl.pallas_call(functools.partial(forward_kernel, rows, parts, first, last...  51.5 us
    convert_element_type x30, other arithmetic, rounded(): return values.astype(jnp.bfloat16)  32.1 us
    dot_general x11, matrix products, matmul(): return jnp.dot(left, right, preferred_element_type=jnp.float32)  22.9 us
    squeeze x24, local copies, waits for them, and re-layouts, take(): return lax.dynamic_index_in_dim(array, index, axis, keepdims=False)  17.9 us
    dot_general x12, matrix products, back_matmul(): lax.dot_general(left, right, LANES_IN, preferred_element_type=jnp.float32)  17.3 us
  transfers between devices with their start and end apart: 70, of which 19 were waited for; matrix products, arithmetic and copies ran while one was open for 27% of the time, Pallas kernels for 27%

profile of v2, /device:TPU:0, one launch (start us, length us, event | category | flops | bytes accessed | tf_op | source)
XLA Modules:
  0.0 539.0 jit_solution(9673859045944131858)
XLA Ops:
  34.0 7.2 %pick_rows.1 = bf16[16,64,768]{2,1,0:T(8,128)(2,1)} custom-call(s32[32]{0:T(128)} %pad_add_fusion.table, bf16[8,64,768]{2,1,0:T(8,128)(2,1)} %bitcast.429), custom_call_target="tpu_custom_call" | custom-call | tf_op jit(solution)/shard_map/pick_rows/pallas_call | solution.py:507
  48.3 7.6 %collective-permute-done.4 = bf16[2,4,24,640]{3,2,1,0:T(8,128)(2,1)} collective-permute-done((bf16[2,4,24,640]{3,2,1,0:T(8,128)(2,1)S(1)}, bf16[2,4,24,640]{3,2,1,0:T(8,128)(2,1)}, u32[]{:S(2)}, u32[]{:S(2)}) %collective-permute-start.4) | collective-permute-done | bytes 245792 | tf_op jit(solution)/shard_map/ppermute | solution.py:88
  55.9 15.0 %collective-permute-done.5 = bf16[256,768]{1,0:T(8,128)(2,1)S(1)} collective-permute-done((bf16[256,768]{1,0:T(8,128)(2,1)S(1)}, bf16[256,768]{1,0:T(8,128)(2,1)S(1)}, u32[]{:S(2)}, u32[]{:S(2)}) %collective-permute-start.5) | collective-permute-done | bytes 393248 | tf_op jit(solution)/shard_map/ppermute | solution.py:88
  75.2 16.6 %collective-permute-done.9 = bf16[256,768]{1,0:T(8,128)(2,1)S(1)} collective-permute-done((bf16[256,768]{1,0:T(8,128)(2,1)S(1)}, bf16[256,768]{1,0:T(8,128)(2,1)S(1)}, u32[]{:S(2)}, u32[]{:S(2)}) %collective-permute-start.9) | collective-permute-done | bytes 393248 | tf_op jit(solution)/shard_map/ppermute | solution.py:88
  104.8 13.2 %self_forward.4 = (f32[4,3,128,256]{3,2,1,0:T(8,128)}, f32[4,16,256]{2,1,0:T(8,128)}) custom-call(s32[9]{0:T(128)} %get-tuple-element.573.table, bf16[4,256,256]{2,1,0:T(8,128)(2,1)} %pad_maximum_fusion.11.query_in, bf16[1024,384]{1,0:T(8,128)(2,1)} %copy-done.91), custom_call_target="tpu_custom_call" | custom-call | flops 3221225472 | bytes 1572864 | tf_op jit(solution)/shard_map/self_forward/pallas_call | solution.py:317
  118.9 12.5 %self_forward.5 = (f32[4,3,128,256]{3,2,1,0:T(8,128)}, f32[4,16,256]{2,1,0:T(8,128)}) custom-call(s32[9]{0:T(128)} %get-tuple-element.575.table, bf16[4,256,256]{2,1,0:T(8,128)(2,1)} %pad_maximum_fusion.11.query_in, bf16[1024,384]{1,0:T(8,128)(2,1)} %copy-done.92, f32[4,3,128,256]{3,2,1,0:T(8,128)} %get-tuple-element.204.refs_1_, ...), custom_call_target="tpu_custom_call" | custom-call | flops 3221225472 | bytes 1572864 | tf_op jit(solution)/shard_map/self_forward/pallas_call | solution.py:317
  134.5 12.5 %self_forward.6 = (f32[4,3,128,256]{3,2,1,0:T(8,128)}, f32[4,16,256]{2,1,0:T(8,128)}) custom-call(s32[9]{0:T(128)} %get-tuple-element.574.table, bf16[4,256,256]{2,1,0:T(8,128)(2,1)} %pad_maximum_fusion.11.query_in, bf16[1024,384]{1,0:T(8,128)(2,1)} %copy-done.93, f32[4,3,128,256]{3,2,1,0:T(8,128)} %get-tuple-element.212.refs_1_, ...), custom_call_target="tpu_custom_call" | custom-call | flops 3221225472 | bytes 1572864 | tf_op jit(solution)/shard_map/self_forward/pallas_call | solution.py:317
  147.9 13.3 %self_forward.7 = (f32[4,256,256]{2,1,0:T(8,128)}, f32[4,8,256]{2,1,0:T(8,128)}) custom-call(s32[9]{0:T(128)} %add_add_fusion.4.table, bf16[4,256,256]{2,1,0:T(8,128)(2,1)} %pad_maximum_fusion.11.query_in, bf16[1024,384]{1,0:T(8,128)(2,1)} %copy-done.94, f32[4,3,128,256]{3,2,1,0:T(8,128)} %get-tuple-element.219.refs_1_, f32[4,16,256]{2,1,0:T(8,128)} %get-tuple-element.220.refs_2_), custom_call_target="tpu_custom_call" | custom-call | flops 3221225472 | bytes 1572864 | tf_op jit(solution)/shard_map/self_forward/pallas_call | solution.py:317
  168.6 5.9 %collective-permute-done.19 = bf16[256,256]{1,0:T(8,128)(2,1)S(1)} collective-permute-done((bf16[256,256]{1,0:T(8,128)(2,1)S(1)}, bf16[256,256]{1,0:T(8,128)(2,1)S(1)}, u32[]{:S(2)}, u32[]{:S(2)}) %collective-permute-start.19) | collective-permute-done | bytes 131104 | tf_op jit(solution)/shard_map/ppermute | solution.py:88
  174.5 9.1 %collective-permute-done.20 = bf16[256,256]{1,0:T(8,128)(2,1)S(1)} collective-permute-done((bf16[256,256]{1,0:T(8,128)(2,1)S(1)}, bf16[256,256]{1,0:T(8,128)(2,1)S(1)}, u32[]{:S(2)}, u32[]{:S(2)}) %collective-permute-start.20) | collective-permute-done | bytes 131104 | tf_op jit(solution)/shard_map/ppermute | solution.py:88
  199.0 11.2 %cross_forward.1 = (bf16[256,768]{1,0:T(8,128)(2,1)}, f32[6,8,256]{2,1,0:T(8,128)}) custom-call(bf16[256,768]{1,0:T(8,128)(2,1)} %fusion.22.query, bf16[1024,1536]{1,0:T(8,128)(2,1)} %add_convert_fusion.keys.values, bf16[1024,1536]{1,0:T(8,128)(2,1)} %add_convert_fusion.keys.values), custom_call_target="tpu_custom_call" | custom-call | flops 1610612736 | bytes 3145728 | tf_op jit(solution)/shard_map/cross_forward/pallas_call | solution.py:441
  212.6 10.1 %multiply_convert_fusion = (bf16[256,3072]{1,0:T(8,128)(2,1)S(1)}, f32[256,3072]{1,0:T(8,128)S(1)}, f32[256,3072]{1,0:T(8,128)S(1)}) fusion(f32[3072]{0:T(1024)S(1)} %add.598, bf16[2,768,3072]{2,1,0:T(8,128)(2,1)} %all-gather.5.cloned.1.call-done, f32[256,768]{1,0:T(8,128)S(1)} %get-tuple-element.577, f32[768]{0:T(1024)S(1)} %get-tuple-element.416, ...), kind=kOutput, calls=%fused_computation.21 | convolution fusion | flops 1260847104 | bytes 13389824 | tf_op jit(solution)/shard_map/dot_general | solution.py:45
  252.8 13.6 %cross_backward.1 = (bf16[256,768]{1,0:T(8,128)(2,1)}, bf16[1024,768]{1,0:T(8,128)(2,1)}, bf16[1024,768]{1,0:T(8,128)(2,1)}) custom-call(bf16[256,768]{1,0:T(8,128)(2,1)} %fusion.22.query, bf16[1024,1536]{1,0:T(8,128)(2,1)} %add_convert_fusion.keys.values, bf16[1024,1536]{1,0:T(8,128)(2,1)} %add_convert_fusion.keys.values, ...), custom_call_target="tpu_custom_call" | custom-call | flops 4026531840 | bytes 6291456 | tf_op jit(solution)/shard_map/cross_backward/pallas_call | solution.py:469
  279.5 11.6 %collective-permute-start.26 = (bf16[256,256]{1,0:T(8,128)(2,1)S(1)}, bf16[256,256]{1,0:T(8,128)(2,1)}, u32[]{:S(2)}, u32[]{:S(2)}) collective-permute-start(bf16[256,256]{1,0:T(8,128)(2,1)S(1)} %bitcast.449), channel_id=1, source_target_pairs={{0,14},{1,15},{2,12},{3,13},{4,10},{5,11},{6,8},{7,9},{8,6},{9,7},... | collective-permute-start | bytes 393224 | tf_op jit(solution)/shard_map/ppermute | solution.py:88
  317.3 13.6 %self_backward.4 = (bf16[1024,384]{1,0:T(8,128)(2,1)}, f32[4,3,128,256]{3,2,1,0:T(8,128)}, f32[4,8,256]{2,1,0:T(8,128)}) custom-call(s32[9]{0:T(128)} %add_add_fusion.4.table, bf16[4,256,256]{2,1,0:T(8,128)(2,1)} %pad_maximum_fusion.11.query_in, bf16[4,256,256]{2,1,0:T(8,128)(2,1)} %pad_maximum_fusion.12.dout, f32[4,8,256]{2,1,0:T(8,128)} %get-tuple-element.254.state, ...), custom_call_target="tpu_custom_call" | custom-call | flops 4026531840 | bytes 3145728 | tf_op jit(solution)/shard_map/self_backward/pallas_call | solution.py:359
  345.5 13.6 %self_backward.5 = (bf16[1024,384]{1,0:T(8,128)(2,1)}, f32[4,3,128,256]{3,2,1,0:T(8,128)}) custom-call(s32[9]{0:T(128)} %get-tuple-element.574.table, bf16[4,256,256]{2,1,0:T(8,128)(2,1)} %pad_maximum_fusion.11.query_in, bf16[4,256,256]{2,1,0:T(8,128)(2,1)} %pad_maximum_fusion.12.dout, f32[4,8,256]{2,1,0:T(8,128)} %get-tuple-element.255.state, ...), custom_call_target="tpu_custom_call" | custom-call | flops 4026531840 | bytes 3145728 | tf_op jit(solution)/shard_map/self_backward/pallas_call | solution.py:359
  371.6 13.2 %self_backward.6 = (bf16[1024,384]{1,0:T(8,128)(2,1)}, f32[4,3,128,256]{3,2,1,0:T(8,128)}) custom-call(s32[9]{0:T(128)} %get-tuple-element.575.table, bf16[4,256,256]{2,1,0:T(8,128)(2,1)} %pad_maximum_fusion.11.query_in, bf16[4,256,256]{2,1,0:T(8,128)(2,1)} %pad_maximum_fusion.12.dout, f32[4,8,256]{2,1,0:T(8,128)} %get-tuple-element.255.state, ...), custom_call_target="tpu_custom_call" | custom-call | flops 4026531840 | bytes 3145728 | tf_op jit(solution)/shard_map/self_backward/pallas_call | solution.py:359
  384.9 6.5 %collective-permute-done.40 = bf16[2,2,24,3072]{3,2,1,0:T(8,128)(2,1)} collective-permute-done((bf16[2,2,24,3072]{3,2,1,0:T(8,128)(2,1)}, bf16[2,2,24,3072]{3,2,1,0:T(8,128)(2,1)}, u32[]{:S(2)}, u32[]{:S(2)}) %collective-permute-start.40) | collective-permute-done | bytes 589856 | tf_op jit(solution)/shard_map/ppermute | solution.py:88
  403.4 14.7 %self_backward.7 = (bf16[1024,384]{1,0:T(8,128)(2,1)}, bf16[4,256,256]{2,1,0:T(8,128)(2,1)}) custom-call(s32[9]{0:T(128)} %get-tuple-element.573.table, bf16[4,256,256]{2,1,0:T(8,128)(2,1)} %pad_maximum_fusion.11.query_in, bf16[4,256,256]{2,1,0:T(8,128)(2,1)} %pad_maximum_fusion.12.dout, f32[4,8,256]{2,1,0:T(8,128)} %get-tuple-element.255.state, ...), custom_call_target="tpu_custom_call" | custom-call | flops 4026531840 | bytes 3145728 | tf_op jit(solution)/shard_map/self_backward/pallas_call | solution.py:359
  442.2 6.9 %collective-permute-done.49 = bf16[2,2,2,24,1664]{4,3,2,1,0:T(8,128)(2,1)S(1)} collective-permute-done((bf16[2,2,2,24,1664]{4,3,2,1,0:T(8,128)(2,1)S(1)}, bf16[2,2,2,24,1664]{4,3,2,1,0:T(8,128)(2,1)S(1)}, u32[]{:S(2)}, u32[]{:S(2)}) %collective-permute-start.49) | collective-permute-done | bytes 639008 | tf_op jit(solution)/shard_map/ppermute | solution.py:88
  463.2 5.5 %collective-permute-done.54 = bf16[2,2,24,1664]{3,2,1,0:T(8,128)(2,1)S(1)} collective-permute-done((bf16[2,2,24,1664]{3,2,1,0:T(8,128)(2,1)S(1)}, bf16[2,2,24,1664]{3,2,1,0:T(8,128)(2,1)S(1)}, u32[]{:S(2)}, u32[]{:S(2)}) %collective-permute-start.54) | collective-permute-done | bytes 319520 | tf_op jit(solution)/shard_map/ppermute | solution.py:88
  471.6 5.3 collective-permute-done.55
  492.3 11.5 %collective-permute-done.61 = bf16[3,24,768]{2,1,0:T(8,128)(2,1)} collective-permute-done((bf16[3,24,768]{2,1,0:T(8,128)(2,1)}, bf16[3,24,768]{2,1,0:T(8,128)(2,1)}, u32[]{:S(2)}, u32[]{:S(2)}) %collective-permute-start.61) | collective-permute-done | bytes 110624 | tf_op jit(solution)/shard_map/ppermute | solution.py:88
  516.7 5.6 %place_rows.1 = f32[8,64,768]{2,1,0:T(8,128)} custom-call(s32[16]{0:T(128)} %and_select_fusion.3.table, bf16[16,64,768]{2,1,0:T(8,128)(2,1)} %bitcast.406), custom_call_target="tpu_custom_call" | custom-call | tf_op jit(solution)/shard_map/place_rows/pallas_call | solution.py:533
  (600 shorter events, 265.9 us)
Async XLA Ops:
  7.2 180.5 %all-gather.3.cloned.1.call-start = ((), (), s32[]{:S(2)}) async-start(), calls=%async_computation | async-start | bytes 6285312 | tf_op jit(solution)/shard_map/all_gather | solution.py:659
  14.2 198.3 %all-gather.5.cloned.1.call-start = ((), (), s32[]{:S(2)}) async-start(), calls=%async_computation.1 | async-start | bytes 9732096 | tf_op jit(solution)/shard_map/all_gather | solution.py:660
  42.7 28.2 %collective-permute-start.7 = (bf16[2,2,2,1,64,768]{5,4,2,1,0,3:T(8,128)(2,1)S(1)}, bf16[2,2,2,1,64,768]{5,4,2,1,0,3:T(8,128)(2,1)S(1)}, u32[]{:S(2)}, u32[]{:S(2)}) collective-permute-start(bf16[2,2,2,1,64,768]{5,4,2,1,0,3:T(8,128)(2,1)S(1)} %get-tuple-element.466), channel_id=1, source_target_pairs={{0,2},{1,3},{2,0},{3,1},{4,6},{5,7},{6,4},{7,5},{8,10},{9,11},{10,... | collective-permute-start | bytes 2359304 | tf_op jit(solution)/shard_map/ppermute | solution.py:88
  42.8 28.1 %collective-permute-start.5 = (bf16[256,768]{1,0:T(8,128)(2,1)S(1)}, bf16[256,768]{1,0:T(8,128)(2,1)S(1)}, u32[]{:S(2)}, u32[]{:S(2)}) collective-permute-start(bf16[256,768]{1,0:T(8,128)(2,1)S(1)} %bitcast.439), channel_id=1, source_target_pairs={{0,16},{1,17},{2,18},{3,19},{4,20},{5,21},{6,22},{7,23},{8,24},{9,... | collective-permute-start | bytes 1179656 | tf_op jit(solution)/shard_map/ppermute | solution.py:88
  42.9 28.0 %collective-permute-start.6 = (bf16[256,768]{1,0:T(8,128)(2,1)S(1)}, bf16[256,768]{1,0:T(8,128)(2,1)}, u32[]{:S(2)}, u32[]{:S(2)}) collective-permute-start(bf16[256,768]{1,0:T(8,128)(2,1)S(1)} %bitcast.440), channel_id=1, source_target_pairs={{0,8},{1,9},{2,10},{3,11},{4,12},{5,13},{6,14},{7,15},{8,0},{9,1},... | collective-permute-start | bytes 1179656 | tf_op jit(solution)/shard_map/ppermute | solution.py:88
  95.7 22.3 %collective-permute-start.12 = (bf16[1024,384]{1,0:T(8,128)(2,1)S(1)}, bf16[1024,384]{1,0:T(8,128)(2,1)S(1)}, u32[]{:S(2)}, u32[]{:S(2)}) collective-permute-start(bf16[1024,384]{1,0:T(8,128)(2,1)S(1)} %add_convert_fusion.13.refs_0_), channel_id=1, source_target_pairs={{0,2},{1,3},{2,0},{3,1},{4,6},{5,7},{6,4},{7,5},{8,10},{9,11},{10,... | collective-permute-start | bytes 2359304 | tf_op jit(solution)/shard_map/ppermute | solution.py:88
  100.7 30.7 %collective-permute-start.14 = (bf16[1024,384]{1,0:T(8,128)(2,1)S(1)}, bf16[1024,384]{1,0:T(8,128)(2,1)S(1)}, u32[]{:S(2)}, u32[]{:S(2)}) collective-permute-start(bf16[1024,384]{1,0:T(8,128)(2,1)S(1)} %add_convert_fusion.13.refs_0_), channel_id=1, source_target_pairs={{0,4},{1,5},{2,6},{3,7},{4,0},{5,1},{6,2},{7,3},{8,12},{9,13},{10,... | collective-permute-start | bytes 2359304 | tf_op jit(solution)/shard_map/ppermute | solution.py:88
  161.3 22.4 %collective-permute-start.22 = (bf16[2,2,64,768]{3,2,1,0:T(8,128)(2,1)S(1)}, bf16[2,2,64,768]{3,2,1,0:T(8,128)(2,1)S(1)}, u32[]{:S(2)}, u32[]{:S(2)}) collective-permute-start(bf16[2,2,64,768]{3,2,1,0:T(8,128)(2,1)S(1)} %pad_maximum_fusion.15), channel_id=1, source_target_pairs={{0,4},{1,5},{2,6},{3,7},{4,0},{5,1},{6,2},{7,3},{8,12},{9,13},{10,... | collective-permute-start | bytes 1179656 | tf_op jit(solution)/shard_map/ppermute | solution.py:88
  229.9 36.5 %collective-permute-start.24 = (bf16[4,2,2,2,2,24,768]{6,5,4,3,2,1,0:T(8,128)(2,1)}, bf16[4,2,2,2,2,24,768]{6,5,4,3,2,1,0:T(8,128)(2,1)}, u32[]{:S(2)}, u32[]{:S(2)}) collective-permute-start(bf16[4,2,2,2,2,24,768]{6,5,4,3,2,1,0:T(8,128)(2,1)} %get-tuple-element.450), channel_id=1, source_target_pairs={{0,2},{1,3},{2,0},{3,1},{4,6},{5,7},{6,4},{7,5},{8,10},{9,11},{10,... | collective-permute-start | bytes 7077896 | tf_op jit(solution)/shard_map/ppermute | solution.py:88
  239.6 26.9 %collective-permute-start.25 = (bf16[2,2,2,2,24,3072]{5,4,2,1,0,3:T(8,128)(2,1)}, bf16[2,2,2,2,24,3072]{5,4,2,1,0,3:T(8,128)(2,1)}, u32[]{:S(2)}, u32[]{:S(2)}) collective-permute-start(bf16[2,2,2,2,24,3072]{5,4,2,1,0,3:T(8,128)(2,1)} %bitcast.383), channel_id=1, source_target_pairs={{0,2},{1,3},{2,0},{3,1},{4,6},{5,7},{6,4},{7,5},{8,10},{9,11},{10,... | collective-permute-start | bytes 7077896 | tf_op jit(solution)/shard_map/ppermute | solution.py:88
  279.5 28.1 %collective-permute-start.26 = (bf16[256,256]{1,0:T(8,128)(2,1)S(1)}, bf16[256,256]{1,0:T(8,128)(2,1)}, u32[]{:S(2)}, u32[]{:S(2)}) collective-permute-start(bf16[256,256]{1,0:T(8,128)(2,1)S(1)} %bitcast.449), channel_id=1, source_target_pairs={{0,14},{1,15},{2,12},{3,13},{4,10},{5,11},{6,8},{7,9},{8,6},{9,7},... | collective-permute-start | bytes 393224 | tf_op jit(solution)/shard_map/ppermute | solution.py:88
  302.4 29.2 %collective-permute-start.30 = (bf16[4,2,2,2,24,768]{5,4,3,2,1,0:T(8,128)(2,1)}, bf16[4,2,2,2,24,768]{5,4,3,2,1,0:T(8,128)(2,1)}, u32[]{:S(2)}, u32[]{:S(2)}) collective-permute-start(bf16[4,2,2,2,24,768]{5,4,3,2,1,0:T(8,128)(2,1)} %get-tuple-element.460), channel_id=1, source_target_pairs={{0,1},{1,0},{2,3},{3,2},{4,5},{5,4},{6,7},{7,6},{8,9},{9,8},{10,11... | collective-permute-start | bytes 3538952 | tf_op jit(solution)/shard_map/ppermute | solution.py:88
  313.5 45.7 %collective-permute-start.36 = (bf16[2,2,2,24,3072]{4,3,2,1,0:T(8,128)(2,1)}, bf16[2,2,2,24,3072]{4,3,2,1,0:T(8,128)(2,1)}, u32[]{:S(2)}, u32[]{:S(2)}) collective-permute-start(bf16[2,2,2,24,3072]{4,3,2,1,0:T(8,128)(2,1)} %get-tuple-element.458), channel_id=1, source_target_pairs={{0,1},{1,0},{2,3},{3,2},{4,5},{5,4},{6,7},{7,6},{8,9},{9,8},{10,11... | collective-permute-start | bytes 3538952 | tf_op jit(solution)/shard_map/ppermute | solution.py:88
  332.4 26.8 %collective-permute-start.33 = (bf16[1024,384]{1,0:T(8,128)(2,1)}, bf16[1024,384]{1,0:T(8,128)(2,1)}, u32[]{:S(2)}, u32[]{:S(2)}) collective-permute-start(bf16[1024,384]{1,0:T(8,128)(2,1)} %get-tuple-element.265), channel_id=1, source_target_pairs={{0,2},{1,3},{2,0},{3,1},{4,6},{5,7},{6,4},{7,5},{8,10},{9,11},{10,... | collective-permute-start | bytes 2359304 | tf_op jit(solution)/shard_map/ppermute | solution.py:88
  334.8 24.4 %collective-permute-start.34 = (bf16[2,64,1536]{2,1,0:T(8,128)(2,1)}, bf16[2,64,1536]{2,1,0:T(8,128)(2,1)S(1)}, u32[]{:S(2)}, u32[]{:S(2)}) collective-permute-start(bf16[2,64,1536]{2,1,0:T(8,128)(2,1)} %get-tuple-element.483), channel_id=1, source_target_pairs={{0,8},{1,9},{2,10},{3,11},{4,12},{5,13},{6,14},{7,15},{8,0},{9,1},... | collective-permute-start | bytes 1179656 | tf_op jit(solution)/shard_map/ppermute | solution.py:88
  343.5 41.4 %collective-permute-start.41 = (bf16[3,2,2,2,24,768]{5,4,3,2,1,0:T(8,128)(2,1)S(1)}, bf16[3,2,2,2,24,768]{5,4,3,2,1,0:T(8,128)(2,1)S(1)}, u32[]{:S(2)}, u32[]{:S(2)}) collective-permute-start(bf16[3,2,2,2,24,768]{5,4,3,2,1,0:T(8,128)(2,1)S(1)} %get-tuple-element.462), channel_id=1, source_target_pairs={{0,1},{1,0},{2,3},{3,2},{4,5},{5,4},{6,7},{7,6},{8,9},{9,8},{10,11... | collective-permute-start | bytes 2654216 | tf_op jit(solution)/shard_map/ppermute | solution.py:88
  361.8 29.6 %collective-permute-start.37 = (bf16[1024,384]{1,0:T(8,128)(2,1)}, bf16[1024,384]{1,0:T(8,128)(2,1)}, u32[]{:S(2)}, u32[]{:S(2)}) collective-permute-start(bf16[1024,384]{1,0:T(8,128)(2,1)} %add_convert_fusion.11), channel_id=1, source_target_pairs={{0,4},{1,5},{2,6},{3,7},{4,0},{5,1},{6,2},{7,3},{8,12},{9,13},{10,... | collective-permute-start | bytes 2359304 | tf_op jit(solution)/shard_map/ppermute | solution.py:88
  368.3 23.1 %collective-permute-start.40 = (bf16[2,2,24,3072]{3,2,1,0:T(8,128)(2,1)}, bf16[2,2,24,3072]{3,2,1,0:T(8,128)(2,1)}, u32[]{:S(2)}, u32[]{:S(2)}) collective-permute-start(bf16[2,2,24,3072]{3,2,1,0:T(8,128)(2,1)} %get-tuple-element.472), channel_id=1, source_target_pairs={{0,4},{1,5},{2,6},{3,7},{4,0},{5,1},{6,2},{7,3},{8,12},{9,13},{10,... | collective-permute-start | bytes 1769480 | tf_op jit(solution)/shard_map/ppermute | solution.py:88
  392.4 35.3 %collective-permute-start.42 = (bf16[1024,384]{1,0:T(8,128)(2,1)}, bf16[1024,384]{1,0:T(8,128)(2,1)}, u32[]{:S(2)}, u32[]{:S(2)}) collective-permute-start(bf16[1024,384]{1,0:T(8,128)(2,1)} %get-tuple-element.288), channel_id=1, source_target_pairs={{0,2},{1,3},{2,0},{3,1},{4,6},{5,7},{6,4},{7,5},{8,10},{9,11},{10,... | collective-permute-start | bytes 2359304 | tf_op jit(solution)/shard_map/ppermute | solution.py:88
  396.3 31.4 %collective-permute-start.43 = (bf16[2,2,2,2,24,1664]{5,4,2,1,0,3:T(8,128)(2,1)}, bf16[2,2,2,2,24,1664]{5,4,2,1,0,3:T(8,128)(2,1)}, u32[]{:S(2)}, u32[]{:S(2)}) collective-permute-start(bf16[2,2,2,2,24,1664]{5,4,2,1,0,3:T(8,128)(2,1)} %bitcast.387), channel_id=1, source_target_pairs={{0,2},{1,3},{2,0},{3,1},{4,6},{5,7},{6,4},{7,5},{8,10},{9,11},{10,... | collective-permute-start | bytes 3833864 | tf_op jit(solution)/shard_map/ppermute | solution.py:88
  398.9 28.8 %collective-permute-start.45 = (bf16[2,24,3072]{2,1,0:T(8,128)(2,1)}, bf16[2,24,3072]{2,1,0:T(8,128)(2,1)S(1)}, u32[]{:S(2)}, u32[]{:S(2)}) collective-permute-start(bf16[2,24,3072]{2,1,0:T(8,128)(2,1)} %get-tuple-element.491), channel_id=1, source_target_pairs={{0,8},{1,9},{2,10},{3,11},{4,12},{5,13},{6,14},{7,15},{8,0},{9,1},... | collective-permute-start | bytes 884744 | tf_op jit(solution)/shard_map/ppermute | solution.py:88
  401.7 26.0 %collective-permute-start.46 = (bf16[3,2,2,24,768]{4,3,2,1,0:T(8,128)(2,1)}, bf16[3,2,2,24,768]{4,3,2,1,0:T(8,128)(2,1)}, u32[]{:S(2)}, u32[]{:S(2)}) collective-permute-start(bf16[3,2,2,24,768]{4,3,2,1,0:T(8,128)(2,1)} %get-tuple-element.480), channel_id=1, source_target_pairs={{0,4},{1,5},{2,6},{3,7},{4,0},{5,1},{6,2},{7,3},{8,12},{9,13},{10,... | collective-permute-start | bytes 1327112 | tf_op jit(solution)/shard_map/ppermute | solution.py:88
  436.5 23.9 %collective-permute-start.56 = (bf16[3,2,24,768]{3,2,1,0:T(8,128)(2,1)}, bf16[3,2,24,768]{3,2,1,0:T(8,128)(2,1)}, u32[]{:S(2)}, u32[]{:S(2)}) collective-permute-start(bf16[3,2,24,768]{3,2,1,0:T(8,128)(2,1)} %get-tuple-element.511), channel_id=1, source_target_pairs={{0,8},{1,9},{2,10},{3,11},{4,12},{5,13},{6,14},{7,15},{8,0},{9,1},... | collective-permute-start | bytes 663560 | tf_op jit(solution)/shard_map/ppermute | solution.py:88
  478.9 24.9 %collective-permute-start.57 = (bf16[256,768]{1,0:T(8,128)(2,1)}, bf16[256,768]{1,0:T(8,128)(2,1)}, u32[]{:S(2)}, u32[]{:S(2)}) collective-permute-start(bf16[256,768]{1,0:T(8,128)(2,1)} %fusion.46), channel_id=1, source_target_pairs={{0,16},{1,17},{2,18},{3,19},{4,20},{5,21},{6,22},{7,23},{8,24},{9,... | collective-permute-start | bytes 1179656 | tf_op jit(solution)/shard_map/ppermute | solution.py:88
  (141 other events, 1342.1 us)
Sparse Core Ops, SparseCore 0:
  14.4 92.2 all-gather.2
  110.2 95.9 all-gather.4

commit v3 on v2

--- a/solution.py
+++ b/solution.py
@@ -563,6 +563,13 @@
     return values
 
 
+def settle(values, *chains):
+    values, kept = lax.optimization_barrier((values, [chain.pending[0] for chain in chains]))
+    for chain, array in zip(chains, kept):
+        chain.pending = [array] + list(chain.pending[1:])
+    return values
+
+
 def total_of(arrays):
     total = wide(arrays[0])
     for array in arrays[1:]:
@@ -904,11 +911,12 @@
     reduce_late = Chain(reduction(sharded(grad_late), "cyxlh"))
     spread_back = Chain(spreading(rounded(back_matmul(dcross_pair, crosskv_full))))
 
+    slopes = settle(slopes, reduce_late, spread_back, reduce_ffnin, reduce_mid)
     near_own_grad, query_grad = self_backward(
         tables["near own"], queries, dout, state, [own_side], slopes, False, True
     )
     near_own_grad, near_moved, query_grad = meet(
-        (near_own_grad, near_moved, query_grad), reduce_late, spread_back, reduce_ffnin, reduce_mid
+        (near_own_grad, near_moved, query_grad), reduce_late, spread_back, reduce_mid
     )
 
     far_query_grad = grid.send(query_grad[1::2], "z", 0, mirror=True)
@@ -919,10 +927,9 @@
     dqkv = jnp.concatenate([query_grad.reshape(GROUPS * rows, QUERY), side_grad], axis=1)
     far_tokens_grad = rounded(back_matmul(dqkv[rows:], qkv_weight)).reshape(Z - 1, rows, width)
     dqkv, far_tokens_grad = meet(
-        (dqkv, far_tokens_grad), reduce_ffnin, reduce_late, spread_back
+        (dqkv, far_tokens_grad), reduce_ffnin, reduce_late, spread_back, reduce_mid
     )
     third = grid.send(far_tokens_grad[2], "l", 1)
-    first = grid.send(far_tokens_grad[0], "l", 1)
     grad_group = weight_grad(token_column, dqkv)
     sums = jnp.sum(wide(dqkv), axis=0)
     sums = jnp.stack([jnp.where(is_query, sums, 0.0), jnp.where(is_value, sums, 0.0)])
@@ -932,14 +939,21 @@
     )
     reduce_group = Chain(reduction(sharded(rounded(grad_group)), "cyx", final=False))
     tokens_base = dresid_one + back_matmul(dqkv[:rows], qkv_weight)
-    tokens_base, first, third = meet(
-        (tokens_base, first, third), reduce_group, reduce_late, spread_back, reduce_mid
-    )
-    second = grid.send(rounded(total_of([far_tokens_grad[1], third])), "h", 1)
-    tokens_base, second = meet((tokens_base, second), reduce_group, reduce_late, spread_back, reduce_mid)
+    tokens_base, third, near_tokens_grad = meet(
+        (tokens_base, third, far_tokens_grad[:2]),
+        reduce_group,
+        reduce_late,
+        spread_back,
+        reduce_mid,
+    )
+    second = grid.send(rounded(total_of([near_tokens_grad[1], third])), "h", 1)
+    first = grid.send(near_tokens_grad[0], "l", 1)
+    tokens_base, second = meet((tokens_base, second), reduce_group, reduce_late, spread_back)
+    drows = spread_back.result
+    meet((), reduce_group, reduce_late, reduce_ffnout, reduce_ffnin)
+    pieces = parted(reduce_group.result.reshape(Z, part, PACK), "z", 0)
+    drows, pieces[0] = lax.optimization_barrier((drows, pieces[0]))
     tokens_grad = total_of([tokens_base, first, second])
-    meet((), reduce_group, reduce_late, reduce_ffnout)
-    pieces = parted(reduce_group.result.reshape(Z, part, PACK), "z", 0)
 
     spot = jnp.arange(grid.seq, dtype=jnp.int32)
     spot_z = my_z ^ (spot % 2 * 2 + spot // 2 % 2)
@@ -947,7 +961,7 @@
     target = jnp.take(blocks[0], source // per_block) - home
     inside = (target >= 0) & (target < local_blocks)
     places = jnp.where(inside, target * per_block + source % per_block, -1)
-    drows = spread_back.result.reshape(grid.seq, chunk, width)
+    drows = drows.reshape(grid.seq, chunk, width)
     bank_grad = place_rows(drows, places, local_chunks).reshape(bank.shape[1], width)
 
     grad_groups = wide(in_order(pieces, my_z))

time: 546 us -> 540 us (0.989)
  other arithmetic: 64.5 us -> 55.6 us
  Pallas kernels: 144 us -> 150 us
  waiting for transfers between devices: 107 us -> 113 us
    ppermute x68, waiting for transfers between devices: 107 us -> 113 us  [send(): return lax.ppermute(array, ('seq', 'batch'), pairs)]
    unnamed x206 -> x204, local copies, waits for them, and re-layouts: 12.2 us -> 11.6 us
  transfers between devices with their start and end apart: 70 -> 70, of which waited for: 19 -> 20; matrix products, arithmetic and copies ran while one was open for 27% -> 24% of each run, Pallas kernels for 27% -> 28%
where the time goes in v3:
time: 540 us; the launch traced here: 533 us
  Pallas kernels  150 us (28%)
  waiting for transfers between devices  113 us (21%)
  starting transfers between devices  75.5 us (14%)
  local copies, waits for them, and re-layouts  73 us (14%)
  other arithmetic  55.6 us (10%)
  matrix products  47.9 us (9%)
  between operations  17.4 us (3%)
    ppermute x68, waiting for transfers between devices, send(): return lax.ppermute(array, ('seq', 'batch'), pairs)  113 us
    ppermute x68, starting transfers between devices, send(): return lax.ppermute(array, ('seq', 'batch'), pairs)  75.4 us
    pallas_call x4, Pallas kernels, self_backward(): pl.pallas_call(functools.partial(backward_kernel, rows, parts, first, las...  58 us
    pallas_call x4, Pallas kernels, self_forward(): pl.pallas_call(functools.partial(forward_kernel, rows, parts, first, last...  54.5 us
    convert_element_type x30, other arithmetic, rounded(): return values.astype(jnp.bfloat16)  26.7 us
    dot_general x11, matrix products, matmul(): return jnp.dot(left, right, preferred_element_type=jnp.float32)  23.1 us
    dot_general x12, matrix products, back_matmul(): lax.dot_general(left, right, LANES_IN, preferred_element_type=jnp.float32)  16.4 us
    squeeze x24, local copies, waits for them, and re-layouts, take(): return lax.dynamic_index_in_dim(array, index, axis, keepdims=False)  15 us
  transfers between devices with their start and end apart: 70, of which 20 were waited for; matrix products, arithmetic and copies ran while one was open for 24% of the time, Pallas kernels for 28%

profile of v3, /device:TPU:0, one launch (start us, length us, event | category | flops | bytes accessed | tf_op | source)
XLA Modules:
  0.0 532.9 jit_solution(4417321565005634814)
XLA Ops:
  34.0 7.5 %pick_rows.1 = bf16[16,64,768]{2,1,0:T(8,128)(2,1)} custom-call(s32[32]{0:T(128)} %pad_add_fusion.table, bf16[8,64,768]{2,1,0:T(8,128)(2,1)} %bitcast.422), custom_call_target="tpu_custom_call" | custom-call | tf_op jit(solution)/shard_map/pick_rows/pallas_call | solution.py:507
  48.4 7.5 %collective-permute-done.4 = bf16[2,4,24,640]{3,2,1,0:T(8,128)(2,1)} collective-permute-done((bf16[2,4,24,640]{3,2,1,0:T(8,128)(2,1)S(1)}, bf16[2,4,24,640]{3,2,1,0:T(8,128)(2,1)}, u32[]{:S(2)}, u32[]{:S(2)}) %collective-permute-start.4) | collective-permute-done | bytes 245792 | tf_op jit(solution)/shard_map/ppermute | solution.py:88
  55.9 14.4 %collective-permute-done.5 = bf16[256,768]{1,0:T(8,128)(2,1)S(1)} collective-permute-done((bf16[256,768]{1,0:T(8,128)(2,1)S(1)}, bf16[256,768]{1,0:T(8,128)(2,1)S(1)}, u32[]{:S(2)}, u32[]{:S(2)}) %collective-permute-start.5) | collective-permute-done | bytes 393248 | tf_op jit(solution)/shard_map/ppermute | solution.py:88
  75.2 16.0 %collective-permute-done.9 = bf16[256,768]{1,0:T(8,128)(2,1)S(1)} collective-permute-done((bf16[256,768]{1,0:T(8,128)(2,1)S(1)}, bf16[256,768]{1,0:T(8,128)(2,1)S(1)}, u32[]{:S(2)}, u32[]{:S(2)}) %collective-permute-start.9) | collective-permute-done | bytes 393248 | tf_op jit(solution)/shard_map/ppermute | solution.py:88
  104.8 14.2 %self_forward.4 = (f32[4,3,128,256]{3,2,1,0:T(8,128)}, f32[4,16,256]{2,1,0:T(8,128)}) custom-call(s32[9]{0:T(128)} %get-tuple-element.586.table, bf16[4,256,256]{2,1,0:T(8,128)(2,1)} %pad_maximum_fusion.11.query_in, bf16[1024,384]{1,0:T(8,128)(2,1)} %copy-done.90), custom_call_target="tpu_custom_call" | custom-call | flops 3221225472 | bytes 1572864 | tf_op jit(solution)/shard_map/self_forward/pallas_call | solution.py:317
  119.9 13.4 %self_forward.5 = (f32[4,3,128,256]{3,2,1,0:T(8,128)}, f32[4,16,256]{2,1,0:T(8,128)}) custom-call(s32[9]{0:T(128)} %get-tuple-element.588.table, bf16[4,256,256]{2,1,0:T(8,128)(2,1)} %pad_maximum_fusion.11.query_in, bf16[1024,384]{1,0:T(8,128)(2,1)} %copy-done.91, f32[4,3,128,256]{3,2,1,0:T(8,128)} %get-tuple-element.211.refs_1_, ...), custom_call_target="tpu_custom_call" | custom-call | flops 3221225472 | bytes 1572864 | tf_op jit(solution)/shard_map/self_forward/pallas_call | solution.py:317
  136.4 13.6 %self_forward.6 = (f32[4,3,128,256]{3,2,1,0:T(8,128)}, f32[4,16,256]{2,1,0:T(8,128)}) custom-call(s32[9]{0:T(128)} %get-tuple-element.587.table, bf16[4,256,256]{2,1,0:T(8,128)(2,1)} %pad_maximum_fusion.11.query_in, bf16[1024,384]{1,0:T(8,128)(2,1)} %copy-done.92, f32[4,3,128,256]{3,2,1,0:T(8,128)} %get-tuple-element.219.refs_1_, ...), custom_call_target="tpu_custom_call" | custom-call | flops 3221225472 | bytes 1572864 | tf_op jit(solution)/shard_map/self_forward/pallas_call | solution.py:317
  150.9 13.3 %self_forward.7 = (f32[4,256,256]{2,1,0:T(8,128)}, f32[4,8,256]{2,1,0:T(8,128)}) custom-call(s32[9]{0:T(128)} %add_add_fusion.4.table, bf16[4,256,256]{2,1,0:T(8,128)(2,1)} %pad_maximum_fusion.11.query_in, bf16[1024,384]{1,0:T(8,128)(2,1)} %copy-done.93, f32[4,3,128,256]{3,2,1,0:T(8,128)} %get-tuple-element.226.refs_1_, f32[4,16,256]{2,1,0:T(8,128)} %get-tuple-element.227.refs_2_), custom_call_target="tpu_custom_call" | custom-call | flops 3221225472 | bytes 1572864 | tf_op jit(solution)/shard_map/self_forward/pallas_call | solution.py:317
  171.5 10.5 %collective-permute-done.19 = bf16[256,256]{1,0:T(8,128)(2,1)S(1)} collective-permute-done((bf16[256,256]{1,0:T(8,128)(2,1)S(1)}, bf16[256,256]{1,0:T(8,128)(2,1)S(1)}, u32[]{:S(2)}, u32[]{:S(2)}) %collective-permute-start.19) | collective-permute-done | bytes 131104 | tf_op jit(solution)/shard_map/ppermute | solution.py:88
  204.8 11.1 %cross_forward.1 = (bf16[256,768]{1,0:T(8,128)(2,1)}, f32[6,8,256]{2,1,0:T(8,128)}) custom-call(bf16[256,768]{1,0:T(8,128)(2,1)} %fusion.22.query, bf16[1024,1536]{1,0:T(8,128)(2,1)} %add_convert_fusion.keys.values, bf16[1024,1536]{1,0:T(8,128)(2,1)} %add_convert_fusion.keys.values), custom_call_target="tpu_custom_call" | custom-call | flops 1610612736 | bytes 3145728 | tf_op jit(solution)/shard_map/cross_forward/pallas_call | solution.py:441
  218.2 10.1 %multiply_convert_fusion = (bf16[256,3072]{1,0:T(8,128)(2,1)S(1)}, f32[256,3072]{1,0:T(8,128)S(1)}, f32[256,3072]{1,0:T(8,128)S(1)}) fusion(f32[3072]{0:T(1024)S(1)} %add.598, bf16[2,768,3072]{2,1,0:T(8,128)(2,1)} %all-gather.5.cloned.1.call-done, f32[256,768]{1,0:T(8,128)S(1)} %get-tuple-element.590, f32[768]{0:T(1024)S(1)} %get-tuple-element.430, ...), kind=kOutput, calls=%fused_computation.21 | convolution fusion | flops 1260847104 | bytes 13389824 | tf_op jit(solution)/shard_map/dot_general | solution.py:45
  258.4 13.6 %cross_backward.1 = (bf16[256,768]{1,0:T(8,128)(2,1)}, bf16[1024,768]{1,0:T(8,128)(2,1)}, bf16[1024,768]{1,0:T(8,128)(2,1)}) custom-call(bf16[256,768]{1,0:T(8,128)(2,1)} %fusion.22.query, bf16[1024,1536]{1,0:T(8,128)(2,1)} %add_convert_fusion.keys.values, bf16[1024,1536]{1,0:T(8,128)(2,1)} %add_convert_fusion.keys.values, ...), custom_call_target="tpu_custom_call" | custom-call | flops 4026531840 | bytes 6291456 | tf_op jit(solution)/shard_map/cross_backward/pallas_call | solution.py:469
  285.0 4.2 collective-permute-start.26
  316.9 13.6 %self_backward.4 = (bf16[1024,384]{1,0:T(8,128)(2,1)}, f32[4,3,128,256]{3,2,1,0:T(8,128)}, f32[4,8,256]{2,1,0:T(8,128)}) custom-call(s32[9]{0:T(128)} %add_add_fusion.4.table, bf16[4,256,256]{2,1,0:T(8,128)(2,1)} %pad_maximum_fusion.11.query_in, bf16[4,256,256]{2,1,0:T(8,128)(2,1)} %pad_maximum_fusion.12.dout, f32[4,8,256]{2,1,0:T(8,128)} %get-tuple-element.261.state, ...), custom_call_target="tpu_custom_call" | custom-call | flops 4026531840 | bytes 3145728 | tf_op jit(solution)/shard_map/self_backward/pallas_call | solution.py:359
  345.2 14.6 %self_backward.5 = (bf16[1024,384]{1,0:T(8,128)(2,1)}, f32[4,3,128,256]{3,2,1,0:T(8,128)}) custom-call(s32[9]{0:T(128)} %get-tuple-element.587.table, bf16[4,256,256]{2,1,0:T(8,128)(2,1)} %pad_maximum_fusion.11.query_in, bf16[4,256,256]{2,1,0:T(8,128)(2,1)} %pad_maximum_fusion.12.dout, f32[4,8,256]{2,1,0:T(8,128)} %get-tuple-element.262.state, ...), custom_call_target="tpu_custom_call" | custom-call | flops 4026531840 | bytes 3145728 | tf_op jit(solution)/shard_map/self_backward/pallas_call | solution.py:359
  373.4 14.2 %self_backward.6 = (bf16[1024,384]{1,0:T(8,128)(2,1)}, f32[4,3,128,256]{3,2,1,0:T(8,128)}) custom-call(s32[9]{0:T(128)} %get-tuple-element.588.table, bf16[4,256,256]{2,1,0:T(8,128)(2,1)} %pad_maximum_fusion.11.query_in, bf16[4,256,256]{2,1,0:T(8,128)(2,1)} %pad_maximum_fusion.12.dout, f32[4,8,256]{2,1,0:T(8,128)} %get-tuple-element.262.state, ...), custom_call_target="tpu_custom_call" | custom-call | flops 4026531840 | bytes 3145728 | tf_op jit(solution)/shard_map/self_backward/pallas_call | solution.py:359
  387.7 5.3 collective-permute-done.40
  407.8 15.6 %self_backward.7 = (bf16[1024,384]{1,0:T(8,128)(2,1)}, bf16[4,256,256]{2,1,0:T(8,128)(2,1)}) custom-call(s32[9]{0:T(128)} %get-tuple-element.586.table, bf16[4,256,256]{2,1,0:T(8,128)(2,1)} %pad_maximum_fusion.11.query_in, bf16[4,256,256]{2,1,0:T(8,128)(2,1)} %pad_maximum_fusion.12.dout, f32[4,8,256]{2,1,0:T(8,128)} %get-tuple-element.262.state, ...), custom_call_target="tpu_custom_call" | custom-call | flops 4026531840 | bytes 3145728 | tf_op jit(solution)/shard_map/self_backward/pallas_call | solution.py:359
  456.3 5.4 %collective-permute-done.55 = bf16[3,24,768]{2,1,0:T(8,128)(2,1)S(1)} collective-permute-done((bf16[3,24,768]{2,1,0:T(8,128)(2,1)S(1)}, bf16[3,24,768]{2,1,0:T(8,128)(2,1)S(1)}, u32[]{:S(2)}, u32[]{:S(2)}) %collective-permute-start.55) | collective-permute-done | bytes 110624 | tf_op jit(solution)/shard_map/ppermute | solution.py:88
  461.7 7.8 %collective-permute-done.54 = bf16[2,2,64,768]{3,2,1,0:T(8,128)(2,1)S(1)} collective-permute-done((bf16[2,2,64,768]{3,2,1,0:T(8,128)(2,1)S(1)}, bf16[2,2,64,768]{3,2,1,0:T(8,128)(2,1)S(1)}, u32[]{:S(2)}, u32[]{:S(2)}) %collective-permute-start.54) | collective-permute-done | bytes 393248 | tf_op jit(solution)/shard_map/ppermute | solution.py:88
  474.7 9.7 %collective-permute-done.58 = bf16[2,24,1664]{2,1,0:T(8,128)(2,1)S(1)} collective-permute-done((bf16[2,24,1664]{2,1,0:T(8,128)(2,1)S(1)}, bf16[2,24,1664]{2,1,0:T(8,128)(2,1)S(1)}, u32[]{:S(2)}, u32[]{:S(2)}) %collective-permute-start.58) | collective-permute-done | bytes 159776 | tf_op jit(solution)/shard_map/ppermute | solution.py:88
  487.2 7.6 %collective-permute-done.56 = bf16[256,768]{1,0:T(8,128)(2,1)S(1)} collective-permute-done((bf16[256,768]{1,0:T(8,128)(2,1)S(1)}, bf16[256,768]{1,0:T(8,128)(2,1)S(1)}, u32[]{:S(2)}, u32[]{:S(2)}) %collective-permute-start.56) | collective-permute-done | bytes 393248 | tf_op jit(solution)/shard_map/ppermute | solution.py:88
  496.3 7.7 %collective-permute-done.60 = bf16[256,768]{1,0:T(8,128)(2,1)S(1)} collective-permute-done((bf16[256,768]{1,0:T(8,128)(2,1)S(1)}, bf16[256,768]{1,0:T(8,128)(2,1)S(1)}, u32[]{:S(2)}, u32[]{:S(2)}) %collective-permute-start.60) | collective-permute-done | bytes 393248 | tf_op jit(solution)/shard_map/ppermute | solution.py:88
  518.1 5.6 %place_rows.1 = f32[8,64,768]{2,1,0:T(8,128)} custom-call(s32[16]{0:T(128)} %and_select_fusion.3.table, bf16[16,64,768]{2,1,0:T(8,128)(2,1)} %bitcast.397), custom_call_target="tpu_custom_call" | custom-call | tf_op jit(solution)/shard_map/place_rows/pallas_call | solution.py:533
  (600 shorter events, 258.9 us)
Async XLA Ops:
  7.2 186.1 %all-gather.3.cloned.1.call-start = ((), (), s32[]{:S(2)}) async-start(), calls=%async_computation | async-start | bytes 6285312 | tf_op jit(solution)/shard_map/all_gather | solution.py:666
  14.2 204.0 %all-gather.5.cloned.1.call-start = ((), (), s32[]{:S(2)}) async-start(), calls=%async_computation.1 | async-start | bytes 9732096 | tf_op jit(solution)/shard_map/all_gather | solution.py:667
  43.0 27.2 %collective-permute-start.7 = (bf16[2,2,2,1,64,768]{5,4,2,1,0,3:T(8,128)(2,1)S(1)}, bf16[2,2,2,1,64,768]{5,4,2,1,0,3:T(8,128)(2,1)S(1)}, u32[]{:S(2)}, u32[]{:S(2)}) collective-permute-start(bf16[2,2,2,1,64,768]{5,4,2,1,0,3:T(8,128)(2,1)S(1)} %get-tuple-element.480), channel_id=1, source_target_pairs={{0,2},{1,3},{2,0},{3,1},{4,6},{5,7},{6,4},{7,5},{8,10},{9,11},{10,... | collective-permute-start | bytes 2359304 | tf_op jit(solution)/shard_map/ppermute | solution.py:88
  43.1 27.1 %collective-permute-start.5 = (bf16[256,768]{1,0:T(8,128)(2,1)S(1)}, bf16[256,768]{1,0:T(8,128)(2,1)S(1)}, u32[]{:S(2)}, u32[]{:S(2)}) collective-permute-start(bf16[256,768]{1,0:T(8,128)(2,1)S(1)} %bitcast.432), channel_id=1, source_target_pairs={{0,16},{1,17},{2,18},{3,19},{4,20},{5,21},{6,22},{7,23},{8,24},{9,... | collective-permute-start | bytes 1179656 | tf_op jit(solution)/shard_map/ppermute | solution.py:88
  43.2 27.1 %collective-permute-start.6 = (bf16[256,768]{1,0:T(8,128)(2,1)S(1)}, bf16[256,768]{1,0:T(8,128)(2,1)}, u32[]{:S(2)}, u32[]{:S(2)}) collective-permute-start(bf16[256,768]{1,0:T(8,128)(2,1)S(1)} %bitcast.433), channel_id=1, source_target_pairs={{0,8},{1,9},{2,10},{3,11},{4,12},{5,13},{6,14},{7,15},{8,0},{9,1},... | collective-permute-start | bytes 1179656 | tf_op jit(solution)/shard_map/ppermute | solution.py:88
  95.7 23.2 %collective-permute-start.12 = (bf16[1024,384]{1,0:T(8,128)(2,1)S(1)}, bf16[1024,384]{1,0:T(8,128)(2,1)S(1)}, u32[]{:S(2)}, u32[]{:S(2)}) collective-permute-start(bf16[1024,384]{1,0:T(8,128)(2,1)S(1)} %add_convert_fusion.13.refs_0_), channel_id=1, source_target_pairs={{0,2},{1,3},{2,0},{3,1},{4,6},{5,7},{6,4},{7,5},{8,10},{9,11},{10,... | collective-permute-start | bytes 2359304 | tf_op jit(solution)/shard_map/ppermute | solution.py:88
  100.1 33.2 %collective-permute-start.14 = (bf16[1024,384]{1,0:T(8,128)(2,1)S(1)}, bf16[1024,384]{1,0:T(8,128)(2,1)S(1)}, u32[]{:S(2)}, u32[]{:S(2)}) collective-permute-start(bf16[1024,384]{1,0:T(8,128)(2,1)S(1)} %add_convert_fusion.13.refs_0_), channel_id=1, source_target_pairs={{0,4},{1,5},{2,6},{3,7},{4,0},{5,1},{6,2},{7,3},{8,12},{9,13},{10,... | collective-permute-start | bytes 2359304 | tf_op jit(solution)/shard_map/ppermute | solution.py:88
  164.3 25.0 %collective-permute-start.22 = (bf16[2,2,64,768]{3,2,1,0:T(8,128)(2,1)S(1)}, bf16[2,2,64,768]{3,2,1,0:T(8,128)(2,1)S(1)}, u32[]{:S(2)}, u32[]{:S(2)}) collective-permute-start(bf16[2,2,64,768]{3,2,1,0:T(8,128)(2,1)S(1)} %pad_maximum_fusion.15), channel_id=1, source_target_pairs={{0,4},{1,5},{2,6},{3,7},{4,0},{5,1},{6,2},{7,3},{8,12},{9,13},{10,... | collective-permute-start | bytes 1179656 | tf_op jit(solution)/shard_map/ppermute | solution.py:88
  235.6 36.5 %collective-permute-start.24 = (bf16[4,2,2,2,2,24,768]{6,5,4,3,2,1,0:T(8,128)(2,1)}, bf16[4,2,2,2,2,24,768]{6,5,4,3,2,1,0:T(8,128)(2,1)}, u32[]{:S(2)}, u32[]{:S(2)}) collective-permute-start(bf16[4,2,2,2,2,24,768]{6,5,4,3,2,1,0:T(8,128)(2,1)} %get-tuple-element.464), channel_id=1, source_target_pairs={{0,2},{1,3},{2,0},{3,1},{4,6},{5,7},{6,4},{7,5},{8,10},{9,11},{10,... | collective-permute-start | bytes 7077896 | tf_op jit(solution)/shard_map/ppermute | solution.py:88
  245.3 26.7 %collective-permute-start.25 = (bf16[2,2,2,2,24,3072]{5,4,2,1,0,3:T(8,128)(2,1)}, bf16[2,2,2,2,24,3072]{5,4,2,1,0,3:T(8,128)(2,1)}, u32[]{:S(2)}, u32[]{:S(2)}) collective-permute-start(bf16[2,2,2,2,24,3072]{5,4,2,1,0,3:T(8,128)(2,1)} %bitcast.374), channel_id=1, source_target_pairs={{0,2},{1,3},{2,0},{3,1},{4,6},{5,7},{6,4},{7,5},{8,10},{9,11},{10,... | collective-permute-start | bytes 7077896 | tf_op jit(solution)/shard_map/ppermute | solution.py:88
  300.5 30.0 %collective-permute-start.30 = (bf16[4,2,2,2,24,768]{5,4,3,2,1,0:T(8,128)(2,1)}, bf16[4,2,2,2,24,768]{5,4,3,2,1,0:T(8,128)(2,1)}, u32[]{:S(2)}, u32[]{:S(2)}) collective-permute-start(bf16[4,2,2,2,24,768]{5,4,3,2,1,0:T(8,128)(2,1)} %get-tuple-element.474), channel_id=1, source_target_pairs={{0,1},{1,0},{2,3},{3,2},{4,5},{5,4},{6,7},{7,6},{8,9},{9,8},{10,11... | collective-permute-start | bytes 3538952 | tf_op jit(solution)/shard_map/ppermute | solution.py:88
  308.3 22.2 %collective-permute-start.31 = (bf16[3,2,2,2,2,24,768]{6,5,3,2,1,0,4:T(8,128)(2,1)}, bf16[3,2,2,2,2,24,768]{6,5,3,2,1,0,4:T(8,128)(2,1)}, u32[]{:S(2)}, u32[]{:S(2)}) collective-permute-start(bf16[3,2,2,2,2,24,768]{6,5,3,2,1,0,4:T(8,128)(2,1)} %bitcast.376), channel_id=1, source_target_pairs={{0,2},{1,3},{2,0},{3,1},{4,6},{5,7},{6,4},{7,5},{8,10},{9,11},{10,... | collective-permute-start | bytes 5308424 | tf_op jit(solution)/shard_map/ppermute | solution.py:88
  313.1 46.7 %collective-permute-start.36 = (bf16[2,2,2,24,3072]{4,3,2,1,0:T(8,128)(2,1)}, bf16[2,2,2,24,3072]{4,3,2,1,0:T(8,128)(2,1)}, u32[]{:S(2)}, u32[]{:S(2)}) collective-permute-start(bf16[2,2,2,24,3072]{4,3,2,1,0:T(8,128)(2,1)} %get-tuple-element.472), channel_id=1, source_target_pairs={{0,1},{1,0},{2,3},{3,2},{4,5},{5,4},{6,7},{7,6},{8,9},{9,8},{10,11... | collective-permute-start | bytes 3538952 | tf_op jit(solution)/shard_map/ppermute | solution.py:88
  331.3 28.5 %collective-permute-start.33 = (bf16[1024,384]{1,0:T(8,128)(2,1)}, bf16[1024,384]{1,0:T(8,128)(2,1)}, u32[]{:S(2)}, u32[]{:S(2)}) collective-permute-start(bf16[1024,384]{1,0:T(8,128)(2,1)} %get-tuple-element.272), channel_id=1, source_target_pairs={{0,2},{1,3},{2,0},{3,1},{4,6},{5,7},{6,4},{7,5},{8,10},{9,11},{10,... | collective-permute-start | bytes 2359304 | tf_op jit(solution)/shard_map/ppermute | solution.py:88
  334.6 25.1 %collective-permute-start.34 = (bf16[2,64,1536]{2,1,0:T(8,128)(2,1)}, bf16[2,64,1536]{2,1,0:T(8,128)(2,1)S(1)}, u32[]{:S(2)}, u32[]{:S(2)}) collective-permute-start(bf16[2,64,1536]{2,1,0:T(8,128)(2,1)} %get-tuple-element.495), channel_id=1, source_target_pairs={{0,8},{1,9},{2,10},{3,11},{4,12},{5,13},{6,14},{7,15},{8,0},{9,1},... | collective-permute-start | bytes 1179656 | tf_op jit(solution)/shard_map/ppermute | solution.py:88
  343.7 44.0 %collective-permute-start.41 = (bf16[3,2,2,2,24,768]{5,4,3,2,1,0:T(8,128)(2,1)S(1)}, bf16[3,2,2,2,24,768]{5,4,3,2,1,0:T(8,128)(2,1)S(1)}, u32[]{:S(2)}, u32[]{:S(2)}) collective-permute-start(bf16[3,2,2,2,24,768]{5,4,3,2,1,0:T(8,128)(2,1)S(1)} %get-tuple-element.476), channel_id=1, source_target_pairs={{0,1},{1,0},{2,3},{3,2},{4,5},{5,4},{6,7},{7,6},{8,9},{9,8},{10,11... | collective-permute-start | bytes 2654216 | tf_op jit(solution)/shard_map/ppermute | solution.py:88
  362.5 30.6 %collective-permute-start.37 = (bf16[1024,384]{1,0:T(8,128)(2,1)}, bf16[1024,384]{1,0:T(8,128)(2,1)}, u32[]{:S(2)}, u32[]{:S(2)}) collective-permute-start(bf16[1024,384]{1,0:T(8,128)(2,1)} %add_convert_fusion.11), channel_id=1, source_target_pairs={{0,4},{1,5},{2,6},{3,7},{4,0},{5,1},{6,2},{7,3},{8,12},{9,13},{10,... | collective-permute-start | bytes 2359304 | tf_op jit(solution)/shard_map/ppermute | solution.py:88
  365.2 22.5 %collective-permute-start.38 = (bf16[64,1536]{1,0:T(8,128)(2,1)S(1)}, bf16[64,1536]{1,0:T(8,128)(2,1)S(1)}, u32[]{:S(2)}, u32[]{:S(2)}) collective-permute-start(bf16[64,1536]{1,0:T(8,128)(2,1)S(1)} %get-tuple-element.525), channel_id=1, source_target_pairs={{0,16},{1,17},{2,18},{3,19},{4,20},{5,21},{6,22},{7,23},{8,24},{9,... | collective-permute-start | bytes 589832 | tf_op jit(solution)/shard_map/ppermute | solution.py:88
  368.9 24.1 %collective-permute-start.40 = (bf16[2,2,24,3072]{3,2,1,0:T(8,128)(2,1)}, bf16[2,2,24,3072]{3,2,1,0:T(8,128)(2,1)}, u32[]{:S(2)}, u32[]{:S(2)}) collective-permute-start(bf16[2,2,24,3072]{3,2,1,0:T(8,128)(2,1)} %get-tuple-element.484), channel_id=1, source_target_pairs={{0,4},{1,5},{2,6},{3,7},{4,0},{5,1},{6,2},{7,3},{8,12},{9,13},{10,... | collective-permute-start | bytes 1769480 | tf_op jit(solution)/shard_map/ppermute | solution.py:88
  396.7 27.5 %collective-permute-start.42 = (bf16[1024,384]{1,0:T(8,128)(2,1)}, bf16[1024,384]{1,0:T(8,128)(2,1)}, u32[]{:S(2)}, u32[]{:S(2)}) collective-permute-start(bf16[1024,384]{1,0:T(8,128)(2,1)} %get-tuple-element.302), channel_id=1, source_target_pairs={{0,2},{1,3},{2,0},{3,1},{4,6},{5,7},{6,4},{7,5},{8,10},{9,11},{10,... | collective-permute-start | bytes 2359304 | tf_op jit(solution)/shard_map/ppermute | solution.py:88
  396.9 27.3 %collective-permute-start.43 = (bf16[2,2,2,2,24,1664]{5,4,2,1,0,3:T(8,128)(2,1)S(1)}, bf16[2,2,2,2,24,1664]{5,4,2,1,0,3:T(8,128)(2,1)}, u32[]{:S(2)}, u32[]{:S(2)}) collective-permute-start(bf16[2,2,2,2,24,1664]{5,4,2,1,0,3:T(8,128)(2,1)S(1)} %bitcast.416), channel_id=1, source_target_pairs={{0,2},{1,3},{2,0},{3,1},{4,6},{5,7},{6,4},{7,5},{8,10},{9,11},{10,... | collective-permute-start | bytes 3833864 | tf_op jit(solution)/shard_map/ppermute | solution.py:88
  406.4 30.1 %collective-permute-start.47 = (bf16[2,24,3072]{2,1,0:T(8,128)(2,1)}, bf16[2,24,3072]{2,1,0:T(8,128)(2,1)S(1)}, u32[]{:S(2)}, u32[]{:S(2)}) collective-permute-start(bf16[2,24,3072]{2,1,0:T(8,128)(2,1)} %get-tuple-element.503), channel_id=1, source_target_pairs={{0,8},{1,9},{2,10},{3,11},{4,12},{5,13},{6,14},{7,15},{8,0},{9,1},... | collective-permute-start | bytes 884744 | tf_op jit(solution)/shard_map/ppermute | solution.py:88
  461.7 44.6 %collective-permute-start.63 = (bf16[4,24,768]{2,1,0:T(8,128)(2,1)S(1)}, bf16[4,24,768]{2,1,0:T(8,128)(2,1)S(1)}, u32[]{:S(2)}, u32[]{:S(2)}) collective-permute-start(bf16[4,24,768]{2,1,0:T(8,128)(2,1)S(1)} %copy-done.56), channel_id=1, source_target_pairs={{0,16},{1,17},{2,18},{3,19},{4,20},{5,21},{6,22},{7,23},{8,24},{9,... | collective-permute-start | bytes 442376 | tf_op jit(solution)/shard_map/ppermute | solution.py:88
  470.7 24.1 %collective-permute-start.56 = (bf16[256,768]{1,0:T(8,128)(2,1)S(1)}, bf16[256,768]{1,0:T(8,128)(2,1)S(1)}, u32[]{:S(2)}, u32[]{:S(2)}) collective-permute-start(bf16[256,768]{1,0:T(8,128)(2,1)S(1)} %fusion.46), channel_id=1, source_target_pairs={{0,16},{1,17},{2,18},{3,19},{4,20},{5,21},{6,22},{7,23},{8,24},{9,... | collective-permute-start | bytes 1179656 | tf_op jit(solution)/shard_map/ppermute | solution.py:88
  (140 other events, 1311.9 us)
Sparse Core Ops, SparseCore 0:
  14.4 92.0 all-gather.2
  110.0 98.6 all-gather.4

commit v4 on v3

--- a/solution.py
+++ b/solution.py
@@ -926,9 +926,7 @@
     )
     dqkv = jnp.concatenate([query_grad.reshape(GROUPS * rows, QUERY), side_grad], axis=1)
     far_tokens_grad = rounded(back_matmul(dqkv[rows:], qkv_weight)).reshape(Z - 1, rows, width)
-    dqkv, far_tokens_grad = meet(
-        (dqkv, far_tokens_grad), reduce_ffnin, reduce_late, spread_back, reduce_mid
-    )
+    dqkv, far_tokens_grad = lax.optimization_barrier((dqkv, far_tokens_grad))
     third = grid.send(far_tokens_grad[2], "l", 1)
     grad_group = weight_grad(token_column, dqkv)
     sums = jnp.sum(wide(dqkv), axis=0)
@@ -945,12 +943,22 @@
         reduce_late,
         spread_back,
         reduce_mid,
+        reduce_ffnin,
     )
     second = grid.send(rounded(total_of([near_tokens_grad[1], third])), "h", 1)
-    first = grid.send(near_tokens_grad[0], "l", 1)
-    tokens_base, second = meet((tokens_base, second), reduce_group, reduce_late, spread_back)
+    tokens_base, second, last_tokens_grad = meet(
+        (tokens_base, second, near_tokens_grad[0]),
+        reduce_group,
+        reduce_late,
+        spread_back,
+        reduce_mid,
+    )
+    first = grid.send(last_tokens_grad, "l", 1)
+    tokens_base, second, first = meet(
+        (tokens_base, second, first), reduce_group, reduce_late, spread_back
+    )
     drows = spread_back.result
-    meet((), reduce_group, reduce_late, reduce_ffnout, reduce_ffnin)
+    meet((), reduce_late, reduce_ffnout, reduce_ffnin)
     pieces = parted(reduce_group.result.reshape(Z, part, PACK), "z", 0)
     drows, pieces[0] = lax.optimization_barrier((drows, pieces[0]))
     tokens_grad = total_of([tokens_base, first, second])

time: 540 us -> 545 us (level)
    unnamed x204 -> x182, local copies, waits for them, and re-layouts: 11.6 us -> 12.3 us
  transfers between devices with their start and end apart: 70 -> 70, of which waited for: 20 -> 18; matrix products, arithmetic and copies ran while one was open for 24% -> 24% of each run, Pallas kernels for 28% -> 28%
where the time goes in v4:
time: 545 us; the launch traced here: 538 us
  Pallas kernels  151 us (28%)
  waiting for transfers between devices  118 us (22%)
  local copies, waits for them, and re-layouts  72.6 us (13%)
  starting transfers between devices  71.1 us (13%)
  other arithmetic  58.2 us (11%)
  matrix products  48.8 us (9%)
  between operations  17.3 us (3%)
    ppermute x68, waiting for transfers between devices, send(): return lax.ppermute(array, ('seq', 'batch'), pairs)  118 us
    ppermute x68, starting transfers between devices, send(): return lax.ppermute(array, ('seq', 'batch'), pairs)  71 us
    pallas_call x4, Pallas kernels, self_backward(): pl.pallas_call(functools.partial(backward_kernel, rows, parts, first, las...  58 us
    pallas_call x4, Pallas kernels, self_forward(): pl.pallas_call(functools.partial(forward_kernel, rows, parts, first, last...  54.7 us
    convert_element_type x30, other arithmetic, rounded(): return values.astype(jnp.bfloat16)  28.5 us
    dot_general x11, matrix products, matmul(): return jnp.dot(left, right, preferred_element_type=jnp.float32)  22.9 us
    dot_general x12, matrix products, back_matmul(): lax.dot_general(left, right, LANES_IN, preferred_element_type=jnp.float32)  17.4 us
    squeeze x24, local copies, waits for them, and re-layouts, take(): return lax.dynamic_index_in_dim(array, index, axis, keepdims=False)  14.8 us
  transfers between devices with their start and end apart: 70, of which 18 were waited for; matrix products, arithmetic and copies ran while one was open for 24% of the time, Pallas kernels for 28%

profile of v4, /device:TPU:0, one launch (start us, length us, event | category | flops | bytes accessed | tf_op | source)
XLA Modules:
  0.0 537.5 jit_solution(11338135331729459155)
XLA Ops:
  34.0 8.1 %pick_rows.1 = bf16[16,64,768]{2,1,0:T(8,128)(2,1)} custom-call(s32[32]{0:T(128)} %pad_add_fusion.table, bf16[8,64,768]{2,1,0:T(8,128)(2,1)} %bitcast.422), custom_call_target="tpu_custom_call" | custom-call | tf_op jit(solution)/shard_map/pick_rows/pallas_call | solution.py:507
  47.8 8.1 %collective-permute-done.4 = bf16[2,4,24,640]{3,2,1,0:T(8,128)(2,1)} collective-permute-done((bf16[2,4,24,640]{3,2,1,0:T(8,128)(2,1)S(1)}, bf16[2,4,24,640]{3,2,1,0:T(8,128)(2,1)}, u32[]{:S(2)}, u32[]{:S(2)}) %collective-permute-start.4) | collective-permute-done | bytes 245792 | tf_op jit(solution)/shard_map/ppermute | solution.py:88
  55.9 15.2 %collective-permute-done.5 = bf16[256,768]{1,0:T(8,128)(2,1)S(1)} collective-permute-done((bf16[256,768]{1,0:T(8,128)(2,1)S(1)}, bf16[256,768]{1,0:T(8,128)(2,1)S(1)}, u32[]{:S(2)}, u32[]{:S(2)}) %collective-permute-start.5) | collective-permute-done | bytes 393248 | tf_op jit(solution)/shard_map/ppermute | solution.py:88
  75.2 17.1 %collective-permute-done.9 = bf16[256,768]{1,0:T(8,128)(2,1)S(1)} collective-permute-done((bf16[256,768]{1,0:T(8,128)(2,1)S(1)}, bf16[256,768]{1,0:T(8,128)(2,1)S(1)}, u32[]{:S(2)}, u32[]{:S(2)}) %collective-permute-start.9) | collective-permute-done | bytes 393248 | tf_op jit(solution)/shard_map/ppermute | solution.py:88
  104.9 14.3 %self_forward.4 = (f32[4,3,128,256]{3,2,1,0:T(8,128)}, f32[4,16,256]{2,1,0:T(8,128)}) custom-call(s32[9]{0:T(128)} %get-tuple-element.594.table, bf16[4,256,256]{2,1,0:T(8,128)(2,1)} %pad_maximum_fusion.11.query_in, bf16[1024,384]{1,0:T(8,128)(2,1)} %copy-done.79), custom_call_target="tpu_custom_call" | custom-call | flops 3221225472 | bytes 1572864 | tf_op jit(solution)/shard_map/self_forward/pallas_call | solution.py:317
  120.0 13.5 %self_forward.5 = (f32[4,3,128,256]{3,2,1,0:T(8,128)}, f32[4,16,256]{2,1,0:T(8,128)}) custom-call(s32[9]{0:T(128)} %get-tuple-element.596.table, bf16[4,256,256]{2,1,0:T(8,128)(2,1)} %pad_maximum_fusion.11.query_in, bf16[1024,384]{1,0:T(8,128)(2,1)} %copy-done.80, f32[4,3,128,256]{3,2,1,0:T(8,128)} %get-tuple-element.215.refs_1_, ...), custom_call_target="tpu_custom_call" | custom-call | flops 3221225472 | bytes 1572864 | tf_op jit(solution)/shard_map/self_forward/pallas_call | solution.py:317
  136.7 13.7 %self_forward.6 = (f32[4,3,128,256]{3,2,1,0:T(8,128)}, f32[4,16,256]{2,1,0:T(8,128)}) custom-call(s32[9]{0:T(128)} %get-tuple-element.595.table, bf16[4,256,256]{2,1,0:T(8,128)(2,1)} %pad_maximum_fusion.11.query_in, bf16[1024,384]{1,0:T(8,128)(2,1)} %copy-done.81, f32[4,3,128,256]{3,2,1,0:T(8,128)} %get-tuple-element.223.refs_1_, ...), custom_call_target="tpu_custom_call" | custom-call | flops 3221225472 | bytes 1572864 | tf_op jit(solution)/shard_map/self_forward/pallas_call | solution.py:317
  151.2 13.3 %self_forward.7 = (f32[4,256,256]{2,1,0:T(8,128)}, f32[4,8,256]{2,1,0:T(8,128)}) custom-call(s32[9]{0:T(128)} %add_add_fusion.4.table, bf16[4,256,256]{2,1,0:T(8,128)(2,1)} %pad_maximum_fusion.11.query_in, bf16[1024,384]{1,0:T(8,128)(2,1)} %copy-done.82, f32[4,3,128,256]{3,2,1,0:T(8,128)} %get-tuple-element.230.refs_1_, f32[4,16,256]{2,1,0:T(8,128)} %get-tuple-element.231.refs_2_), custom_call_target="tpu_custom_call" | custom-call | flops 3221225472 | bytes 1572864 | tf_op jit(solution)/shard_map/self_forward/pallas_call | solution.py:317
  172.0 10.2 %collective-permute-done.19 = bf16[256,256]{1,0:T(8,128)(2,1)S(1)} collective-permute-done((bf16[256,256]{1,0:T(8,128)(2,1)S(1)}, bf16[256,256]{1,0:T(8,128)(2,1)S(1)}, u32[]{:S(2)}, u32[]{:S(2)}) %collective-permute-start.19) | collective-permute-done | bytes 131104 | tf_op jit(solution)/shard_map/ppermute | solution.py:88
  183.3 4.8 collective-permute-done.21
  200.9 4.0 add_convert_fusion.keys.values
  205.0 11.1 %cross_forward.1 = (bf16[256,768]{1,0:T(8,128)(2,1)}, f32[6,8,256]{2,1,0:T(8,128)}) custom-call(bf16[256,768]{1,0:T(8,128)(2,1)} %fusion.22.query, bf16[1024,1536]{1,0:T(8,128)(2,1)} %add_convert_fusion.keys.values, bf16[1024,1536]{1,0:T(8,128)(2,1)} %add_convert_fusion.keys.values), custom_call_target="tpu_custom_call" | custom-call | flops 1610612736 | bytes 3145728 | tf_op jit(solution)/shard_map/cross_forward/pallas_call | solution.py:441
  218.4 10.1 %multiply_convert_fusion = (bf16[256,3072]{1,0:T(8,128)(2,1)S(1)}, f32[256,3072]{1,0:T(8,128)S(1)}, f32[256,3072]{1,0:T(8,128)S(1)}) fusion(f32[3072]{0:T(1024)S(1)} %add.598, bf16[2,768,3072]{2,1,0:T(8,128)(2,1)} %all-gather.5.cloned.1.call-done, f32[256,768]{1,0:T(8,128)S(1)} %get-tuple-element.598, f32[768]{0:T(1024)S(1)} %get-tuple-element.438, ...), kind=kOutput, calls=%fused_computation.21 | convolution fusion | flops 1260847104 | bytes 13389824 | tf_op jit(solution)/shard_map/dot_general | solution.py:45
  258.5 13.6 %cross_backward.1 = (bf16[256,768]{1,0:T(8,128)(2,1)}, bf16[1024,768]{1,0:T(8,128)(2,1)}, bf16[1024,768]{1,0:T(8,128)(2,1)}) custom-call(bf16[256,768]{1,0:T(8,128)(2,1)} %fusion.22.query, bf16[1024,1536]{1,0:T(8,128)(2,1)} %add_convert_fusion.keys.values, bf16[1024,1536]{1,0:T(8,128)(2,1)} %add_convert_fusion.keys.values, ...), custom_call_target="tpu_custom_call" | custom-call | flops 4026531840 | bytes 6291456 | tf_op jit(solution)/shard_map/cross_backward/pallas_call | solution.py:469
  285.1 3.9 collective-permute-start.26
  316.6 13.6 %self_backward.4 = (bf16[1024,384]{1,0:T(8,128)(2,1)}, f32[4,3,128,256]{3,2,1,0:T(8,128)}, f32[4,8,256]{2,1,0:T(8,128)}) custom-call(s32[9]{0:T(128)} %add_add_fusion.4.table, bf16[4,256,256]{2,1,0:T(8,128)(2,1)} %pad_maximum_fusion.11.query_in, bf16[4,256,256]{2,1,0:T(8,128)(2,1)} %pad_maximum_fusion.12.dout, f32[4,8,256]{2,1,0:T(8,128)} %get-tuple-element.265.state, ...), custom_call_target="tpu_custom_call" | custom-call | flops 4026531840 | bytes 3145728 | tf_op jit(solution)/shard_map/self_backward/pallas_call | solution.py:359
  345.0 14.6 %self_backward.5 = (bf16[1024,384]{1,0:T(8,128)(2,1)}, f32[4,3,128,256]{3,2,1,0:T(8,128)}) custom-call(s32[9]{0:T(128)} %get-tuple-element.595.table, bf16[4,256,256]{2,1,0:T(8,128)(2,1)} %pad_maximum_fusion.11.query_in, bf16[4,256,256]{2,1,0:T(8,128)(2,1)} %pad_maximum_fusion.12.dout, f32[4,8,256]{2,1,0:T(8,128)} %get-tuple-element.266.state, ...), custom_call_target="tpu_custom_call" | custom-call | flops 4026531840 | bytes 3145728 | tf_op jit(solution)/shard_map/self_backward/pallas_call | solution.py:359
  373.2 14.2 %self_backward.6 = (bf16[1024,384]{1,0:T(8,128)(2,1)}, f32[4,3,128,256]{3,2,1,0:T(8,128)}) custom-call(s32[9]{0:T(128)} %get-tuple-element.596.table, bf16[4,256,256]{2,1,0:T(8,128)(2,1)} %pad_maximum_fusion.11.query_in, bf16[4,256,256]{2,1,0:T(8,128)(2,1)} %pad_maximum_fusion.12.dout, f32[4,8,256]{2,1,0:T(8,128)} %get-tuple-element.266.state, ...), custom_call_target="tpu_custom_call" | custom-call | flops 4026531840 | bytes 3145728 | tf_op jit(solution)/shard_map/self_backward/pallas_call | solution.py:359
  387.5 5.3 collective-permute-done.40
  407.6 15.7 %self_backward.7 = (bf16[1024,384]{1,0:T(8,128)(2,1)}, bf16[4,256,256]{2,1,0:T(8,128)(2,1)}) custom-call(s32[9]{0:T(128)} %get-tuple-element.594.table, bf16[4,256,256]{2,1,0:T(8,128)(2,1)} %pad_maximum_fusion.11.query_in, bf16[4,256,256]{2,1,0:T(8,128)(2,1)} %pad_maximum_fusion.12.dout, f32[4,8,256]{2,1,0:T(8,128)} %get-tuple-element.266.state, ...), custom_call_target="tpu_custom_call" | custom-call | flops 4026531840 | bytes 3145728 | tf_op jit(solution)/shard_map/self_backward/pallas_call | solution.py:359
  445.6 13.5 %collective-permute-done.51 = bf16[3,2,24,768]{3,2,1,0:T(8,128)(2,1)S(1)} collective-permute-done((bf16[3,2,24,768]{3,2,1,0:T(8,128)(2,1)S(1)}, bf16[3,2,24,768]{3,2,1,0:T(8,128)(2,1)S(1)}, u32[]{:S(2)}, u32[]{:S(2)}) %collective-permute-start.51) | collective-permute-done | bytes 221216 | tf_op jit(solution)/shard_map/ppermute | solution.py:88
  469.6 14.4 %collective-permute-done.57 = bf16[3,24,768]{2,1,0:T(8,128)(2,1)S(1)} collective-permute-done((bf16[3,24,768]{2,1,0:T(8,128)(2,1)S(1)}, bf16[3,24,768]{2,1,0:T(8,128)(2,1)S(1)}, u32[]{:S(2)}, u32[]{:S(2)}) %collective-permute-start.57) | collective-permute-done | bytes 110624 | tf_op jit(solution)/shard_map/ppermute | solution.py:88
  492.0 12.2 %collective-permute-done.60 = bf16[2,24,1664]{2,1,0:T(8,128)(2,1)S(1)} collective-permute-done((bf16[2,24,1664]{2,1,0:T(8,128)(2,1)S(1)}, bf16[2,24,1664]{2,1,0:T(8,128)(2,1)S(1)}, u32[]{:S(2)}, u32[]{:S(2)}) %collective-permute-start.60) | collective-permute-done | bytes 159776 | tf_op jit(solution)/shard_map/ppermute | solution.py:88
  511.1 5.7 %place_rows.1 = f32[8,64,768]{2,1,0:T(8,128)} custom-call(s32[16]{0:T(128)} %and_select_fusion.3.table, bf16[16,64,768]{2,1,0:T(8,128)(2,1)} %bitcast.397), custom_call_target="tpu_custom_call" | custom-call | tf_op jit(solution)/shard_map/place_rows/pallas_call | solution.py:533
  (578 shorter events, 250.4 us)
Async XLA Ops:
  7.2 186.4 %all-gather.3.cloned.1.call-start = ((), (), s32[]{:S(2)}) async-start(), calls=%async_computation | async-start | bytes 6285312 | tf_op jit(solution)/shard_map/all_gather | solution.py:666
  14.2 204.1 %all-gather.5.cloned.1.call-start = ((), (), s32[]{:S(2)}) async-start(), calls=%async_computation.1 | async-start | bytes 9732096 | tf_op jit(solution)/shard_map/all_gather | solution.py:667
  43.7 27.4 %collective-permute-start.7 = (bf16[2,2,2,1,64,768]{5,4,2,1,0,3:T(8,128)(2,1)S(1)}, bf16[2,2,2,1,64,768]{5,4,2,1,0,3:T(8,128)(2,1)S(1)}, u32[]{:S(2)}, u32[]{:S(2)}) collective-permute-start(bf16[2,2,2,1,64,768]{5,4,2,1,0,3:T(8,128)(2,1)S(1)} %get-tuple-element.488), channel_id=1, source_target_pairs={{0,2},{1,3},{2,0},{3,1},{4,6},{5,7},{6,4},{7,5},{8,10},{9,11},{10,... | collective-permute-start | bytes 2359304 | tf_op jit(solution)/shard_map/ppermute | solution.py:88
  43.8 27.2 %collective-permute-start.5 = (bf16[256,768]{1,0:T(8,128)(2,1)S(1)}, bf16[256,768]{1,0:T(8,128)(2,1)S(1)}, u32[]{:S(2)}, u32[]{:S(2)}) collective-permute-start(bf16[256,768]{1,0:T(8,128)(2,1)S(1)} %bitcast.431), channel_id=1, source_target_pairs={{0,16},{1,17},{2,18},{3,19},{4,20},{5,21},{6,22},{7,23},{8,24},{9,... | collective-permute-start | bytes 1179656 | tf_op jit(solution)/shard_map/ppermute | solution.py:88
  43.9 27.2 %collective-permute-start.6 = (bf16[256,768]{1,0:T(8,128)(2,1)S(1)}, bf16[256,768]{1,0:T(8,128)(2,1)}, u32[]{:S(2)}, u32[]{:S(2)}) collective-permute-start(bf16[256,768]{1,0:T(8,128)(2,1)S(1)} %bitcast.432), channel_id=1, source_target_pairs={{0,8},{1,9},{2,10},{3,11},{4,12},{5,13},{6,14},{7,15},{8,0},{9,1},... | collective-permute-start | bytes 1179656 | tf_op jit(solution)/shard_map/ppermute | solution.py:88
  95.8 23.3 %collective-permute-start.12 = (bf16[1024,384]{1,0:T(8,128)(2,1)S(1)}, bf16[1024,384]{1,0:T(8,128)(2,1)S(1)}, u32[]{:S(2)}, u32[]{:S(2)}) collective-permute-start(bf16[1024,384]{1,0:T(8,128)(2,1)S(1)} %add_convert_fusion.13.refs_0_), channel_id=1, source_target_pairs={{0,2},{1,3},{2,0},{3,1},{4,6},{5,7},{6,4},{7,5},{8,10},{9,11},{10,... | collective-permute-start | bytes 2359304 | tf_op jit(solution)/shard_map/ppermute | solution.py:88
  101.8 31.7 %collective-permute-start.14 = (bf16[1024,384]{1,0:T(8,128)(2,1)S(1)}, bf16[1024,384]{1,0:T(8,128)(2,1)S(1)}, u32[]{:S(2)}, u32[]{:S(2)}) collective-permute-start(bf16[1024,384]{1,0:T(8,128)(2,1)S(1)} %add_convert_fusion.13.refs_0_), channel_id=1, source_target_pairs={{0,4},{1,5},{2,6},{3,7},{4,0},{5,1},{6,2},{7,3},{8,12},{9,13},{10,... | collective-permute-start | bytes 2359304 | tf_op jit(solution)/shard_map/ppermute | solution.py:88
  164.6 25.1 %collective-permute-start.22 = (bf16[2,2,64,768]{3,2,1,0:T(8,128)(2,1)S(1)}, bf16[2,2,64,768]{3,2,1,0:T(8,128)(2,1)S(1)}, u32[]{:S(2)}, u32[]{:S(2)}) collective-permute-start(bf16[2,2,64,768]{3,2,1,0:T(8,128)(2,1)S(1)} %pad_maximum_fusion.15), channel_id=1, source_target_pairs={{0,4},{1,5},{2,6},{3,7},{4,0},{5,1},{6,2},{7,3},{8,12},{9,13},{10,... | collective-permute-start | bytes 1179656 | tf_op jit(solution)/shard_map/ppermute | solution.py:88
  235.8 36.4 %collective-permute-start.24 = (bf16[4,2,2,2,2,24,768]{6,5,4,3,2,1,0:T(8,128)(2,1)}, bf16[4,2,2,2,2,24,768]{6,5,4,3,2,1,0:T(8,128)(2,1)}, u32[]{:S(2)}, u32[]{:S(2)}) collective-permute-start(bf16[4,2,2,2,2,24,768]{6,5,4,3,2,1,0:T(8,128)(2,1)} %get-tuple-element.472), channel_id=1, source_target_pairs={{0,2},{1,3},{2,0},{3,1},{4,6},{5,7},{6,4},{7,5},{8,10},{9,11},{10,... | collective-permute-start | bytes 7077896 | tf_op jit(solution)/shard_map/ppermute | solution.py:88
  245.6 26.5 %collective-permute-start.25 = (bf16[2,2,2,2,24,3072]{5,4,2,1,0,3:T(8,128)(2,1)}, bf16[2,2,2,2,24,3072]{5,4,2,1,0,3:T(8,128)(2,1)}, u32[]{:S(2)}, u32[]{:S(2)}) collective-permute-start(bf16[2,2,2,2,24,3072]{5,4,2,1,0,3:T(8,128)(2,1)} %bitcast.374), channel_id=1, source_target_pairs={{0,2},{1,3},{2,0},{3,1},{4,6},{5,7},{6,4},{7,5},{8,10},{9,11},{10,... | collective-permute-start | bytes 7077896 | tf_op jit(solution)/shard_map/ppermute | solution.py:88
  300.2 29.9 %collective-permute-start.30 = (bf16[4,2,2,2,24,768]{5,4,3,2,1,0:T(8,128)(2,1)}, bf16[4,2,2,2,24,768]{5,4,3,2,1,0:T(8,128)(2,1)}, u32[]{:S(2)}, u32[]{:S(2)}) collective-permute-start(bf16[4,2,2,2,24,768]{5,4,3,2,1,0:T(8,128)(2,1)} %get-tuple-element.482), channel_id=1, source_target_pairs={{0,1},{1,0},{2,3},{3,2},{4,5},{5,4},{6,7},{7,6},{8,9},{9,8},{10,11... | collective-permute-start | bytes 3538952 | tf_op jit(solution)/shard_map/ppermute | solution.py:88
  312.7 46.9 %collective-permute-start.36 = (bf16[2,2,2,24,3072]{4,3,2,1,0:T(8,128)(2,1)}, bf16[2,2,2,24,3072]{4,3,2,1,0:T(8,128)(2,1)}, u32[]{:S(2)}, u32[]{:S(2)}) collective-permute-start(bf16[2,2,2,24,3072]{4,3,2,1,0:T(8,128)(2,1)} %get-tuple-element.480), channel_id=1, source_target_pairs={{0,1},{1,0},{2,3},{3,2},{4,5},{5,4},{6,7},{7,6},{8,9},{9,8},{10,11... | collective-permute-start | bytes 3538952 | tf_op jit(solution)/shard_map/ppermute | solution.py:88
  331.0 28.6 %collective-permute-start.33 = (bf16[1024,384]{1,0:T(8,128)(2,1)}, bf16[1024,384]{1,0:T(8,128)(2,1)}, u32[]{:S(2)}, u32[]{:S(2)}) collective-permute-start(bf16[1024,384]{1,0:T(8,128)(2,1)} %get-tuple-element.276), channel_id=1, source_target_pairs={{0,2},{1,3},{2,0},{3,1},{4,6},{5,7},{6,4},{7,5},{8,10},{9,11},{10,... | collective-permute-start | bytes 2359304 | tf_op jit(solution)/shard_map/ppermute | solution.py:88
  334.3 25.3 %collective-permute-start.34 = (bf16[2,64,1536]{2,1,0:T(8,128)(2,1)}, bf16[2,64,1536]{2,1,0:T(8,128)(2,1)S(1)}, u32[]{:S(2)}, u32[]{:S(2)}) collective-permute-start(bf16[2,64,1536]{2,1,0:T(8,128)(2,1)} %get-tuple-element.503), channel_id=1, source_target_pairs={{0,8},{1,9},{2,10},{3,11},{4,12},{5,13},{6,14},{7,15},{8,0},{9,1},... | collective-permute-start | bytes 1179656 | tf_op jit(solution)/shard_map/ppermute | solution.py:88
  343.5 44.0 %collective-permute-start.41 = (bf16[3,2,2,2,24,768]{5,4,3,2,1,0:T(8,128)(2,1)S(1)}, bf16[3,2,2,2,24,768]{5,4,3,2,1,0:T(8,128)(2,1)S(1)}, u32[]{:S(2)}, u32[]{:S(2)}) collective-permute-start(bf16[3,2,2,2,24,768]{5,4,3,2,1,0:T(8,128)(2,1)S(1)} %get-tuple-element.484), channel_id=1, source_target_pairs={{0,1},{1,0},{2,3},{3,2},{4,5},{5,4},{6,7},{7,6},{8,9},{9,8},{10,11... | collective-permute-start | bytes 2654216 | tf_op jit(solution)/shard_map/ppermute | solution.py:88
  362.3 30.6 %collective-permute-start.37 = (bf16[1024,384]{1,0:T(8,128)(2,1)}, bf16[1024,384]{1,0:T(8,128)(2,1)}, u32[]{:S(2)}, u32[]{:S(2)}) collective-permute-start(bf16[1024,384]{1,0:T(8,128)(2,1)} %add_convert_fusion.11), channel_id=1, source_target_pairs={{0,4},{1,5},{2,6},{3,7},{4,0},{5,1},{6,2},{7,3},{8,12},{9,13},{10,... | collective-permute-start | bytes 2359304 | tf_op jit(solution)/shard_map/ppermute | solution.py:88
  368.7 24.2 %collective-permute-start.40 = (bf16[2,2,24,3072]{3,2,1,0:T(8,128)(2,1)}, bf16[2,2,24,3072]{3,2,1,0:T(8,128)(2,1)}, u32[]{:S(2)}, u32[]{:S(2)}) collective-permute-start(bf16[2,2,24,3072]{3,2,1,0:T(8,128)(2,1)} %get-tuple-element.492), channel_id=1, source_target_pairs={{0,4},{1,5},{2,6},{3,7},{4,0},{5,1},{6,2},{7,3},{8,12},{9,13},{10,... | collective-permute-start | bytes 1769480 | tf_op jit(solution)/shard_map/ppermute | solution.py:88
  396.5 27.5 %collective-permute-start.42 = (bf16[1024,384]{1,0:T(8,128)(2,1)}, bf16[1024,384]{1,0:T(8,128)(2,1)}, u32[]{:S(2)}, u32[]{:S(2)}) collective-permute-start(bf16[1024,384]{1,0:T(8,128)(2,1)} %get-tuple-element.306), channel_id=1, source_target_pairs={{0,2},{1,3},{2,0},{3,1},{4,6},{5,7},{6,4},{7,5},{8,10},{9,11},{10,... | collective-permute-start | bytes 2359304 | tf_op jit(solution)/shard_map/ppermute | solution.py:88
  396.7 27.4 %collective-permute-start.43 = (bf16[2,2,2,2,24,1664]{5,4,2,1,0,3:T(8,128)(2,1)S(1)}, bf16[2,2,2,2,24,1664]{5,4,2,1,0,3:T(8,128)(2,1)}, u32[]{:S(2)}, u32[]{:S(2)}) collective-permute-start(bf16[2,2,2,2,24,1664]{5,4,2,1,0,3:T(8,128)(2,1)S(1)} %bitcast.416), channel_id=1, source_target_pairs={{0,2},{1,3},{2,0},{3,1},{4,6},{5,7},{6,4},{7,5},{8,10},{9,11},{10,... | collective-permute-start | bytes 3833864 | tf_op jit(solution)/shard_map/ppermute | solution.py:88
  406.1 38.0 %collective-permute-start.52 = (bf16[2,24,3072]{2,1,0:T(8,128)(2,1)}, bf16[2,24,3072]{2,1,0:T(8,128)(2,1)}, u32[]{:S(2)}, u32[]{:S(2)}) collective-permute-start(bf16[2,24,3072]{2,1,0:T(8,128)(2,1)} %get-tuple-element.511), channel_id=1, source_target_pairs={{0,8},{1,9},{2,10},{3,11},{4,12},{5,13},{6,14},{7,15},{8,0},{9,1},... | collective-permute-start | bytes 884744 | tf_op jit(solution)/shard_map/ppermute | solution.py:88
  428.0 31.0 %collective-permute-start.49 = (bf16[2,2,2,24,1664]{4,3,2,1,0:T(8,128)(2,1)}, bf16[2,2,2,24,1664]{4,3,2,1,0:T(8,128)(2,1)}, u32[]{:S(2)}, u32[]{:S(2)}) collective-permute-start(bf16[2,2,2,24,1664]{4,3,2,1,0:T(8,128)(2,1)} %get-tuple-element.490), channel_id=1, source_target_pairs={{0,1},{1,0},{2,3},{3,2},{4,5},{5,4},{6,7},{7,6},{8,9},{9,8},{10,11... | collective-permute-start | bytes 1916936 | tf_op jit(solution)/shard_map/ppermute | solution.py:88
  459.2 24.8 %collective-permute-start.53 = (bf16[256,768]{1,0:T(8,128)(2,1)S(1)}, bf16[256,768]{1,0:T(8,128)(2,1)S(1)}, u32[]{:S(2)}, u32[]{:S(2)}) collective-permute-start(bf16[256,768]{1,0:T(8,128)(2,1)S(1)} %fusion.46), channel_id=1, source_target_pairs={{0,16},{1,17},{2,18},{3,19},{4,20},{5,21},{6,22},{7,23},{8,24},{9,... | collective-permute-start | bytes 1179656 | tf_op jit(solution)/shard_map/ppermute | solution.py:88
  483.9 34.9 %collective-permute-start.66 = (bf16[4,24,768]{2,1,0:T(8,128)(2,1)S(1)}, bf16[4,24,768]{2,1,0:T(8,128)(2,1)S(1)}, u32[]{:S(2)}, u32[]{:S(2)}) collective-permute-start(bf16[4,24,768]{2,1,0:T(8,128)(2,1)S(1)} %copy-done.45), channel_id=1, source_target_pairs={{0,16},{1,17},{2,18},{3,19},{4,20},{5,21},{6,22},{7,23},{8,24},{9,... | collective-permute-start | bytes 442376 | tf_op jit(solution)/shard_map/ppermute | solution.py:88
  491.2 27.6 %collective-permute-start.67 = (bf16[24,3072]{1,0:T(8,128)(2,1)S(1)}, bf16[24,3072]{1,0:T(8,128)(2,1)S(1)}, u32[]{:S(2)}, u32[]{:S(2)}) collective-permute-start(bf16[24,3072]{1,0:T(8,128)(2,1)S(1)} %get-tuple-element.543), channel_id=1, source_target_pairs={{0,16},{1,17},{2,18},{3,19},{4,20},{5,21},{6,22},{7,23},{8,24},{9,... | collective-permute-start | bytes 442376 | tf_op jit(solution)/shard_map/ppermute | solution.py:88
  (129 other events, 1297.2 us)
Sparse Core Ops, SparseCore 0:
  14.4 92.6 all-gather.2
  110.5 98.4 all-gather.4

commit v5 on v3

--- a/solution.py
+++ b/solution.py
@@ -908,7 +908,7 @@
     bias_rows = jnp.concatenate([bias_rows, inner_sums.reshape(fan, width)], axis=0)
     bias_columns = jnp.pad(rounded(bias_rows.T), ((0, 0), (0, 128 - bias_rows.shape[0])))
     grad_late = jnp.concatenate([rounded(weight_grad(own_rows, dcross_pair)), bias_columns], axis=1)
-    reduce_late = Chain(reduction(sharded(grad_late), "cyxlh"))
+    reduce_late = Chain(reduction(sharded(grad_late), "cxylh"))
     spread_back = Chain(spreading(rounded(back_matmul(dcross_pair, crosskv_full))))
 
     slopes = settle(slopes, reduce_late, spread_back, reduce_ffnin, reduce_mid)

time: 540 us -> 540 us (level)
  transfers between devices with their start and end apart: 70 -> 70, of which waited for: 20 -> 19; matrix products, arithmetic and copies ran while one was open for 24% -> 24% of each run, Pallas kernels for 28% -> 28%
where the time goes in v5:
time: 540 us; the launch traced here: 534 us
  Pallas kernels  147 us (27%)
  waiting for transfers between devices  115 us (21%)
  starting transfers between devices  76.8 us (14%)
  local copies, waits for them, and re-layouts  73.6 us (14%)
  other arithmetic  55.9 us (10%)
  matrix products  47.8 us (9%)
  between operations  17.4 us (3%)
    ppermute x68, waiting for transfers between devices, send(): return lax.ppermute(array, ('seq', 'batch'), pairs)  115 us
    ppermute x68, starting transfers between devices, send(): return lax.ppermute(array, ('seq', 'batch'), pairs)  76.7 us
    pallas_call x4, Pallas kernels, self_backward(): pl.pallas_call(functools.partial(backward_kernel, rows, parts, first, las...  56 us
    pallas_call x4, Pallas kernels, self_forward(): pl.pallas_call(functools.partial(forward_kernel, rows, parts, first, last...  52.5 us
    convert_element_type x30, other arithmetic, rounded(): return values.astype(jnp.bfloat16)  27.1 us
    dot_general x11, matrix products, matmul(): return jnp.dot(left, right, preferred_element_type=jnp.float32)  23 us
    dot_general x12, matrix products, back_matmul(): lax.dot_general(left, right, LANES_IN, preferred_element_type=jnp.float32)  16.4 us
    squeeze x24, local copies, waits for them, and re-layouts, take(): return lax.dynamic_index_in_dim(array, index, axis, keepdims=False)  15.2 us
  transfers between devices with their start and end apart: 70, of which 19 were waited for; matrix products, arithmetic and copies ran while one was open for 24% of the time, Pallas kernels for 28%

profile of v5, /device:TPU:0, one launch (start us, length us, event | category | flops | bytes accessed | tf_op | source)
XLA Modules:
  0.0 533.6 jit_solution(15615683217639123274)
XLA Ops:
  34.0 8.1 %pick_rows.1 = bf16[16,64,768]{2,1,0:T(8,128)(2,1)} custom-call(s32[32]{0:T(128)} %pad_add_fusion.table, bf16[8,64,768]{2,1,0:T(8,128)(2,1)} %bitcast.422), custom_call_target="tpu_custom_call" | custom-call | tf_op jit(solution)/shard_map/pick_rows/pallas_call | solution.py:507
  47.5 8.4 %collective-permute-done.4 = bf16[2,4,24,640]{3,2,1,0:T(8,128)(2,1)} collective-permute-done((bf16[2,4,24,640]{3,2,1,0:T(8,128)(2,1)S(1)}, bf16[2,4,24,640]{3,2,1,0:T(8,128)(2,1)}, u32[]{:S(2)}, u32[]{:S(2)}) %collective-permute-start.4) | collective-permute-done | bytes 245792 | tf_op jit(solution)/shard_map/ppermute | solution.py:88
  55.9 15.2 %collective-permute-done.5 = bf16[256,768]{1,0:T(8,128)(2,1)S(1)} collective-permute-done((bf16[256,768]{1,0:T(8,128)(2,1)S(1)}, bf16[256,768]{1,0:T(8,128)(2,1)S(1)}, u32[]{:S(2)}, u32[]{:S(2)}) %collective-permute-start.5) | collective-permute-done | bytes 393248 | tf_op jit(solution)/shard_map/ppermute | solution.py:88
  75.2 17.2 %collective-permute-done.9 = bf16[256,768]{1,0:T(8,128)(2,1)S(1)} collective-permute-done((bf16[256,768]{1,0:T(8,128)(2,1)S(1)}, bf16[256,768]{1,0:T(8,128)(2,1)S(1)}, u32[]{:S(2)}, u32[]{:S(2)}) %collective-permute-start.9) | collective-permute-done | bytes 393248 | tf_op jit(solution)/shard_map/ppermute | solution.py:88
  104.9 14.3 %self_forward.4 = (f32[4,3,128,256]{3,2,1,0:T(8,128)}, f32[4,16,256]{2,1,0:T(8,128)}) custom-call(s32[9]{0:T(128)} %get-tuple-element.586.table, bf16[4,256,256]{2,1,0:T(8,128)(2,1)} %pad_maximum_fusion.11.query_in, bf16[1024,384]{1,0:T(8,128)(2,1)} %copy-done.90), custom_call_target="tpu_custom_call" | custom-call | flops 3221225472 | bytes 1572864 | tf_op jit(solution)/shard_map/self_forward/pallas_call | solution.py:317
  120.0 12.5 %self_forward.5 = (f32[4,3,128,256]{3,2,1,0:T(8,128)}, f32[4,16,256]{2,1,0:T(8,128)}) custom-call(s32[9]{0:T(128)} %get-tuple-element.588.table, bf16[4,256,256]{2,1,0:T(8,128)(2,1)} %pad_maximum_fusion.11.query_in, bf16[1024,384]{1,0:T(8,128)(2,1)} %copy-done.91, f32[4,3,128,256]{3,2,1,0:T(8,128)} %get-tuple-element.211.refs_1_, ...), custom_call_target="tpu_custom_call" | custom-call | flops 3221225472 | bytes 1572864 | tf_op jit(solution)/shard_map/self_forward/pallas_call | solution.py:317
  135.6 12.5 %self_forward.6 = (f32[4,3,128,256]{3,2,1,0:T(8,128)}, f32[4,16,256]{2,1,0:T(8,128)}) custom-call(s32[9]{0:T(128)} %get-tuple-element.587.table, bf16[4,256,256]{2,1,0:T(8,128)(2,1)} %pad_maximum_fusion.11.query_in, bf16[1024,384]{1,0:T(8,128)(2,1)} %copy-done.92, f32[4,3,128,256]{3,2,1,0:T(8,128)} %get-tuple-element.219.refs_1_, ...), custom_call_target="tpu_custom_call" | custom-call | flops 3221225472 | bytes 1572864 | tf_op jit(solution)/shard_map/self_forward/pallas_call | solution.py:317
  149.0 13.3 %self_forward.7 = (f32[4,256,256]{2,1,0:T(8,128)}, f32[4,8,256]{2,1,0:T(8,128)}) custom-call(s32[9]{0:T(128)} %add_add_fusion.4.table, bf16[4,256,256]{2,1,0:T(8,128)(2,1)} %pad_maximum_fusion.11.query_in, bf16[1024,384]{1,0:T(8,128)(2,1)} %copy-done.93, f32[4,3,128,256]{3,2,1,0:T(8,128)} %get-tuple-element.226.refs_1_, f32[4,16,256]{2,1,0:T(8,128)} %get-tuple-element.227.refs_2_), custom_call_target="tpu_custom_call" | custom-call | flops 3221225472 | bytes 1572864 | tf_op jit(solution)/shard_map/self_forward/pallas_call | solution.py:317
  170.3 9.0 %collective-permute-done.19 = bf16[256,256]{1,0:T(8,128)(2,1)S(1)} collective-permute-done((bf16[256,256]{1,0:T(8,128)(2,1)S(1)}, bf16[256,256]{1,0:T(8,128)(2,1)S(1)}, u32[]{:S(2)}, u32[]{:S(2)}) %collective-permute-start.19) | collective-permute-done | bytes 131104 | tf_op jit(solution)/shard_map/ppermute | solution.py:88
  179.3 6.6 %collective-permute-done.20 = bf16[256,256]{1,0:T(8,128)(2,1)S(1)} collective-permute-done((bf16[256,256]{1,0:T(8,128)(2,1)S(1)}, bf16[256,256]{1,0:T(8,128)(2,1)S(1)}, u32[]{:S(2)}, u32[]{:S(2)}) %collective-permute-start.20) | collective-permute-done | bytes 131104 | tf_op jit(solution)/shard_map/ppermute | solution.py:88
  201.2 11.1 %cross_forward.1 = (bf16[256,768]{1,0:T(8,128)(2,1)}, f32[6,8,256]{2,1,0:T(8,128)}) custom-call(bf16[256,768]{1,0:T(8,128)(2,1)} %fusion.22.query, bf16[1024,1536]{1,0:T(8,128)(2,1)} %add_convert_fusion.keys.values, bf16[1024,1536]{1,0:T(8,128)(2,1)} %add_convert_fusion.keys.values), custom_call_target="tpu_custom_call" | custom-call | flops 1610612736 | bytes 3145728 | tf_op jit(solution)/shard_map/cross_forward/pallas_call | solution.py:441
  214.7 10.1 %multiply_convert_fusion = (bf16[256,3072]{1,0:T(8,128)(2,1)S(1)}, f32[256,3072]{1,0:T(8,128)S(1)}, f32[256,3072]{1,0:T(8,128)S(1)}) fusion(f32[3072]{0:T(1024)S(1)} %add.598, bf16[2,768,3072]{2,1,0:T(8,128)(2,1)} %all-gather.5.cloned.1.call-done, f32[256,768]{1,0:T(8,128)S(1)} %get-tuple-element.590, f32[768]{0:T(1024)S(1)} %get-tuple-element.430, ...), kind=kOutput, calls=%fused_computation.21 | convolution fusion | flops 1260847104 | bytes 13389824 | tf_op jit(solution)/shard_map/dot_general | solution.py:45
  254.8 13.6 %cross_backward.1 = (bf16[256,768]{1,0:T(8,128)(2,1)}, bf16[1024,768]{1,0:T(8,128)(2,1)}, bf16[1024,768]{1,0:T(8,128)(2,1)}) custom-call(bf16[256,768]{1,0:T(8,128)(2,1)} %fusion.22.query, bf16[1024,1536]{1,0:T(8,128)(2,1)} %add_convert_fusion.keys.values, bf16[1024,1536]{1,0:T(8,128)(2,1)} %add_convert_fusion.keys.values, ...), custom_call_target="tpu_custom_call" | custom-call | flops 4026531840 | bytes 6291456 | tf_op jit(solution)/shard_map/cross_backward/pallas_call | solution.py:469
  281.5 10.6 %collective-permute-start.26 = (bf16[256,256]{1,0:T(8,128)(2,1)S(1)}, bf16[256,256]{1,0:T(8,128)(2,1)}, u32[]{:S(2)}, u32[]{:S(2)}) collective-permute-start(bf16[256,256]{1,0:T(8,128)(2,1)S(1)} %bitcast.442), channel_id=1, source_target_pairs={{0,14},{1,15},{2,12},{3,13},{4,10},{5,11},{6,8},{7,9},{8,6},{9,7},... | collective-permute-start | bytes 393224 | tf_op jit(solution)/shard_map/ppermute | solution.py:88
  318.6 13.6 %self_backward.4 = (bf16[1024,384]{1,0:T(8,128)(2,1)}, f32[4,3,128,256]{3,2,1,0:T(8,128)}, f32[4,8,256]{2,1,0:T(8,128)}) custom-call(s32[9]{0:T(128)} %add_add_fusion.4.table, bf16[4,256,256]{2,1,0:T(8,128)(2,1)} %pad_maximum_fusion.11.query_in, bf16[4,256,256]{2,1,0:T(8,128)(2,1)} %pad_maximum_fusion.12.dout, f32[4,8,256]{2,1,0:T(8,128)} %get-tuple-element.261.state, ...), custom_call_target="tpu_custom_call" | custom-call | flops 4026531840 | bytes 3145728 | tf_op jit(solution)/shard_map/self_backward/pallas_call | solution.py:359
  346.9 13.6 %self_backward.5 = (bf16[1024,384]{1,0:T(8,128)(2,1)}, f32[4,3,128,256]{3,2,1,0:T(8,128)}) custom-call(s32[9]{0:T(128)} %get-tuple-element.587.table, bf16[4,256,256]{2,1,0:T(8,128)(2,1)} %pad_maximum_fusion.11.query_in, bf16[4,256,256]{2,1,0:T(8,128)(2,1)} %pad_maximum_fusion.12.dout, f32[4,8,256]{2,1,0:T(8,128)} %get-tuple-element.262.state, ...), custom_call_target="tpu_custom_call" | custom-call | flops 4026531840 | bytes 3145728 | tf_op jit(solution)/shard_map/self_backward/pallas_call | solution.py:359
  373.7 13.2 %self_backward.6 = (bf16[1024,384]{1,0:T(8,128)(2,1)}, f32[4,3,128,256]{3,2,1,0:T(8,128)}) custom-call(s32[9]{0:T(128)} %get-tuple-element.588.table, bf16[4,256,256]{2,1,0:T(8,128)(2,1)} %pad_maximum_fusion.11.query_in, bf16[4,256,256]{2,1,0:T(8,128)(2,1)} %pad_maximum_fusion.12.dout, f32[4,8,256]{2,1,0:T(8,128)} %get-tuple-element.262.state, ...), custom_call_target="tpu_custom_call" | custom-call | flops 4026531840 | bytes 3145728 | tf_op jit(solution)/shard_map/self_backward/pallas_call | solution.py:359
  387.1 6.3 %collective-permute-done.40 = bf16[2,2,24,3072]{3,2,1,0:T(8,128)(2,1)} collective-permute-done((bf16[2,2,24,3072]{3,2,1,0:T(8,128)(2,1)}, bf16[2,2,24,3072]{3,2,1,0:T(8,128)(2,1)}, u32[]{:S(2)}, u32[]{:S(2)}) %collective-permute-start.40) | collective-permute-done | bytes 589856 | tf_op jit(solution)/shard_map/ppermute | solution.py:88
  408.2 15.7 %self_backward.7 = (bf16[1024,384]{1,0:T(8,128)(2,1)}, bf16[4,256,256]{2,1,0:T(8,128)(2,1)}) custom-call(s32[9]{0:T(128)} %get-tuple-element.586.table, bf16[4,256,256]{2,1,0:T(8,128)(2,1)} %pad_maximum_fusion.11.query_in, bf16[4,256,256]{2,1,0:T(8,128)(2,1)} %pad_maximum_fusion.12.dout, f32[4,8,256]{2,1,0:T(8,128)} %get-tuple-element.262.state, ...), custom_call_target="tpu_custom_call" | custom-call | flops 4026531840 | bytes 3145728 | tf_op jit(solution)/shard_map/self_backward/pallas_call | solution.py:359
  460.1 5.4 %collective-permute-done.55 = bf16[3,24,768]{2,1,0:T(8,128)(2,1)S(1)} collective-permute-done((bf16[3,24,768]{2,1,0:T(8,128)(2,1)S(1)}, bf16[3,24,768]{2,1,0:T(8,128)(2,1)S(1)}, u32[]{:S(2)}, u32[]{:S(2)}) %collective-permute-start.55) | collective-permute-done | bytes 110624 | tf_op jit(solution)/shard_map/ppermute | solution.py:88
  472.8 7.9 %collective-permute-done.58 = bf16[2,24,1664]{2,1,0:T(8,128)(2,1)S(1)} collective-permute-done((bf16[2,24,1664]{2,1,0:T(8,128)(2,1)S(1)}, bf16[2,24,1664]{2,1,0:T(8,128)(2,1)S(1)}, u32[]{:S(2)}, u32[]{:S(2)}) %collective-permute-start.58) | collective-permute-done | bytes 159776 | tf_op jit(solution)/shard_map/ppermute | solution.py:88
  484.0 10.5 %collective-permute-done.56 = bf16[256,768]{1,0:T(8,128)(2,1)S(1)} collective-permute-done((bf16[256,768]{1,0:T(8,128)(2,1)S(1)}, bf16[256,768]{1,0:T(8,128)(2,1)S(1)}, u32[]{:S(2)}, u32[]{:S(2)}) %collective-permute-start.56) | collective-permute-done | bytes 393248 | tf_op jit(solution)/shard_map/ppermute | solution.py:88
  495.1 9.7 %collective-permute-done.60 = bf16[256,768]{1,0:T(8,128)(2,1)S(1)} collective-permute-done((bf16[256,768]{1,0:T(8,128)(2,1)S(1)}, bf16[256,768]{1,0:T(8,128)(2,1)S(1)}, u32[]{:S(2)}, u32[]{:S(2)}) %collective-permute-start.60) | collective-permute-done | bytes 393248 | tf_op jit(solution)/shard_map/ppermute | solution.py:88
  518.9 5.6 %place_rows.1 = f32[8,64,768]{2,1,0:T(8,128)} custom-call(s32[16]{0:T(128)} %and_select_fusion.3.table, bf16[16,64,768]{2,1,0:T(8,128)(2,1)} %bitcast.397), custom_call_target="tpu_custom_call" | custom-call | tf_op jit(solution)/shard_map/place_rows/pallas_call | solution.py:533
  (600 shorter events, 252.6 us)
Async XLA Ops:
  7.2 182.6 %all-gather.3.cloned.1.call-start = ((), (), s32[]{:S(2)}) async-start(), calls=%async_computation | async-start | bytes 6285312 | tf_op jit(solution)/shard_map/all_gather | solution.py:666
  14.2 200.4 %all-gather.5.cloned.1.call-start = ((), (), s32[]{:S(2)}) async-start(), calls=%async_computation.1 | async-start | bytes 9732096 | tf_op jit(solution)/shard_map/all_gather | solution.py:667
  43.7 27.4 %collective-permute-start.7 = (bf16[2,2,2,1,64,768]{5,4,2,1,0,3:T(8,128)(2,1)S(1)}, bf16[2,2,2,1,64,768]{5,4,2,1,0,3:T(8,128)(2,1)S(1)}, u32[]{:S(2)}, u32[]{:S(2)}) collective-permute-start(bf16[2,2,2,1,64,768]{5,4,2,1,0,3:T(8,128)(2,1)S(1)} %get-tuple-element.480), channel_id=1, source_target_pairs={{0,2},{1,3},{2,0},{3,1},{4,6},{5,7},{6,4},{7,5},{8,10},{9,11},{10,... | collective-permute-start | bytes 2359304 | tf_op jit(solution)/shard_map/ppermute | solution.py:88
  43.8 27.2 %collective-permute-start.5 = (bf16[256,768]{1,0:T(8,128)(2,1)S(1)}, bf16[256,768]{1,0:T(8,128)(2,1)S(1)}, u32[]{:S(2)}, u32[]{:S(2)}) collective-permute-start(bf16[256,768]{1,0:T(8,128)(2,1)S(1)} %bitcast.432), channel_id=1, source_target_pairs={{0,16},{1,17},{2,18},{3,19},{4,20},{5,21},{6,22},{7,23},{8,24},{9,... | collective-permute-start | bytes 1179656 | tf_op jit(solution)/shard_map/ppermute | solution.py:88
  43.9 27.2 %collective-permute-start.6 = (bf16[256,768]{1,0:T(8,128)(2,1)S(1)}, bf16[256,768]{1,0:T(8,128)(2,1)}, u32[]{:S(2)}, u32[]{:S(2)}) collective-permute-start(bf16[256,768]{1,0:T(8,128)(2,1)S(1)} %bitcast.433), channel_id=1, source_target_pairs={{0,8},{1,9},{2,10},{3,11},{4,12},{5,13},{6,14},{7,15},{8,0},{9,1},... | collective-permute-start | bytes 1179656 | tf_op jit(solution)/shard_map/ppermute | solution.py:88
  95.8 23.3 %collective-permute-start.12 = (bf16[1024,384]{1,0:T(8,128)(2,1)S(1)}, bf16[1024,384]{1,0:T(8,128)(2,1)S(1)}, u32[]{:S(2)}, u32[]{:S(2)}) collective-permute-start(bf16[1024,384]{1,0:T(8,128)(2,1)S(1)} %add_convert_fusion.13.refs_0_), channel_id=1, source_target_pairs={{0,2},{1,3},{2,0},{3,1},{4,6},{5,7},{6,4},{7,5},{8,10},{9,11},{10,... | collective-permute-start | bytes 2359304 | tf_op jit(solution)/shard_map/ppermute | solution.py:88
  101.9 30.6 %collective-permute-start.14 = (bf16[1024,384]{1,0:T(8,128)(2,1)S(1)}, bf16[1024,384]{1,0:T(8,128)(2,1)S(1)}, u32[]{:S(2)}, u32[]{:S(2)}) collective-permute-start(bf16[1024,384]{1,0:T(8,128)(2,1)S(1)} %add_convert_fusion.13.refs_0_), channel_id=1, source_target_pairs={{0,4},{1,5},{2,6},{3,7},{4,0},{5,1},{6,2},{7,3},{8,12},{9,13},{10,... | collective-permute-start | bytes 2359304 | tf_op jit(solution)/shard_map/ppermute | solution.py:88
  162.3 23.6 %collective-permute-start.22 = (bf16[2,2,64,768]{3,2,1,0:T(8,128)(2,1)S(1)}, bf16[2,2,64,768]{3,2,1,0:T(8,128)(2,1)S(1)}, u32[]{:S(2)}, u32[]{:S(2)}) collective-permute-start(bf16[2,2,64,768]{3,2,1,0:T(8,128)(2,1)S(1)} %pad_maximum_fusion.15), channel_id=1, source_target_pairs={{0,4},{1,5},{2,6},{3,7},{4,0},{5,1},{6,2},{7,3},{8,12},{9,13},{10,... | collective-permute-start | bytes 1179656 | tf_op jit(solution)/shard_map/ppermute | solution.py:88
  232.0 36.5 %collective-permute-start.24 = (bf16[4,2,2,2,2,24,768]{6,5,4,3,2,1,0:T(8,128)(2,1)}, bf16[4,2,2,2,2,24,768]{6,5,4,3,2,1,0:T(8,128)(2,1)}, u32[]{:S(2)}, u32[]{:S(2)}) collective-permute-start(bf16[4,2,2,2,2,24,768]{6,5,4,3,2,1,0:T(8,128)(2,1)} %get-tuple-element.464), channel_id=1, source_target_pairs={{0,2},{1,3},{2,0},{3,1},{4,6},{5,7},{6,4},{7,5},{8,10},{9,11},{10,... | collective-permute-start | bytes 7077896 | tf_op jit(solution)/shard_map/ppermute | solution.py:88
  241.9 26.6 %collective-permute-start.25 = (bf16[2,2,2,2,24,3072]{5,4,2,1,0,3:T(8,128)(2,1)}, bf16[2,2,2,2,24,3072]{5,4,2,1,0,3:T(8,128)(2,1)}, u32[]{:S(2)}, u32[]{:S(2)}) collective-permute-start(bf16[2,2,2,2,24,3072]{5,4,2,1,0,3:T(8,128)(2,1)} %bitcast.374), channel_id=1, source_target_pairs={{0,2},{1,3},{2,0},{3,1},{4,6},{5,7},{6,4},{7,5},{8,10},{9,11},{10,... | collective-permute-start | bytes 7077896 | tf_op jit(solution)/shard_map/ppermute | solution.py:88
  281.5 26.7 %collective-permute-start.26 = (bf16[256,256]{1,0:T(8,128)(2,1)S(1)}, bf16[256,256]{1,0:T(8,128)(2,1)}, u32[]{:S(2)}, u32[]{:S(2)}) collective-permute-start(bf16[256,256]{1,0:T(8,128)(2,1)S(1)} %bitcast.442), channel_id=1, source_target_pairs={{0,14},{1,15},{2,12},{3,13},{4,10},{5,11},{6,8},{7,9},{8,6},{9,7},... | collective-permute-start | bytes 393224 | tf_op jit(solution)/shard_map/ppermute | solution.py:88
  303.3 29.2 %collective-permute-start.30 = (bf16[4,2,2,2,24,768]{5,4,3,2,1,0:T(8,128)(2,1)}, bf16[4,2,2,2,24,768]{5,4,3,2,1,0:T(8,128)(2,1)}, u32[]{:S(2)}, u32[]{:S(2)}) collective-permute-start(bf16[4,2,2,2,24,768]{5,4,3,2,1,0:T(8,128)(2,1)} %get-tuple-element.474), channel_id=1, source_target_pairs={{0,1},{1,0},{2,3},{3,2},{4,5},{5,4},{6,7},{7,6},{8,9},{9,8},{10,11... | collective-permute-start | bytes 3538952 | tf_op jit(solution)/shard_map/ppermute | solution.py:88
  314.6 45.9 %collective-permute-start.36 = (bf16[2,2,2,24,3072]{4,3,2,1,0:T(8,128)(2,1)}, bf16[2,2,2,24,3072]{4,3,2,1,0:T(8,128)(2,1)}, u32[]{:S(2)}, u32[]{:S(2)}) collective-permute-start(bf16[2,2,2,24,3072]{4,3,2,1,0:T(8,128)(2,1)} %get-tuple-element.472), channel_id=1, source_target_pairs={{0,1},{1,0},{2,3},{3,2},{4,5},{5,4},{6,7},{7,6},{8,9},{9,8},{10,11... | collective-permute-start | bytes 3538952 | tf_op jit(solution)/shard_map/ppermute | solution.py:88
  333.4 27.2 %collective-permute-start.33 = (bf16[1024,384]{1,0:T(8,128)(2,1)}, bf16[1024,384]{1,0:T(8,128)(2,1)}, u32[]{:S(2)}, u32[]{:S(2)}) collective-permute-start(bf16[1024,384]{1,0:T(8,128)(2,1)} %get-tuple-element.272), channel_id=1, source_target_pairs={{0,2},{1,3},{2,0},{3,1},{4,6},{5,7},{6,4},{7,5},{8,10},{9,11},{10,... | collective-permute-start | bytes 2359304 | tf_op jit(solution)/shard_map/ppermute | solution.py:88
  335.8 24.8 %collective-permute-start.34 = (bf16[2,64,1536]{2,1,0:T(8,128)(2,1)}, bf16[2,64,1536]{2,1,0:T(8,128)(2,1)S(1)}, u32[]{:S(2)}, u32[]{:S(2)}) collective-permute-start(bf16[2,64,1536]{2,1,0:T(8,128)(2,1)} %get-tuple-element.495), channel_id=1, source_target_pairs={{0,8},{1,9},{2,10},{3,11},{4,12},{5,13},{6,14},{7,15},{8,0},{9,1},... | collective-permute-start | bytes 1179656 | tf_op jit(solution)/shard_map/ppermute | solution.py:88
  345.4 41.6 %collective-permute-start.41 = (bf16[3,2,2,2,24,768]{5,4,3,2,1,0:T(8,128)(2,1)S(1)}, bf16[3,2,2,2,24,768]{5,4,3,2,1,0:T(8,128)(2,1)S(1)}, u32[]{:S(2)}, u32[]{:S(2)}) collective-permute-start(bf16[3,2,2,2,24,768]{5,4,3,2,1,0:T(8,128)(2,1)S(1)} %get-tuple-element.476), channel_id=1, source_target_pairs={{0,1},{1,0},{2,3},{3,2},{4,5},{5,4},{6,7},{7,6},{8,9},{9,8},{10,11... | collective-permute-start | bytes 2654216 | tf_op jit(solution)/shard_map/ppermute | solution.py:88
  363.2 30.1 %collective-permute-start.37 = (bf16[1024,384]{1,0:T(8,128)(2,1)}, bf16[1024,384]{1,0:T(8,128)(2,1)}, u32[]{:S(2)}, u32[]{:S(2)}) collective-permute-start(bf16[1024,384]{1,0:T(8,128)(2,1)} %add_convert_fusion.11), channel_id=1, source_target_pairs={{0,4},{1,5},{2,6},{3,7},{4,0},{5,1},{6,2},{7,3},{8,12},{9,13},{10,... | collective-permute-start | bytes 2359304 | tf_op jit(solution)/shard_map/ppermute | solution.py:88
  397.0 27.7 %collective-permute-start.42 = (bf16[1024,384]{1,0:T(8,128)(2,1)}, bf16[1024,384]{1,0:T(8,128)(2,1)}, u32[]{:S(2)}, u32[]{:S(2)}) collective-permute-start(bf16[1024,384]{1,0:T(8,128)(2,1)} %get-tuple-element.302), channel_id=1, source_target_pairs={{0,2},{1,3},{2,0},{3,1},{4,6},{5,7},{6,4},{7,5},{8,10},{9,11},{10,... | collective-permute-start | bytes 2359304 | tf_op jit(solution)/shard_map/ppermute | solution.py:88
  397.2 27.5 %collective-permute-start.43 = (bf16[2,2,2,2,24,1664]{5,4,3,1,0,2:T(8,128)(2,1)S(1)}, bf16[2,2,2,2,24,1664]{5,4,3,1,0,2:T(8,128)(2,1)}, u32[]{:S(2)}, u32[]{:S(2)}) collective-permute-start(bf16[2,2,2,2,24,1664]{5,4,3,1,0,2:T(8,128)(2,1)S(1)} %bitcast.416), channel_id=1, source_target_pairs={{0,2},{1,3},{2,0},{3,1},{4,6},{5,7},{6,4},{7,5},{8,10},{9,11},{10,... | collective-permute-start | bytes 3833864 | tf_op jit(solution)/shard_map/ppermute | solution.py:88
  406.1 30.2 %collective-permute-start.47 = (bf16[2,24,3072]{2,1,0:T(8,128)(2,1)}, bf16[2,24,3072]{2,1,0:T(8,128)(2,1)S(1)}, u32[]{:S(2)}, u32[]{:S(2)}) collective-permute-start(bf16[2,24,3072]{2,1,0:T(8,128)(2,1)} %get-tuple-element.503), channel_id=1, source_target_pairs={{0,8},{1,9},{2,10},{3,11},{4,12},{5,13},{6,14},{7,15},{8,0},{9,1},... | collective-permute-start | bytes 884744 | tf_op jit(solution)/shard_map/ppermute | solution.py:88
  465.4 41.6 %collective-permute-start.63 = (bf16[4,24,768]{2,1,0:T(8,128)(2,1)S(1)}, bf16[4,24,768]{2,1,0:T(8,128)(2,1)S(1)}, u32[]{:S(2)}, u32[]{:S(2)}) collective-permute-start(bf16[4,24,768]{2,1,0:T(8,128)(2,1)S(1)} %copy-done.56), channel_id=1, source_target_pairs={{0,16},{1,17},{2,18},{3,19},{4,20},{5,21},{6,22},{7,23},{8,24},{9,... | collective-permute-start | bytes 442376 | tf_op jit(solution)/shard_map/ppermute | solution.py:88
  467.7 26.7 %collective-permute-start.56 = (bf16[256,768]{1,0:T(8,128)(2,1)S(1)}, bf16[256,768]{1,0:T(8,128)(2,1)S(1)}, u32[]{:S(2)}, u32[]{:S(2)}) collective-permute-start(bf16[256,768]{1,0:T(8,128)(2,1)S(1)} %fusion.46), channel_id=1, source_target_pairs={{0,16},{1,17},{2,18},{3,19},{4,20},{5,21},{6,22},{7,23},{8,24},{9,... | collective-permute-start | bytes 1179656 | tf_op jit(solution)/shard_map/ppermute | solution.py:88
  470.9 23.5 %collective-permute-start.59 = (bf16[2,2,2,64,768]{4,3,2,1,0:T(8,128)(2,1)S(1)}, bf16[2,2,2,64,768]{4,3,2,1,0:T(8,128)(2,1)S(1)}, u32[]{:S(2)}, u32[]{:S(2)}) collective-permute-start(bf16[2,2,2,64,768]{4,3,2,1,0:T(8,128)(2,1)S(1)} %pad_maximum_fusion.7), channel_id=1, source_target_pairs={{0,2},{1,3},{2,0},{3,1},{4,6},{5,7},{6,4},{7,5},{8,10},{9,11},{10,... | collective-permute-start | bytes 2359304 | tf_op jit(solution)/shard_map/ppermute | solution.py:88
  480.7 26.4 %collective-permute-start.64 = (bf16[24,3072]{1,0:T(8,128)(2,1)S(1)}, bf16[24,3072]{1,0:T(8,128)(2,1)S(1)}, u32[]{:S(2)}, u32[]{:S(2)}) collective-permute-start(bf16[24,3072]{1,0:T(8,128)(2,1)S(1)} %get-tuple-element.535), channel_id=1, source_target_pairs={{0,16},{1,17},{2,18},{3,19},{4,20},{5,21},{6,22},{7,23},{8,24},{9,... | collective-permute-start | bytes 442376 | tf_op jit(solution)/shard_map/ppermute | solution.py:88
  (140 other events, 1331.7 us)
Sparse Core Ops, SparseCore 0:
  14.4 92.6 all-gather.2
  110.5 96.5 all-gather.4

commit v6 on v0

--- a/solution.py
+++ b/solution.py
@@ -563,6 +563,20 @@
     return values
 
 
+def hold(values, *chains):
+    values, pending = lax.optimization_barrier((values, [chain.pending for chain in chains]))
+    for chain, arrays in zip(chains, pending):
+        chain.pending = arrays
+    return values
+
+
+def settle(values, *chains):
+    values, kept = lax.optimization_barrier((values, [chain.pending[0] for chain in chains]))
+    for chain, array in zip(chains, kept):
+        chain.pending = [array] + list(chain.pending[1:])
+    return values
+
+
 def total_of(arrays):
     total = wide(arrays[0])
     for array in arrays[1:]:
@@ -871,8 +885,8 @@
     near_other_grad, slopes = self_backward(
         tables["near other"], queries, dout, state, [near_other], slopes, False, False
     )
-    near_other_grad, slopes = meet(
-        (near_other_grad, slopes), unspread, reduce_ffnout, reduce_ffnin, reduce_mid
+    near_other_grad, far_moved, slopes = meet(
+        (near_other_grad, far_moved, slopes), unspread, reduce_ffnout, reduce_ffnin, reduce_mid
     )
     near_moved = grid.send(near_other_grad, "c", 1)
 
@@ -899,11 +913,12 @@
     reduce_late = Chain(reduction(sharded(grad_late), "cyxlh"))
     spread_back = Chain(spreading(rounded(back_matmul(dcross_pair, crosskv_full))))
 
+    slopes = settle(slopes, reduce_late, spread_back)
     near_own_grad, query_grad = self_backward(
         tables["near own"], queries, dout, state, [own_side], slopes, False, True
     )
-    near_own_grad, near_moved, far_moved, query_grad = meet(
-        (near_own_grad, near_moved, far_moved, query_grad)
+    near_own_grad, near_moved, query_grad = hold(
+        (near_own_grad, near_moved, query_grad), reduce_late, spread_back
     )
 
     far_query_grad = grid.send(query_grad[1::2], "z", 0, mirror=True)

time: 537 us -> 541 us (level)
  waiting for transfers between devices: 115 us -> 123 us
    ppermute x68, waiting for transfers between devices: 115 us -> 123 us  [send(): return lax.ppermute(array, ('seq', 'batch'), pairs)]
    unnamed x190 -> x196, local copies, waits for them, and re-layouts: 12.4 us -> 11.7 us
  transfers between devices with their start and end apart: 70 -> 70, of which waited for: 22 -> 21; matrix products, arithmetic and copies ran while one was open for 25% -> 24% of each run, Pallas kernels for 28% -> 27%
where the time goes in v6:
time: 541 us; the launch traced here: 536 us
  Pallas kernels  147 us (27%)
  waiting for transfers between devices  123 us (23%)
  local copies, waits for them, and re-layouts  74 us (14%)
  starting transfers between devices  69.1 us (13%)
  other arithmetic  56.9 us (11%)
  matrix products  48.7 us (9%)
  between operations  17.3 us (3%)
    ppermute x68, waiting for transfers between devices, send(): return lax.ppermute(array, ('seq', 'batch'), pairs)  123 us
    ppermute x68, starting transfers between devices, send(): return lax.ppermute(array, ('seq', 'batch'), pairs)  69.1 us
    pallas_call x4, Pallas kernels, self_backward(): pl.pallas_call(functools.partial(backward_kernel, rows, parts, first, las...  56.2 us
    pallas_call x4, Pallas kernels, self_forward(): pl.pallas_call(functools.partial(forward_kernel, rows, parts, first, last...  52.5 us
    convert_element_type x30, other arithmetic, rounded(): return values.astype(jnp.bfloat16)  29 us
    dot_general x11, matrix products, matmul(): return jnp.dot(left, right, preferred_element_type=jnp.float32)  22.9 us
    dot_general x12, matrix products, back_matmul(): lax.dot_general(left, right, LANES_IN, preferred_element_type=jnp.float32)  17.4 us
    squeeze x24, local copies, waits for them, and re-layouts, take(): return lax.dynamic_index_in_dim(array, index, axis, keepdims=False)  15.5 us
  transfers between devices with their start and end apart: 70, of which 21 were waited for; matrix products, arithmetic and copies ran while one was open for 24% of the time, Pallas kernels for 27%

profile of v6, /device:TPU:0, one launch (start us, length us, event | category | flops | bytes accessed | tf_op | source)
XLA Modules:
  0.0 536.1 jit_solution(9500449279175400562)
XLA Ops:
  18.8 8.1 %pick_rows.1 = bf16[16,64,768]{2,1,0:T(8,128)(2,1)} custom-call(s32[32]{0:T(128)} %pad_add_fusion.table, bf16[8,64,768]{2,1,0:T(8,128)(2,1)} %bitcast.435), custom_call_target="tpu_custom_call" | custom-call | tf_op jit(solution)/shard_map/pick_rows/pallas_call | solution.py:507
  43.2 4.8 collective-permute-done.3
  55.6 14.9 %collective-permute-done.8 = bf16[256,768]{1,0:T(8,128)(2,1)S(1)} collective-permute-done((bf16[256,768]{1,0:T(8,128)(2,1)S(1)}, bf16[256,768]{1,0:T(8,128)(2,1)S(1)}, u32[]{:S(2)}, u32[]{:S(2)}) %collective-permute-start.8) | collective-permute-done | bytes 393248 | tf_op jit(solution)/shard_map/ppermute | solution.py:88
  72.5 12.5 %collective-permute-done.7 = bf16[256,768]{1,0:T(8,128)(2,1)S(1)} collective-permute-done((bf16[256,768]{1,0:T(8,128)(2,1)S(1)}, bf16[256,768]{1,0:T(8,128)(2,1)S(1)}, u32[]{:S(2)}, u32[]{:S(2)}) %collective-permute-start.7) | collective-permute-done | bytes 393248 | tf_op jit(solution)/shard_map/ppermute | solution.py:88
  84.9 15.4 %collective-permute-done.9 = bf16[256,768]{1,0:T(8,128)(2,1)S(1)} collective-permute-done((bf16[256,768]{1,0:T(8,128)(2,1)S(1)}, bf16[256,768]{1,0:T(8,128)(2,1)S(1)}, u32[]{:S(2)}, u32[]{:S(2)}) %collective-permute-start.9) | collective-permute-done | bytes 393248 | tf_op jit(solution)/shard_map/ppermute | solution.py:88
  103.6 6.1 %collective-permute-done.11 = bf16[2,256,256]{2,1,0:T(8,128)(2,1)S(1)} collective-permute-done((bf16[2,256,256]{2,1,0:T(8,128)(2,1)S(1)}, bf16[2,256,256]{2,1,0:T(8,128)(2,1)S(1)}, u32[]{:S(2)}, u32[]{:S(2)}) %collective-permute-start.11) | collective-permute-done | bytes 262176 | tf_op jit(solution)/shard_map/ppermute | solution.py:88
  111.7 14.2 %self_forward.4 = (f32[4,3,128,256]{3,2,1,0:T(8,128)}, f32[4,16,256]{2,1,0:T(8,128)}) custom-call(s32[9]{0:T(128)} %get-tuple-element.547.table, bf16[4,256,256]{2,1,0:T(8,128)(2,1)} %pad_maximum_fusion.11.query_in, bf16[1024,384]{1,0:T(8,128)(2,1)} %copy-done.86), custom_call_target="tpu_custom_call" | custom-call | flops 3221225472 | bytes 1572864 | tf_op jit(solution)/shard_map/self_forward/pallas_call | solution.py:317
  126.8 12.5 %self_forward.5 = (f32[4,3,128,256]{3,2,1,0:T(8,128)}, f32[4,16,256]{2,1,0:T(8,128)}) custom-call(s32[9]{0:T(128)} %get-tuple-element.549.table, bf16[4,256,256]{2,1,0:T(8,128)(2,1)} %pad_maximum_fusion.11.query_in, bf16[1024,384]{1,0:T(8,128)(2,1)} %copy-done.87, f32[4,3,128,256]{3,2,1,0:T(8,128)} %get-tuple-element.185.refs_1_, ...), custom_call_target="tpu_custom_call" | custom-call | flops 3221225472 | bytes 1572864 | tf_op jit(solution)/shard_map/self_forward/pallas_call | solution.py:317
  142.8 12.5 %self_forward.6 = (f32[4,3,128,256]{3,2,1,0:T(8,128)}, f32[4,16,256]{2,1,0:T(8,128)}) custom-call(s32[9]{0:T(128)} %get-tuple-element.548.table, bf16[4,256,256]{2,1,0:T(8,128)(2,1)} %pad_maximum_fusion.11.query_in, bf16[1024,384]{1,0:T(8,128)(2,1)} %copy-done.88, f32[4,3,128,256]{3,2,1,0:T(8,128)} %get-tuple-element.193.refs_1_, ...), custom_call_target="tpu_custom_call" | custom-call | flops 3221225472 | bytes 1572864 | tf_op jit(solution)/shard_map/self_forward/pallas_call | solution.py:317
  156.2 13.3 %self_forward.7 = (f32[4,256,256]{2,1,0:T(8,128)}, f32[4,8,256]{2,1,0:T(8,128)}) custom-call(s32[9]{0:T(128)} %add_add_fusion.4.table, bf16[4,256,256]{2,1,0:T(8,128)(2,1)} %pad_maximum_fusion.11.query_in, bf16[1024,384]{1,0:T(8,128)(2,1)} %copy-done.89, f32[4,3,128,256]{3,2,1,0:T(8,128)} %get-tuple-element.200.refs_1_, f32[4,16,256]{2,1,0:T(8,128)} %get-tuple-element.201.refs_2_), custom_call_target="tpu_custom_call" | custom-call | flops 3221225472 | bytes 1572864 | tf_op jit(solution)/shard_map/self_forward/pallas_call | solution.py:317
  175.8 6.7 %collective-permute-done.19 = bf16[256,256]{1,0:T(8,128)(2,1)S(1)} collective-permute-done((bf16[256,256]{1,0:T(8,128)(2,1)S(1)}, bf16[256,256]{1,0:T(8,128)(2,1)S(1)}, u32[]{:S(2)}, u32[]{:S(2)}) %collective-permute-start.19) | collective-permute-done | bytes 131104 | tf_op jit(solution)/shard_map/ppermute | solution.py:88
  182.5 5.9 %collective-permute-done.21 = bf16[256,256]{1,0:T(8,128)(2,1)S(1)} collective-permute-done((bf16[256,256]{1,0:T(8,128)(2,1)S(1)}, bf16[256,256]{1,0:T(8,128)(2,1)S(1)}, u32[]{:S(2)}, u32[]{:S(2)}) %collective-permute-start.21) | collective-permute-done | bytes 131104 | tf_op jit(solution)/shard_map/ppermute | solution.py:88
  207.0 11.1 %cross_forward.1 = (bf16[256,768]{1,0:T(8,128)(2,1)}, f32[6,8,256]{2,1,0:T(8,128)}) custom-call(bf16[256,768]{1,0:T(8,128)(2,1)} %fusion.22.query, bf16[1024,1536]{1,0:T(8,128)(2,1)} %add_convert_fusion.keys.values, bf16[1024,1536]{1,0:T(8,128)(2,1)} %add_convert_fusion.keys.values), custom_call_target="tpu_custom_call" | custom-call | flops 1610612736 | bytes 3145728 | tf_op jit(solution)/shard_map/cross_forward/pallas_call | solution.py:441
  220.4 10.1 %multiply_convert_fusion = (bf16[256,3072]{1,0:T(8,128)(2,1)S(1)}, f32[256,3072]{1,0:T(8,128)S(1)}, f32[256,3072]{1,0:T(8,128)S(1)}) fusion(f32[3072]{0:T(1024)S(1)} %add.598, bf16[2,768,3072]{2,1,0:T(8,128)(2,1)} %all-gather.5.cloned.1.call-done, f32[256,768]{1,0:T(8,128)S(1)} %get-tuple-element.551, f32[768]{0:T(1024)S(1)} %get-tuple-element.398, ...), kind=kOutput, calls=%fused_computation.21 | convolution fusion | flops 1260847104 | bytes 13389824 | tf_op jit(solution)/shard_map/dot_general | solution.py:45
  260.7 13.6 %cross_backward.1 = (bf16[256,768]{1,0:T(8,128)(2,1)}, bf16[1024,768]{1,0:T(8,128)(2,1)}, bf16[1024,768]{1,0:T(8,128)(2,1)}) custom-call(bf16[256,768]{1,0:T(8,128)(2,1)} %fusion.22.query, bf16[1024,1536]{1,0:T(8,128)(2,1)} %add_convert_fusion.keys.values, bf16[1024,1536]{1,0:T(8,128)(2,1)} %add_convert_fusion.keys.values, ...), custom_call_target="tpu_custom_call" | custom-call | flops 4026531840 | bytes 6291456 | tf_op jit(solution)/shard_map/cross_backward/pallas_call | solution.py:469
  317.4 13.6 %self_backward.4 = (bf16[1024,384]{1,0:T(8,128)(2,1)}, f32[4,3,128,256]{3,2,1,0:T(8,128)}, f32[4,8,256]{2,1,0:T(8,128)}) custom-call(s32[9]{0:T(128)} %add_add_fusion.4.table, bf16[4,256,256]{2,1,0:T(8,128)(2,1)} %pad_maximum_fusion.11.query_in, bf16[4,256,256]{2,1,0:T(8,128)(2,1)} %pad_maximum_fusion.12.dout, f32[4,8,256]{2,1,0:T(8,128)} %get-tuple-element.227.state, ...), custom_call_target="tpu_custom_call" | custom-call | flops 4026531840 | bytes 3145728 | tf_op jit(solution)/shard_map/self_backward/pallas_call | solution.py:359
  345.0 13.6 %self_backward.5 = (bf16[1024,384]{1,0:T(8,128)(2,1)}, f32[4,3,128,256]{3,2,1,0:T(8,128)}) custom-call(s32[9]{0:T(128)} %get-tuple-element.548.table, bf16[4,256,256]{2,1,0:T(8,128)(2,1)} %pad_maximum_fusion.11.query_in, bf16[4,256,256]{2,1,0:T(8,128)(2,1)} %pad_maximum_fusion.12.dout, f32[4,8,256]{2,1,0:T(8,128)} %get-tuple-element.228.state, ...), custom_call_target="tpu_custom_call" | custom-call | flops 4026531840 | bytes 3145728 | tf_op jit(solution)/shard_map/self_backward/pallas_call | solution.py:359
  373.4 13.3 %self_backward.6 = (bf16[1024,384]{1,0:T(8,128)(2,1)}, f32[4,3,128,256]{3,2,1,0:T(8,128)}) custom-call(s32[9]{0:T(128)} %get-tuple-element.549.table, bf16[4,256,256]{2,1,0:T(8,128)(2,1)} %pad_maximum_fusion.11.query_in, bf16[4,256,256]{2,1,0:T(8,128)(2,1)} %pad_maximum_fusion.12.dout, f32[4,8,256]{2,1,0:T(8,128)} %get-tuple-element.228.state, ...), custom_call_target="tpu_custom_call" | custom-call | flops 4026531840 | bytes 3145728 | tf_op jit(solution)/shard_map/self_backward/pallas_call | solution.py:359
  407.6 15.7 %self_backward.7 = (bf16[1024,384]{1,0:T(8,128)(2,1)}, bf16[4,256,256]{2,1,0:T(8,128)(2,1)}) custom-call(s32[9]{0:T(128)} %get-tuple-element.547.table, bf16[4,256,256]{2,1,0:T(8,128)(2,1)} %pad_maximum_fusion.11.query_in, bf16[4,256,256]{2,1,0:T(8,128)(2,1)} %pad_maximum_fusion.12.dout, f32[4,8,256]{2,1,0:T(8,128)} %get-tuple-element.228.state, ...), custom_call_target="tpu_custom_call" | custom-call | flops 4026531840 | bytes 3145728 | tf_op jit(solution)/shard_map/self_backward/pallas_call | solution.py:359
  427.6 10.5 %collective-permute-done.45 = bf16[2,256,256]{2,1,0:T(8,128)(2,1)S(1)} collective-permute-done((bf16[2,256,256]{2,1,0:T(8,128)(2,1)S(1)}, bf16[2,256,256]{2,1,0:T(8,128)(2,1)S(1)}, u32[]{:S(2)}, u32[]{:S(2)}) %collective-permute-start.45) | collective-permute-done | bytes 262176 | tf_op jit(solution)/shard_map/ppermute | solution.py:88
  462.0 5.6 %collective-permute-done.67 = bf16[24,3072]{1,0:T(8,128)(2,1)S(1)} collective-permute-done((bf16[24,3072]{1,0:T(8,128)(2,1)S(1)}, bf16[24,3072]{1,0:T(8,128)(2,1)S(1)}, u32[]{:S(2)}, u32[]{:S(2)}) %collective-permute-start.67) | collective-permute-done | bytes 147488 | tf_op jit(solution)/shard_map/ppermute | solution.py:88
  486.2 6.3 %collective-permute-done.53 = bf16[2,2,64,768]{3,2,1,0:T(8,128)(2,1)S(1)} collective-permute-done((bf16[2,2,64,768]{3,2,1,0:T(8,128)(2,1)S(1)}, bf16[2,2,64,768]{3,2,1,0:T(8,128)(2,1)S(1)}, u32[]{:S(2)}, u32[]{:S(2)}) %collective-permute-start.53) | collective-permute-done | bytes 393248 | tf_op jit(solution)/shard_map/ppermute | solution.py:88
  494.8 7.8 %collective-permute-done.64 = bf16[3,24,768]{2,1,0:T(8,128)(2,1)S(1)} collective-permute-done((bf16[3,24,768]{2,1,0:T(8,128)(2,1)S(1)}, bf16[3,24,768]{2,1,0:T(8,128)(2,1)S(1)}, u32[]{:S(2)}, u32[]{:S(2)}) %collective-permute-start.64) | collective-permute-done | bytes 110624 | tf_op jit(solution)/shard_map/ppermute | solution.py:88
  514.5 5.6 %place_rows.1 = f32[8,64,768]{2,1,0:T(8,128)} custom-call(s32[16]{0:T(128)} %and_select_fusion.3.table, bf16[16,64,768]{2,1,0:T(8,128)(2,1)} %bitcast.412), custom_call_target="tpu_custom_call" | custom-call | tf_op jit(solution)/shard_map/place_rows/pallas_call | solution.py:533
  (590 shorter events, 265.1 us)
Async XLA Ops:
  7.2 188.5 %all-gather.3.cloned.1.call-start = ((), (), s32[]{:S(2)}) async-start(), calls=%async_computation | async-start | bytes 6285312 | tf_op jit(solution)/shard_map/all_gather | solution.py:669
  12.0 208.5 %all-gather.5.cloned.1.call-start = ((), (), s32[]{:S(2)}) async-start(), calls=%async_computation.1 | async-start | bytes 9732096 | tf_op jit(solution)/shard_map/all_gather | solution.py:670
  55.5 29.4 %collective-permute-start.7 = (bf16[256,768]{1,0:T(8,128)(2,1)S(1)}, bf16[256,768]{1,0:T(8,128)(2,1)S(1)}, u32[]{:S(2)}, u32[]{:S(2)}) collective-permute-start(bf16[256,768]{1,0:T(8,128)(2,1)S(1)} %bitcast.445), channel_id=1, source_target_pairs={{0,8},{1,9},{2,10},{3,11},{4,12},{5,13},{6,14},{7,15},{8,0},{9,1},... | collective-permute-start | bytes 1179656 | tf_op jit(solution)/shard_map/ppermute | solution.py:88
  70.5 29.8 %collective-permute-start.9 = (bf16[256,768]{1,0:T(8,128)(2,1)S(1)}, bf16[256,768]{1,0:T(8,128)(2,1)S(1)}, u32[]{:S(2)}, u32[]{:S(2)}) collective-permute-start(bf16[256,768]{1,0:T(8,128)(2,1)S(1)} %collective-permute-done.8), channel_id=1, source_target_pairs={{0,8},{1,9},{2,10},{3,11},{4,12},{5,13},{6,14},{7,15},{8,0},{9,1},... | collective-permute-start | bytes 1179656 | tf_op jit(solution)/shard_map/ppermute | solution.py:88
  70.8 29.6 %collective-permute-start.10 = (bf16[2,2,1,64,768]{4,3,1,0,2:T(8,128)(2,1)S(1)}, bf16[2,2,1,64,768]{4,3,1,0,2:T(8,128)(2,1)S(1)}, u32[]{:S(2)}, u32[]{:S(2)}) collective-permute-start(bf16[2,2,1,64,768]{4,3,1,0,2:T(8,128)(2,1)S(1)} %get-tuple-element.469), channel_id=1, source_target_pairs={{0,4},{1,5},{2,6},{3,7},{4,0},{5,1},{6,2},{7,3},{8,12},{9,13},{10,... | collective-permute-start | bytes 1179656 | tf_op jit(solution)/shard_map/ppermute | solution.py:88
  102.6 23.3 %collective-permute-start.12 = (bf16[1024,384]{1,0:T(8,128)(2,1)S(1)}, bf16[1024,384]{1,0:T(8,128)(2,1)S(1)}, u32[]{:S(2)}, u32[]{:S(2)}) collective-permute-start(bf16[1024,384]{1,0:T(8,128)(2,1)S(1)} %add_convert_fusion.13.refs_0_), channel_id=1, source_target_pairs={{0,2},{1,3},{2,0},{3,1},{4,6},{5,7},{6,4},{7,5},{8,10},{9,11},{10,... | collective-permute-start | bytes 2359304 | tf_op jit(solution)/shard_map/ppermute | solution.py:88
  109.7 29.5 %collective-permute-start.14 = (bf16[1024,384]{1,0:T(8,128)(2,1)S(1)}, bf16[1024,384]{1,0:T(8,128)(2,1)S(1)}, u32[]{:S(2)}, u32[]{:S(2)}) collective-permute-start(bf16[1024,384]{1,0:T(8,128)(2,1)S(1)} %add_convert_fusion.13.refs_0_), channel_id=1, source_target_pairs={{0,4},{1,5},{2,6},{3,7},{4,0},{5,1},{6,2},{7,3},{8,12},{9,13},{10,... | collective-permute-start | bytes 2359304 | tf_op jit(solution)/shard_map/ppermute | solution.py:88
  237.8 36.6 %collective-permute-start.24 = (bf16[4,2,2,2,2,24,768]{6,5,4,3,2,1,0:T(8,128)(2,1)}, bf16[4,2,2,2,2,24,768]{6,5,4,3,2,1,0:T(8,128)(2,1)}, u32[]{:S(2)}, u32[]{:S(2)}) collective-permute-start(bf16[4,2,2,2,2,24,768]{6,5,4,3,2,1,0:T(8,128)(2,1)} %get-tuple-element.432), channel_id=1, source_target_pairs={{0,2},{1,3},{2,0},{3,1},{4,6},{5,7},{6,4},{7,5},{8,10},{9,11},{10,... | collective-permute-start | bytes 7077896 | tf_op jit(solution)/shard_map/ppermute | solution.py:88
  247.8 26.6 %collective-permute-start.25 = (bf16[2,2,2,2,24,3072]{5,4,2,1,0,3:T(8,128)(2,1)}, bf16[2,2,2,2,24,3072]{5,4,2,1,0,3:T(8,128)(2,1)}, u32[]{:S(2)}, u32[]{:S(2)}) collective-permute-start(bf16[2,2,2,2,24,3072]{5,4,2,1,0,3:T(8,128)(2,1)} %bitcast.389), channel_id=1, source_target_pairs={{0,2},{1,3},{2,0},{3,1},{4,6},{5,7},{6,4},{7,5},{8,10},{9,11},{10,... | collective-permute-start | bytes 7077896 | tf_op jit(solution)/shard_map/ppermute | solution.py:88
  301.8 29.2 %collective-permute-start.30 = (bf16[4,2,2,2,24,768]{5,4,3,2,1,0:T(8,128)(2,1)}, bf16[4,2,2,2,24,768]{5,4,3,2,1,0:T(8,128)(2,1)}, u32[]{:S(2)}, u32[]{:S(2)}) collective-permute-start(bf16[4,2,2,2,24,768]{5,4,3,2,1,0:T(8,128)(2,1)} %get-tuple-element.442), channel_id=1, source_target_pairs={{0,1},{1,0},{2,3},{3,2},{4,5},{5,4},{6,7},{7,6},{8,9},{9,8},{10,11... | collective-permute-start | bytes 3538952 | tf_op jit(solution)/shard_map/ppermute | solution.py:88
  313.3 45.3 %collective-permute-start.36 = (bf16[2,2,2,24,3072]{4,3,2,1,0:T(8,128)(2,1)}, bf16[2,2,2,24,3072]{4,3,2,1,0:T(8,128)(2,1)}, u32[]{:S(2)}, u32[]{:S(2)}) collective-permute-start(bf16[2,2,2,24,3072]{4,3,2,1,0:T(8,128)(2,1)} %get-tuple-element.440), channel_id=1, source_target_pairs={{0,1},{1,0},{2,3},{3,2},{4,5},{5,4},{6,7},{7,6},{8,9},{9,8},{10,11... | collective-permute-start | bytes 3538952 | tf_op jit(solution)/shard_map/ppermute | solution.py:88
  332.4 26.3 %collective-permute-start.33 = (bf16[1024,384]{1,0:T(8,128)(2,1)}, bf16[1024,384]{1,0:T(8,128)(2,1)}, u32[]{:S(2)}, u32[]{:S(2)}) collective-permute-start(bf16[1024,384]{1,0:T(8,128)(2,1)} %get-tuple-element.238), channel_id=1, source_target_pairs={{0,2},{1,3},{2,0},{3,1},{4,6},{5,7},{6,4},{7,5},{8,10},{9,11},{10,... | collective-permute-start | bytes 2359304 | tf_op jit(solution)/shard_map/ppermute | solution.py:88
  334.8 23.9 %collective-permute-start.34 = (bf16[2,64,1536]{2,1,0:T(8,128)(2,1)}, bf16[2,64,1536]{2,1,0:T(8,128)(2,1)S(1)}, u32[]{:S(2)}, u32[]{:S(2)}) collective-permute-start(bf16[2,64,1536]{2,1,0:T(8,128)(2,1)} %get-tuple-element.465), channel_id=1, source_target_pairs={{0,8},{1,9},{2,10},{3,11},{4,12},{5,13},{6,14},{7,15},{8,0},{9,1},... | collective-permute-start | bytes 1179656 | tf_op jit(solution)/shard_map/ppermute | solution.py:88
  343.6 43.2 %collective-permute-start.41 = (bf16[3,2,2,2,24,768]{5,4,3,2,1,0:T(8,128)(2,1)S(1)}, bf16[3,2,2,2,24,768]{5,4,3,2,1,0:T(8,128)(2,1)S(1)}, u32[]{:S(2)}, u32[]{:S(2)}) collective-permute-start(bf16[3,2,2,2,24,768]{5,4,3,2,1,0:T(8,128)(2,1)S(1)} %get-tuple-element.444), channel_id=1, source_target_pairs={{0,1},{1,0},{2,3},{3,2},{4,5},{5,4},{6,7},{7,6},{8,9},{9,8},{10,11... | collective-permute-start | bytes 2654216 | tf_op jit(solution)/shard_map/ppermute | solution.py:88
  361.3 30.2 %collective-permute-start.37 = (bf16[1024,384]{1,0:T(8,128)(2,1)}, bf16[1024,384]{1,0:T(8,128)(2,1)}, u32[]{:S(2)}, u32[]{:S(2)}) collective-permute-start(bf16[1024,384]{1,0:T(8,128)(2,1)} %add_convert_fusion.11), channel_id=1, source_target_pairs={{0,4},{1,5},{2,6},{3,7},{4,0},{5,1},{6,2},{7,3},{8,12},{9,13},{10,... | collective-permute-start | bytes 2359304 | tf_op jit(solution)/shard_map/ppermute | solution.py:88
  398.8 25.3 %collective-permute-start.44 = (bf16[64,768]{1,0:T(8,128)(2,1)S(1)}, bf16[64,768]{1,0:T(8,128)(2,1)S(1)}, u32[]{:S(2)}, u32[]{:S(2)}) collective-permute-start(bf16[64,768]{1,0:T(8,128)(2,1)S(1)} %fusion.24), channel_id=1, source_target_pairs={{0,16},{1,17},{2,18},{3,19},{4,20},{5,21},{6,22},{7,23},{8,24},{9,... | collective-permute-start | bytes 294920 | tf_op jit(solution)/shard_map/ppermute | solution.py:88
  403.6 35.9 %collective-permute-start.46 = (bf16[4,24,768]{2,1,0:T(8,128)(2,1)}, bf16[4,24,768]{2,1,0:T(8,128)(2,1)}, u32[]{:S(2)}, u32[]{:S(2)}) collective-permute-start(bf16[4,24,768]{2,1,0:T(8,128)(2,1)} %get-tuple-element.503), channel_id=1, source_target_pairs={{0,16},{1,17},{2,18},{3,19},{4,20},{5,21},{6,22},{7,23},{8,24},{9,... | collective-permute-start | bytes 442376 | tf_op jit(solution)/shard_map/ppermute | solution.py:88
  405.7 33.8 %collective-permute-start.47 = (bf16[2,24,3072]{2,1,0:T(8,128)(2,1)}, bf16[2,24,3072]{2,1,0:T(8,128)(2,1)S(1)}, u32[]{:S(2)}, u32[]{:S(2)}) collective-permute-start(bf16[2,24,3072]{2,1,0:T(8,128)(2,1)} %get-tuple-element.473), channel_id=1, source_target_pairs={{0,8},{1,9},{2,10},{3,11},{4,12},{5,13},{6,14},{7,15},{8,0},{9,1},... | collective-permute-start | bytes 884744 | tf_op jit(solution)/shard_map/ppermute | solution.py:88
  444.3 28.5 %collective-permute-start.59 = (bf16[256,768]{1,0:T(8,128)(2,1)}, bf16[256,768]{1,0:T(8,128)(2,1)}, u32[]{:S(2)}, u32[]{:S(2)}) collective-permute-start(bf16[256,768]{1,0:T(8,128)(2,1)} %get-tuple-element.453), channel_id=1, source_target_pairs={{0,8},{1,9},{2,10},{3,11},{4,12},{5,13},{6,14},{7,15},{8,0},{9,1},... | collective-permute-start | bytes 1179656 | tf_op jit(solution)/shard_map/ppermute | solution.py:88
  447.8 29.8 %collective-permute-start.49 = (bf16[2,2,2,2,24,640]{5,4,2,1,0,3:T(8,128)(2,1)}, bf16[2,2,2,2,24,640]{5,4,2,1,0,3:T(8,128)(2,1)}, u32[]{:S(2)}, u32[]{:S(2)}) collective-permute-start(bf16[2,2,2,2,24,640]{5,4,2,1,0,3:T(8,128)(2,1)} %bitcast.393), channel_id=1, source_target_pairs={{0,2},{1,3},{2,0},{3,1},{4,6},{5,7},{6,4},{7,5},{8,10},{9,11},{10,... | collective-permute-start | bytes 1474568 | tf_op jit(solution)/shard_map/ppermute | solution.py:88
  450.0 25.9 %collective-permute-start.50 = (bf16[2,64,768]{2,1,0:T(8,128)(2,1)}, bf16[2,64,768]{2,1,0:T(8,128)(2,1)}, u32[]{:S(2)}, u32[]{:S(2)}) collective-permute-start(bf16[2,64,768]{2,1,0:T(8,128)(2,1)} %pad_maximum_fusion.20), channel_id=1, source_target_pairs={{0,8},{1,9},{2,10},{3,11},{4,12},{5,13},{6,14},{7,15},{8,0},{9,1},... | collective-permute-start | bytes 589832 | tf_op jit(solution)/shard_map/ppermute | solution.py:88
  454.3 23.3 %collective-permute-start.51 = (bf16[2,2,2,24,1664]{4,3,2,1,0:T(8,128)(2,1)}, bf16[2,2,2,24,1664]{4,3,2,1,0:T(8,128)(2,1)}, u32[]{:S(2)}, u32[]{:S(2)}) collective-permute-start(bf16[2,2,2,24,1664]{4,3,2,1,0:T(8,128)(2,1)} %get-tuple-element.450), channel_id=1, source_target_pairs={{0,1},{1,0},{2,3},{3,2},{4,5},{5,4},{6,7},{7,6},{8,9},{9,8},{10,11... | collective-permute-start | bytes 1916936 | tf_op jit(solution)/shard_map/ppermute | solution.py:88
  472.8 39.3 %collective-permute-start.58 = (bf16[256,768]{1,0:T(8,128)(2,1)S(1)}, bf16[256,768]{1,0:T(8,128)(2,1)S(1)}, u32[]{:S(2)}, u32[]{:S(2)}) collective-permute-start(bf16[256,768]{1,0:T(8,128)(2,1)S(1)} %copy-done.42), channel_id=1, source_target_pairs={{0,8},{1,9},{2,10},{3,11},{4,12},{5,13},{6,14},{7,15},{8,0},{9,1},... | collective-permute-start | bytes 1179656 | tf_op jit(solution)/shard_map/ppermute | solution.py:88
  475.9 36.3 %collective-permute-start.60 = (bf16[256,768]{1,0:T(8,128)(2,1)S(1)}, bf16[256,768]{1,0:T(8,128)(2,1)S(1)}, u32[]{:S(2)}, u32[]{:S(2)}) collective-permute-start(bf16[256,768]{1,0:T(8,128)(2,1)S(1)} %fusion.46), channel_id=1, source_target_pairs={{0,16},{1,17},{2,18},{3,19},{4,20},{5,21},{6,22},{7,23},{8,24},{9,... | collective-permute-start | bytes 1179656 | tf_op jit(solution)/shard_map/ppermute | solution.py:88
  (136 other events, 1319.7 us)
Sparse Core Ops, SparseCore 0:
  12.1 90.3 all-gather.2
  106.0 98.4 all-gather.4
